TPU v7x, 32 devices: a whole 2x2x4 slice. The times are simulated.
32 devices in a mesh: row: 4 (over y, x), col: 8 (over z, core).
Axes of the slice: x: 2, y: 2, z: 4, core: 2. Of those that a mesh axis runs over, the one named last changes fastest.
Arguments:
- inputs: bfloat16 [2048, 25600], P('row', 'col'), may hold values from -6 to 6
- out_grads: bfloat16 [2048, 5120], P('col', 'row'), may hold values from -0.125 to 0.125
- weights: bfloat16 [5120, 25600], P('row', 'col'), may hold values from -3 to 3
- momentum: float32 [5120, 25600], P('row', 'col'), may hold values from -13 to 13
- right_factor: float32 [25600, 256], P('col'), may hold values from -6 to 6
Outputs:
- weights_new: float32 [5120, 25600], P('row', 'col')
- momentum_new: float32 [5120, 25600], P('row', 'col')
- factor_new: float32 [25600, 256], P('col')
All inputs are finite; a program needn't handle non-finite values.
Results may differ from a plain program's by a relative error of at most 0.0003.
Values may be sent and summed in bfloat16 or wider, within the bound.
No kernel may reach another device: no remote copies, remote signals or barrier semaphores. Data moves between devices by JAX's collectives and lax.ppermute only.
A program may use at most 128 MiB of HBM per device.

v0:
```python
import math

import jax
import jax.numpy as jnp
from jax import lax
from jax.sharding import PartitionSpec as P

M = 5120
N = 25600
RANK = 256


mix_rate = 0.95
step_rate = 0.3
weight_decay = 0.1
tiny_eps = 1e-06
highest = lax.Precision.HIGHEST


def inner_rows(left_side, right_in):
    return lax.dot_general(left_side, right_in, (((0,), (0,)), ((), ())), precision=highest)


def orthonormal(sketch_rows, gram_total):
    factor_low = jnp.linalg.cholesky(gram_total)
    return jax.scipy.linalg.solve_triangular(factor_low, sketch_rows.T, lower=True).T


def on_device(inputs, out_grads, weights, momentum, right_factor):
    grads_all = lax.all_gather(out_grads, "col", axis=0, tiled=True)
    gradient = lax.dot_general(
        grads_all,
        lax.all_gather(inputs, "row", axis=0, tiled=True),
        (((0,), (0,)), ((), ())),
        preferred_element_type=jnp.float32,
    )
    moment = momentum + gradient
    sketch_part = jnp.dot(moment, right_factor, precision=highest)
    sketch_rows = lax.psum(sketch_part, "col")
    gram_total = lax.psum(inner_rows(sketch_rows, sketch_rows), "row")
    basis_rows = orthonormal(sketch_rows, gram_total)
    right_part = inner_rows(moment, basis_rows)
    right_share = lax.psum_scatter(right_part, "row", scatter_dimension=0, tiled=True)
    squares = lax.psum(jnp.sum(right_share * right_share, axis=0), ("row", "col"))
    right_side = lax.all_gather(right_share, "row", axis=0, tiled=True)
    column_scale = lax.rsqrt(squares / N + tiny_eps)
    factor_new = right_side * column_scale
    momentum_new = moment - (1.0 - mix_rate) * jnp.dot(basis_rows, right_side.T, precision=highest)
    update = jnp.dot(basis_rows, factor_new.T, precision=highest)
    weights_new = (
        weights.astype(jnp.float32) * (1.0 - step_rate * weight_decay)
        - step_rate * math.sqrt(M / RANK) * update
    )
    return (weights_new, momentum_new, factor_new)


def solution(mesh):
    placed = (P("row", "col"), P("col", "row"), P("row", "col"), P("row", "col"), P("col", None))
    return jax.shard_map(
        on_device,
        mesh=mesh,
        in_specs=placed,
        out_specs=(P("row", "col"), P("row", "col"), P("col", None)),
        check_vma=False,
    )
```

profile of v0, /device:TPU:0, one launch (start us, length us, event | category | flops | bytes accessed | tf_op | source)
XLA Modules:
  0.0 616.2 jit_solution(3706774686516627048)
XLA Ops:
  7.2 0.7 all-gather.4.cloned.1.call-update
  8.0 0.7 all-gather.6.cloned.1.call-update
  8.7 59.7 %all-gather.4.cloned.1.call-done = bf16[2048,1280]{1,0:T(8,128)(2,1)} async-done(((bf16[256,1280]{1,0:T(8,128)(2,1)}), bf16[2048,1280]{1,0:T(8,128)(2,1)}) %all-gather.4.cloned.1.call-update) | async-done | bytes 5242896 | tf_op jit(solution)/shard_map/all_gather | solution.py:30
  68.4 127.4 %all-gather.6.cloned.1.call-done = bf16[2048,3200]{1,0:T(8,128)(2,1)} async-done(((bf16[512,3200]{1,0:T(8,128)(2,1)}), bf16[2048,3200]{1,0:T(8,128)(2,1)}) %all-gather.6.cloned.1.call-update) | async-done | bytes 13107216 | tf_op jit(solution)/shard_map/all_gather | solution.py:33
  195.8 29.4 %convolution_add_fusion = f32[1280,3200]{1,0:T(8,128)} fusion(f32[1280,3200]{1,0:T(8,128)} %param.8, bf16[2048,1280]{1,0:T(8,128)(2,1)} %all-gather.4.cloned.1.call-done, bf16[2048,3200]{1,0:T(8,128)(2,1)} %all-gather.6.cloned.1.call-done), kind=kOutput, calls=%fused_computation.2 | convolution fusion | flops 16781312000 | bytes 51118080 | tf_op jit(solution)/shard_map/dot_general | solution.py:31
  225.1 17.8 %fusion.15 = f32[1280,256]{1,0:T(8,128)} fusion(f32[1280,3200]{1,0:T(8,128)} %convolution_add_fusion, f32[3200,256]{1,0:T(8,128)S(1)} %copy-done), kind=kOutput, calls=%fused_computation.41 | convolution fusion | flops 12582912000 | bytes 20971520 | tf_op jit(solution)/shard_map/dot_general | solution.py:38
  243.0 60.5 %all-reduce.4.cloned.1.call-done = f32[1280,256]{1,0:T(8,128)} async-done(((f32[1280,256]{1,0:T(8,128)}), f32[1280,256]{1,0:T(8,128)}) %all-reduce.4.cloned.1.call-update) | async-done | bytes 1310736 | tf_op jit(solution)/shard_map/psum | solution.py:39
  303.5 4.8 fusion.16
  308.6 42.0 %all-reduce.6.cloned.1.call-done = f32[256,256]{0,1:T(8,128)} async-done(((f32[256,256]{0,1:T(8,128)}), f32[256,256]{0,1:T(8,128)}) %all-reduce.6.cloned.1.call-update) | async-done | bytes 262160 | tf_op jit(solution)/shard_map/psum | solution.py:40
  350.6 1.1 copy.9
  351.7 1.0 fusion.5
  352.7 11.7 %cholesky.50 = f32[128,128]{1,0:T(8,128)S(1)} custom-call(f32[128,128]{1,0:T(8,128)S(1)} %cholesky.118), custom_call_target="Cholesky" | custom-call | tf_op jit(solution)/shard_map/jit(cholesky)/cholesky | solution.py:25
  364.4 9.8 %custom-call.15 = f32[1,128,128]{1,2,0:T(8,128)S(1)} custom-call(f32[1,128,128]{2,1,0:T(8,128)S(1)} %get-tuple-element.24), custom_call_target="InvertDiagBlocksLowerTriangular" | custom-call | tf_op jit(solution)/shard_map/jit(cholesky)/cholesky | solution.py:25
  374.8 11.7 %cholesky.105 = f32[128,128]{1,0:T(8,128)S(1)} custom-call(f32[128,128]{1,0:T(8,128)S(1)} %convolution_subtract_fusion.1), custom_call_target="Cholesky" | custom-call | tf_op jit(solution)/shard_map/jit(cholesky)/cholesky | solution.py:25
  386.5 0.7 compare_reduce_fusion
  388.6 4.2 while.1
  388.8 0.6 fusion.31
  389.4 1.4 bitcast_dynamic-update-slice_fusion.2
  390.8 0.6 fusion.31
  391.4 1.4 bitcast_dynamic-update-slice_fusion.2
  392.8 19.7 %custom-call.16 = f32[2,128,128]{1,2,0:T(8,128)S(1)} custom-call(f32[2,128,128]{2,1,0:T(8,128)S(1)} %get-tuple-element.10), custom_call_target="InvertDiagBlocksLowerTriangular" | custom-call | tf_op jit(solution)/shard_map/jit(_solve_triangular)/triangular_solve | solution.py:26
  412.5 0.8 fusion.3
  413.3 1.2 convolution_subtract_fusion
  414.5 0.8 fusion.7
  415.2 32.1 %fusion.2 = f32[3200,256]{1,0:T(8,128)} fusion(f32[1280,3200]{1,0:T(8,128)} %convolution_add_fusion, f32[128,1280]{1,0:T(8,128)S(1)} %fusion.7, f32[128,1280]{1,0:T(8,128)S(1)} %fusion.3), kind=kOutput, calls=%fused_computation.11 | convolution fusion | flops 12583239680 | bytes 20971520 | tf_op jit(solution)/shard_map/dot_general | solution.py:21
  447.4 45.1 %reduce-scatter.2.cloned.1.call-done = f32[800,256]{1,0:T(8,128)} async-done(((f32[3200,256]{1,0:T(8,128)}), f32[800,256]{1,0:T(8,128)}) %reduce-scatter.2.cloned.1.call-update) | async-done | bytes 819216 | tf_op jit(solution)/shard_map/reduce_scatter | solution.py:43
  492.6 1.3 multiply_reduce_fusion
  493.8 40.3 %psum.23 = f32[256]{0:T(256)S(1)} all-reduce(f32[256]{0:T(256)S(1)} %multiply_reduce_fusion), channel_id=1, replica_groups=mesh['row'=4,'col'=8] {'row','col'}, use_global_device_ids=true, to_apply=%region_8.9 | all-reduce | flops 256 | bytes 2048 | tf_op jit(solution)/shard_map/psum | solution.py:44
  534.1 6.0 all-gather.8.cloned.1.call-done
  540.1 2.1 broadcast_multiply_fusion
  542.3 32.8 %fusion.1 = f32[1280,3200]{1,0:T(8,128)} fusion(f32[3200,256]{1,0:T(8,128)S(1)} %broadcast_multiply_fusion, bf16[1280,3200]{1,0:T(8,128)(2,1)} %param.7, f32[128,1280]{1,0:T(8,128)S(1)} %fusion.7, f32[128,1280]{1,0:T(8,128)S(1)} %fusion.3), kind=kOutput, calls=%fused_computation.6 | convolution fusion | flops 12599623680 | bytes 29163520 | tf_op jit(solution)/shard_map/dot_general | solution.py:49
  575.0 34.1 %fusion = f32[1280,3200]{1,0:T(8,128)} fusion(f32[1280,3200]{1,0:T(8,128)} %convolution_add_fusion, f32[3200,256]{1,0:T(8,128)S(1)} %copy-done.4, f32[128,1280]{1,0:T(8,128)} %copy-done.6, f32[128,1280]{1,0:T(8,128)} %copy-done.2), kind=kOutput, calls=%fused_computation.4 | convolution fusion | flops 12591431680 | bytes 37355520 | tf_op jit(solution)/shard_map/dot_general | solution.py:48
  (37 shorter events, 1.2 us)
Async XLA Ops:
  7.2 217.9 %copy-start = (f32[3200,256]{1,0:T(8,128)S(1)}, f32[3200,256]{1,0:T(8,128)}, u32[]{:S(2)}) copy-start(f32[3200,256]{1,0:T(8,128)} %param.9) | copy-start | bytes 9830404
  7.2 61.2 %all-gather.4.cloned.1.call-start = ((), (), s32[]{:S(2)}) async-start(), calls=%async_computation.1 | async-start | bytes 5898240 | tf_op jit(solution)/shard_map/all_gather | solution.py:30
  7.9 187.8 %all-gather.6.cloned.1.call-start = ((), (), s32[]{:S(2)}) async-start(), calls=%async_computation.2 | async-start | bytes 16384000 | tf_op jit(solution)/shard_map/all_gather | solution.py:33
  8.7 294.8 %all-reduce.4.cloned.1.call-start = ((), (), s32[]{:S(2)}) async-start(), calls=%async_computation.3 | async-start | bytes 2621440 | tf_op jit(solution)/shard_map/psum | solution.py:39
  242.9 107.7 %all-reduce.6.cloned.1.call-start = ((), (), s32[]{:S(2)}) async-start(), calls=%async_computation.4 | async-start | bytes 524288 | tf_op jit(solution)/shard_map/psum | solution.py:40
  303.5 109.0 %copy-start.5 = (f32[1280,256]{1,0:T(8,128)S(1)}, f32[1280,256]{1,0:T(8,128)}, u32[]{:S(2)}) copy-start(f32[1280,256]{1,0:T(8,128)} %all-reduce.4.cloned.1.call-done) | copy-start | bytes 3932164
  308.4 184.2 %reduce-scatter.2.cloned.1.call-start = ((), (), s32[]{:S(2)}) async-start(), calls=%async_computation.5 | async-start | bytes 4096000 | tf_op jit(solution)/shard_map/reduce_scatter | solution.py:43
  413.3 129.0 %copy-start.2 = (f32[128,1280]{1,0:T(8,128)}, f32[128,1280]{1,0:T(8,128)S(1)}, u32[]{:S(2)}) copy-start(f32[128,1280]{1,0:T(8,128)S(1)} %fusion.3) | copy-start | bytes 1966084
  415.2 127.0 %copy-start.6 = (f32[128,1280]{1,0:T(8,128)}, f32[128,1280]{1,0:T(8,128)S(1)}, u32[]{:S(2)}) copy-start(f32[128,1280]{1,0:T(8,128)S(1)} %fusion.7) | copy-start | bytes 1966084
  447.4 92.7 %all-gather.8.cloned.1.call-start = ((), (), s32[]{:S(2)}) async-start(), calls=%async_computation.6 | async-start | bytes 4096000 | tf_op jit(solution)/shard_map/all_gather | solution.py:45
  542.2 32.8 %copy-start.3 = (f32[3200,256]{1,0:T(8,128)}, f32[3200,256]{1,0:T(8,128)S(1)}, u32[]{:S(2)}) copy-start(f32[3200,256]{1,0:T(8,128)S(1)} %broadcast_multiply_fusion) | copy-start | bytes 9830404
  542.3 32.8 %copy-start.4 = (f32[3200,256]{1,0:T(8,128)S(1)}, f32[3200,256]{1,0:T(8,128)}, u32[]{:S(2)}) copy-start(f32[3200,256]{1,0:T(8,128)} %all-gather.8.cloned.1.call-done) | copy-start | bytes 9830404
  575.0 34.1 %copy-start.1 = (f32[3200,256]{1,0:T(8,128)S(1)}, f32[3200,256]{1,0:T(8,128)}, u32[]{:S(2)}) copy-start(f32[3200,256]{1,0:T(8,128)} %param.9) | copy-start | bytes 9830404
Sparse Core Ops, SparseCore 0:
  9.6 58.6 all-gather.3
  70.2 125.5 all-gather.5
  243.0 60.4 all-reduce.3
  308.5 42.0 all-reduce.5
  447.5 44.9 reduce-scatter.1
  494.2 45.7 all-gather.7
where the time goes:
time: 623 us; the launch traced here: 616 us
  waiting for transfers between devices  342 us (55%)
  matrix products  154 us (25%)
  other arithmetic  58.1 us (9%)
  blocking collectives  40.3 us (6%)
  between operations  15.8 us (3%)
    all_gather x1, waiting for transfers between devices, on_device(): lax.all_gather(inputs, 'row', axis=0, tiled=True)  127 us
    psum x1, waiting for transfers between devices, on_device(): sketch_rows = lax.psum(sketch_part, 'col')  60.5 us
    all_gather x1, waiting for transfers between devices, on_device(): grads_all = lax.all_gather(out_grads, 'col', axis=0, tiled=True)  59.7 us
    reduce_scatter x1, waiting for transfers between devices, on_device(): lax.psum_scatter(right_part, 'row', scatter_dimension=0, tiled=True)  45.1 us
    psum x1, waiting for transfers between devices, on_device(): gram_total = lax.psum(inner_rows(sketch_rows, sketch_rows), 'row')  42 us
    psum x1, blocking collectives, on_device(): lax.psum(jnp.sum(right_share * right_share, axis=0), ('row', 'col'))  40.3 us
    dot_general x2, matrix products, inner_rows(): lax.dot_general(left_side, right_in, (((0,), (0,)), ((), ())), precision=...  36.9 us
    dot_general x1, matrix products, on_device(): jnp.dot(basis_rows, right_side.T, precision=highest)  34.1 us
  transfers between devices with their start and end apart: 6, of which 6 were waited for; matrix products, arithmetic and copies ran while one was open for 0% of the time, Pallas kernels for 0%

commit v1 on v0

v1 whole, which is shorter than its diff:
```python
import functools
import math

import jax
import jax.numpy as jnp
from jax import lax
from jax.experimental import pallas as pl
from jax.experimental.pallas import tpu as pltpu
from jax.sharding import PartitionSpec as P


mix_rate = 0.95
step_rate = 0.3
weight_decay = 0.1
tiny_eps = 1e-06
highest = lax.Precision.HIGHEST
high = lax.Precision.HIGH
f32 = jnp.float32


def mm(a, b, dims, precision=None):
    return lax.dot_general(a, b, (dims, ((), ())), precision=precision, preferred_element_type=f32)


def general(n_total, m_total, inputs, out_grads, weights, momentum, right_factor):
    rank = right_factor.shape[1]
    grads_all = lax.all_gather(out_grads, "col", axis=0, tiled=True)
    inputs_all = lax.all_gather(inputs, "row", axis=0, tiled=True)
    moment = momentum + mm(grads_all, inputs_all, ((0,), (0,)))
    sketch = lax.psum(mm(moment, right_factor, ((1,), (0,)), highest), "col")
    gram = lax.psum(mm(sketch, sketch, ((0,), (0,)), highest), "row")
    inverse = inverse_factor(gram)
    basis = mm(sketch, inverse, ((1,), (1,)), highest)
    right_side = lax.psum(mm(moment, basis, ((0,), (0,)), highest), "row")
    squares = lax.psum(jnp.sum(right_side * right_side, axis=0), "col")
    factor_new = right_side * lax.rsqrt(squares / n_total + tiny_eps)
    momentum_new = moment - (1.0 - mix_rate) * mm(basis, right_side, ((1,), (1,)), highest)
    update = mm(basis, factor_new, ((1,), (1,)), highest)
    weights_new = (
        weights.astype(f32) * (1.0 - step_rate * weight_decay)
        - step_rate * math.sqrt(m_total / rank) * update
    )
    return (weights_new, momentum_new, factor_new)


def base_inverse(a):
    n = a.shape[0]
    rows = lax.broadcasted_iota(jnp.int32, (n, n), 0)
    cols = lax.broadcasted_iota(jnp.int32, (n, n), 1)
    left = a
    right = jnp.where(rows == cols, 1.0, 0.0).astype(f32)
    pivots = jnp.ones((n, n), f32)
    step = 8
    for start in range(0, n, step):
        columns = [jnp.broadcast_to(left[:, start + i : start + i + 1], (n, n)) for i in range(step)]
        for i in range(step):
            j = start + i
            pivot = jnp.broadcast_to(columns[i][j : j + 1, :], (n, n))
            pivots = jnp.where(rows == j, pivot, pivots)
            if j + 1 == n:
                break
            ratio = jnp.where(rows > j, columns[i] * (1.0 / pivot), 0.0)
            for k in range(i + 1, step):
                columns[k] = columns[k] - ratio * jnp.broadcast_to(columns[k][j : j + 1, :], (n, n))
            left = left - ratio * jnp.broadcast_to(left[j : j + 1, :], (n, n))
            right = right - ratio * jnp.broadcast_to(right[j : j + 1, :], (n, n))
    root = lax.rsqrt(pivots)
    return right * (root * (1.5 - 0.5 * pivots * root * root))


def inverse_kernel(gram_ref, out_ref, work_ref):
    n = gram_ref.shape[0]
    work_ref[...] = gram_ref[...]
    out_ref[...] = jnp.zeros_like(out_ref)

    def solve(at, size):
        span = slice(at, at + size)
        if size <= 32:
            out_ref[span, span] = base_inverse(work_ref[span, span])
            return
        half = size // 2
        one, two = slice(at, at + half), slice(at + half, at + size)
        solve(at, half)
        inv_one = out_ref[one, one]
        low = mm(work_ref[two, one], inv_one, ((1,), (1,)), highest)
        work_ref[two, two] = work_ref[two, two] - mm(low, low, ((1,), (1,)), highest)
        side = mm(low, inv_one, ((1,), (0,)), highest)
        solve(at + half, half)
        out_ref[two, one] = -mm(out_ref[two, two], side, ((1,), (0,)), highest)

    solve(0, n)


def inverse_factor(gram):
    return pl.pallas_call(
        inverse_kernel,
        out_shape=jax.ShapeDtypeStruct(gram.shape, f32),
        in_specs=[pl.BlockSpec(memory_space=pltpu.VMEM)],
        out_specs=pl.BlockSpec(memory_space=pltpu.VMEM),
        scratch_shapes=[pltpu.VMEM(gram.shape, f32)],
        name="inverse_factor",
        cost_estimate=pl.CostEstimate(flops=20_000_000_000, bytes_accessed=10_000_000, transcendentals=0),
    )(gram)


bf16 = jnp.bfloat16
whole_vmem = pl.BlockSpec(memory_space=pltpu.VMEM)
whole_smem = pl.BlockSpec(memory_space=pltpu.SMEM)


def split(x):
    big = x.astype(bf16)
    return big, (x - big.astype(f32)).astype(bf16)


def tile_of(n):
    return 640 if n % 640 == 0 else n


def call(kernel, outs, ins, specs, out_specs, grid=(), scratch=(), flops=0, moved=0, aliases={}):
    return pl.pallas_call(
        kernel,
        out_shape=outs,
        grid=grid,
        in_specs=specs,
        out_specs=out_specs,
        scratch_shapes=list(scratch),
        input_output_aliases=aliases,
        compiler_params=pltpu.CompilerParams(dimension_semantics=("arbitrary",) * len(grid)),
        cost_estimate=pl.CostEstimate(flops=flops, bytes_accessed=moved, transcendentals=0),
    )(*ins)


def shaped(shape, dtype=f32):
    return jax.ShapeDtypeStruct(shape, dtype)


def sketch_kernel(ids, part, *refs):
    grads, rights, keep, send, big, low = refs[:4], refs[4:8], refs[8], refs[9], refs[10], refs[11]
    z, core, shift = ids[1], ids[2], ids[3]
    for k in range(4):
        big[k], low[k] = split(rights[k][...])
    rows = keep.shape[0] // 4
    for out, half in ((keep, core), (send, 1 - core)):
        for b in range(4):
            at = pl.ds(pl.multiple_of(half * (4 * rows) + (z ^ b) * rows, 32), rows)
            total = part[at, :]
            for k in range(4):
                g = grads[k][at, :]
                total += mm(g, big[k ^ shift], ((1,), (0,)))
                total += mm(g, low[k ^ shift], ((1,), (0,)))
            out[b * rows : (b + 1) * rows, :] = total


def gram_kernel(ids, *refs):
    parts, other, grads = refs[:4], refs[4], refs[5:9]
    sketch, gram, tokens, big_t, low_t, flip = refs[9:]
    row, z, core, shift = ids[0], ids[1], ids[2], ids[3]
    rows = parts[0].shape[0]
    for k in range(4):
        at = pl.multiple_of((z ^ k) * rows, 32)
        sketch[pl.ds(core * (4 * rows) + at, rows), :] = parts[k][...]
        sketch[pl.ds((1 - core) * (4 * rows) + at, rows), :] = other[k * rows : (k + 1) * rows, :]
    s = sketch[...]
    gram[...] = mm(s, s, ((0,), (0,)), highest)
    big, low = split(s)
    for k in range(4):
        g = grads[k][...]
        tokens[k ^ shift] = mm(g, big, ((0,), (0,))) + mm(g, low, ((0,), (0,)))
    flip[...] = s.T
    size = flip.shape[0] // 8
    for i in range(8):
        at = pl.multiple_of(rank_block(row, i) * size, 32)
        b, l = split(flip[pl.ds(at, size), :])
        big_t[i * size : (i + 1) * size, :] = b
        low_t[i * size : (i + 1) * size, :] = l


def rank_block(row, i):
    bit_x, bit_y = row % 2, row // 2
    upper, lower = (i // 2) % 2, i % 2
    if i < 4:
        return 2 * (upper ^ bit_x) + (lower ^ bit_y)
    return 4 + 2 * (upper ^ bit_y) + (lower ^ bit_x)


def side_kernel(big_t, low_t, momentum, top_keep, top_send, low_keep, low_send):
    mb, ml = split(momentum[...])
    total = mm(big_t[...], mb, ((1,), (0,)))
    total += mm(big_t[...], ml, ((1,), (0,)))
    total += mm(low_t[...], mb, ((1,), (0,)))
    n = top_keep.shape[0]
    for i, ref in enumerate((top_keep, top_send, low_keep, low_send)):
        ref[...] = total[i * n : (i + 1) * n, :]


def token_kernel(ids, own, other, inputs, *refs):
    before, after_refs, flip, tok = refs[:4], refs[4:8], refs[8], refs[9]
    row, core = ids[0], ids[2]
    half = own.shape[0]
    size = flip.shape[0] // 8

    @pl.when(pl.program_id(0) == 0)
    def _():
        for ref, place in ((own, core), (other, 1 - core)):
            flip[...] = ref[...].T
            for i in range(8):
                at = pl.multiple_of(rank_block(row, i) * size, 32)
                b, l = split(flip[pl.ds(at, size), :])
                tok[place, 0, i * size : (i + 1) * size, :] = b
                tok[place, 1, i * size : (i + 1) * size, :] = l

    total = 0.0
    for h in range(2):
        x = inputs[h * half : (h + 1) * half, :]
        total += mm(tok[h, 0], x, ((1,), (0,)))
        total += mm(tok[h, 1], x, ((1,), (0,)))
    n = after_refs[0].shape[0]
    for i in range(4):
        after_refs[i][...] = before[i][...] + total[i * n : (i + 1) * n, :]


def gradient_kernel(count, ids, *refs):
    own, other, blocks, base, out = refs[:count], refs[count : 2 * count], refs[2 * count : 3 * count], refs[3 * count], refs[3 * count + 1]
    core = ids[2]
    half = blocks[0].shape[0] // 2
    total = base[...]
    for mine, its, x in zip(own, other, blocks):
        at = pl.multiple_of(core * half, half)
        total += mm(mine[0], x[pl.ds(at, half), :], ((1,), (0,)))
        at = pl.multiple_of((1 - core) * half, half)
        total += mm(its[0], x[pl.ds(at, half), :], ((1,), (0,)))
    out[...] = total


def right_kernel(ids, inverse, sketch, *refs):
    pieces, right, squares, basis, work = refs[:6], refs[6], refs[7], refs[8], refs[9]
    row = ids[0]
    size = work.shape[0] // 8

    @pl.when(pl.program_id(0) == 0)
    def _():
        sb, sl = split(sketch[...])
        ib, il = split(inverse[...])
        basis[...] = mm(sb, ib, ((1,), (1,))) + mm(sb, il, ((1,), (1,))) + mm(sl, ib, ((1,), (1,)))
        squares[...] = jnp.zeros_like(squares)

    place = 0
    for ref in pieces:
        for i in range(ref.shape[0] // size):
            at = pl.multiple_of(rank_block(row, place) * size, 32)
            work[pl.ds(at, size), :] = ref[i * size : (i + 1) * size, :]
            place += 1
    ib, il = split(inverse[...])
    tb, tl = split(work[...])
    total = mm(ib, tb, ((1,), (0,))) + mm(ib, tl, ((1,), (0,))) + mm(il, tb, ((1,), (0,)))
    right[...] = total
    sb, sl = split(total * total)
    ones = jnp.ones((8, total.shape[1]), bf16)
    squares[...] += mm(ones, sb, ((1,), (1,))) + mm(ones, sl, ((1,), (1,)))


def weights_kernel(n_total, factor, squares, basis, right, weights, out, factor_out, big, low):
    scale = lax.rsqrt(squares[0:1, :] / n_total + tiny_eps)

    @pl.when(pl.program_id(0) == 0)
    def _():
        big[...], low[...] = split(basis[...] * (scale * -factor))

    rb, rl = split(right[...])
    update = mm(big[...], rb, ((1,), (0,))) + mm(big[...], rl, ((1,), (0,))) + mm(low[...], rb, ((1,), (0,)))
    out[...] = weights[...].astype(f32) * (1.0 - step_rate * weight_decay) + update
    factor_out[...] = right[...].T * scale


def momentum_kernel(ids, own, other, first, second, basis, right, base, out, table, small):
    core = ids[2]

    @pl.when(pl.program_id(0) == 0)
    def _():
        table[core] = own[0]
        table[1 - core] = other[0]
        small[...] = (basis[...] * -(1.0 - mix_rate)).astype(bf16)

    total = base[...]
    total += mm(table[0], first[...], ((1,), (0,)))
    total += mm(table[1], second[...], ((1,), (0,)))
    total += mm(small[...], right[...].astype(bf16), ((1,), (0,)))
    out[...] = total


def swap(x, axis, bit):
    size = lax.axis_size(axis)
    return lax.ppermute(x, axis, [(i, i ^ bit) for i in range(size)])


def plane(n_total, m_total, inputs, out_grads, weights, momentum, right_factor):
    return plane_body(n_total, m_total, inputs, out_grads, weights, momentum, right_factor)


def plane_body(n_total, m_total, inputs, out_grads, weights, momentum, right_factor):
    rank = right_factor.shape[1]
    row = lax.axis_index("row")
    col = lax.axis_index("col")
    core, z = col % 2, col // 2
    ids = jnp.stack([row, z, core, row ^ z]).astype(jnp.int32)
    tokens, n = inputs.shape
    m = momentum.shape[0]
    block = out_grads.shape[0]
    tn = tile_of(n)
    quarter = [1, 2, 3]
    tiles = (n // tn,)

    def columns(rows):
        return pl.BlockSpec((rows, tn), lambda i: (0, i))

    grads = out_grads.T
    own = [grads] + [swap(grads, "col", 2 * k) for k in quarter]

    in_right = mm(inputs.astype(f32), right_factor, ((1,), (0,)), high)
    flipped = jnp.where(core == 0, 0, 1)
    keep = lax.dynamic_slice_in_dim(in_right, flipped * block, block, 0)
    send = lax.dynamic_slice_in_dim(in_right, (1 - flipped) * block, block, 0)
    in_right = keep + swap(send, "col", 1)
    rights = [in_right] + [swap(in_right, "row", k) for k in quarter]
    x_all = swap(inputs, "row", 1)
    y_all = swap(inputs, "row", 2)
    other = [swap(g, "col", 1) for g in own]

    part = mm(momentum, right_factor, ((1,), (0,)), high)
    keep, send = call(
        sketch_kernel, (shaped((m // 2, rank)),) * 2, (ids, part, *own, *rights),
        [whole_smem] + [whole_vmem] * 9, (whole_vmem,) * 2,
        scratch=[pltpu.VMEM((4, block, rank), bf16)] * 2, flops=4 * m * 4 * block * rank, moved=8_000_000)
    mine = keep + swap(send, "col", 1)
    size = m // 8
    total = mine[:size]
    for k in quarter:
        total = total + swap(mine[k * size : (k + 1) * size], "col", 2 * k)
    parts = [total] + [swap(total, "col", 2 * k) for k in quarter]
    rest = swap(jnp.concatenate(parts, axis=0), "col", 1)

    sketch, gram, toks, big_t, low_t = call(
        gram_kernel,
        (shaped((m, rank)), shaped((rank, rank)), shaped((4, block, rank)), shaped((rank, m), bf16), shaped((rank, m), bf16)),
        (ids, *parts, rest, *own), [whole_smem] + [whole_vmem] * 9, (whole_vmem,) * 5,
        scratch=[pltpu.VMEM((rank, m), f32)], flops=20 * m * rank * rank, moved=8_000_000)
    token = toks[0]
    for k in quarter:
        token = token + swap(toks[k], "row", k)
    token_other = swap(token, "col", 1)
    gram = gram + swap(gram, "row", 1)
    gram = gram + swap(gram, "row", 2)

    sides = call(
        side_kernel, (shaped((rank // 4, n)),) * 4, (big_t, low_t, momentum),
        [whole_vmem] * 2 + [columns(m)], (columns(rank // 4),) * 4, tiles,
        flops=6 * m * n * rank, moved=5 * m * n)
    top, top_send, low, low_send = call(
        token_kernel, (shaped((rank // 4, n)),) * 4,
        (ids, token, token_other, inputs, *sides),
        [whole_smem] + [whole_vmem] * 2 + [columns(tokens)] + [columns(rank // 4)] * 4, (columns(rank // 4),) * 4, tiles,
        scratch=[pltpu.VMEM((rank, block), f32), pltpu.VMEM((2, 2, rank, block), bf16)],
        flops=4 * tokens * n * rank, moved=10 * rank * n, aliases={4: 0, 5: 1, 6: 2, 7: 3})
    n8 = rank // 8
    top = top + swap(top_send, "row", 1)
    low = low + swap(low_send, "row", 2)
    top0 = top[:n8] + swap(top[n8:], "row", 2)
    low0 = low[:n8] + swap(low[n8:], "row", 1)
    top1 = swap(top0, "row", 2)
    low1 = swap(low0, "row", 1)
    top2 = swap(jnp.concatenate([top0, top1], axis=0), "row", 1)
    low2 = swap(jnp.concatenate([low0, low1], axis=0), "row", 2)

    inverse = inverse_factor(gram)
    half = tokens // 2
    d_first = swap(x_all[:half], "row", 2)
    d_second = swap(y_all[half:], "row", 1)

    own_all = jnp.stack(own)
    other_all = jnp.stack(other)

    def pick(j):
        return pl.BlockSpec((1, m, block), lambda i, ids: (ids[3] ^ j, 0, 0))

    def cols(rows):
        return pl.BlockSpec((rows, tn), lambda i, ids: (0, i))

    moment = pl.pallas_call(
        functools.partial(gradient_kernel, 3),
        grid_spec=pltpu.PrefetchScalarGridSpec(
            num_scalar_prefetch=1, grid=tiles,
            in_specs=[pick(0), pick(1), pick(2)] * 2 + [cols(tokens)] * 3 + [cols(m)],
            out_specs=cols(m)),
        out_shape=shaped((m, n)), name="gradient",
        cost_estimate=pl.CostEstimate(flops=6 * m * n * tokens, bytes_accessed=8 * m * n, transcendentals=0),
    )(ids, *([own_all] * 3), *([other_all] * 3), inputs, x_all, y_all, momentum)

    right, squares, basis = call(
        right_kernel, (shaped((rank, n)), shaped((8, rank)), shaped((m, rank))),
        (ids, inverse, sketch, top0, top1, top2, low0, low1, low2),
        [whole_smem] + [whole_vmem] * 2 + [columns(n8), columns(n8), columns(2 * n8)] * 2,
        (columns(rank), pl.BlockSpec((8, rank), lambda i: (0, 0)), pl.BlockSpec((m, rank), lambda i: (0, 0))), tiles,
        scratch=[pltpu.VMEM((rank, tn), f32)], flops=6 * n * rank * rank, moved=12 * n * rank)
    for bit in (1, 2, 4):
        squares = squares + swap(squares, "col", bit)
    weights_new, factor_new = call(
        functools.partial(weights_kernel, n_total, step_rate * math.sqrt(m_total / rank)),
        (shaped((m, n)), shaped((n, rank))), (squares, basis, right, weights),
        [whole_vmem] * 2 + [columns(rank), columns(m)],
        (columns(m), pl.BlockSpec((tn, rank), lambda i: (i, 0))), tiles,
        scratch=[pltpu.VMEM((m, rank), bf16)] * 2, flops=6 * m * n * rank, moved=6 * m * n)
    momentum_new = pl.pallas_call(
        momentum_kernel,
        grid_spec=pltpu.PrefetchScalarGridSpec(
            num_scalar_prefetch=1, grid=tiles,
            in_specs=[pick(3), pick(3), cols(half), cols(half), pl.BlockSpec((m, rank), lambda i, ids: (0, 0)), cols(rank), cols(m)],
            out_specs=cols(m),
            scratch_shapes=[pltpu.VMEM((2, m, block), bf16), pltpu.VMEM((m, rank), bf16)]),
        out_shape=shaped((m, n)), name="momentum", input_output_aliases={7: 0},
        cost_estimate=pl.CostEstimate(flops=2 * m * n * (tokens + rank), bytes_accessed=8 * m * n, transcendentals=0),
    )(ids, own_all, other_all, d_first, d_second, basis, right, moment)
    return (weights_new, momentum_new, factor_new)


def solution(mesh):
    n_row, n_col = mesh.shape["row"], mesh.shape["col"]
    fast = (n_row, n_col) == (4, 8)
    body = plane if fast else general

    def whole(inputs, out_grads, weights, momentum, right_factor):
        m_total, n_total = weights.shape
        return jax.shard_map(
            functools.partial(body, n_total, m_total),
            mesh=mesh,
            in_specs=(P("row", "col"), P("col", "row"), P("row", "col"), P("row", "col"), P("col", None)),
            out_specs=(P("row", "col"), P("row", "col"), P("col", None)),
            check_vma=False,
        )(inputs, out_grads, weights, momentum, right_factor)

    return whole
```

time: 623 us -> 409 us (0.66)
  matrix products: 154 us -> 15 us
  waiting for transfers between devices: 342 us -> 206 us
  Pallas kernels: 0 us -> 114 us
  other arithmetic: 58.1 us -> 15.7 us
  starting transfers between devices: 0.41 us -> 42.8 us
  blocking collectives: 40.3 us -> 0 us
  between operations: 15.8 us -> 1.08 us
  local copies, waits for them, and re-layouts: 5.14 us -> 13.4 us
    ppermute x0 -> x40, waiting for transfers between devices: none -> 206 us  [swap(): return lax.ppermute(x, axis, [(i, i ^ bit) for i in range(size)])]
    all_gather x3 -> x0, waiting for transfers between devices: 193 us -> none  [the longest x1 127 us: on_device(): lax.all_gather(inputs, 'row', axis=0, tiled=True)]
    dot_general x6 -> x2, matrix products: 151 us -> 15 us  [mm(): lax.dot_general(a, b, (dims, ((), ())), precision=precision, preferred_el...]
    pallas_call x0 -> x9, Pallas kernels: none -> 114 us  [the longest x6 56.3 us: call(): pl.pallas_call(kernel, out_shape=outs, grid=grid, in_specs=specs, out_spe...]
    psum x2 -> x0, waiting for transfers between devices: 103 us -> none  [the longest x1 60.5 us: on_device(): sketch_rows = lax.psum(sketch_part, 'col')]
    another operation x9 -> x3, other arithmetic: 53.7 us -> 7.52 us  [the longest x1 3.48 us: plane_body(): other_all = jnp.stack(other)]
    reduce_scatter x1 -> x0, waiting for transfers between devices: 45.1 us -> none  [on_device(): lax.psum_scatter(right_part, 'row', scatter_dimension=0, tiled=True)]
    ppermute x0 -> x40, starting transfers between devices: none -> 42.8 us  [swap(): return lax.ppermute(x, axis, [(i, i ^ bit) for i in range(size)])]
  transfers between devices with their start and end apart: 6 -> 40, of which waited for: 6 -> 20; matrix products, arithmetic and copies ran while one was open for 0% -> 6% of each run, Pallas kernels for 0% -> 19%
where the time goes in v1:
time: 409 us; the launch traced here: 408 us
  waiting for transfers between devices  206 us (50%)
  Pallas kernels  114 us (28%)
  starting transfers between devices  42.8 us (10%)
  other arithmetic  15.7 us (4%)
  matrix products  15 us (4%)
  local copies, waits for them, and re-layouts  13.4 us (3%)
    ppermute x40, waiting for transfers between devices, swap(): return lax.ppermute(x, axis, [(i, i ^ bit) for i in range(size)])  206 us
    pallas_call x6, Pallas kernels, call(): pl.pallas_call(kernel, out_shape=outs, grid=grid, in_specs=specs, out_spe...  56.3 us
    ppermute x40, starting transfers between devices, swap(): return lax.ppermute(x, axis, [(i, i ^ bit) for i in range(size)])  42.8 us
    pallas_call x1, Pallas kernels, plane_body(): pl.pallas_call(functools.partial(gradient_kernel, 3), grid_spec=pltpu.Pre...  23.7 us
    pallas_call x1, Pallas kernels, plane_body(): pl.pallas_call(momentum_kernel, grid_spec=pltpu.PrefetchScalarGridSpec(nu...  20.3 us
    dot_general x2, matrix products, mm(): lax.dot_general(a, b, (dims, ((), ())), precision=precision, preferred_el...  15 us
    pallas_call x1, Pallas kernels, inverse_factor(): pl.pallas_call(inverse_kernel, out_shape=jax.ShapeDtypeStruct(gram.shape,...  13.7 us
    unnamed x53, local copies, waits for them, and re-layouts  10.8 us
  transfers between devices with their start and end apart: 40, of which 20 were waited for; matrix products, arithmetic and copies ran while one was open for 6% of the time, Pallas kernels for 19%

profile of v1, /device:TPU:0, one launch (start us, length us, event | category | flops | bytes accessed | tf_op | source)
XLA Modules:
  0.0 408.1 jit_solution(6834028070640678564)
XLA Ops:
  2.6 3.9 fusion.6
  10.2 3.9 collective-permute-start.6
  16.2 3.6 collective-permute-start.2
  22.4 11.2 %fusion.5.part = f32[1280,256]{1,0:T(8,128)} fusion(f32[1280,3200]{1,0:T(8,128)} %refs_9_.1, f32[3200,256]{1,0:T(8,128)S(1)} %copy-done), kind=kOutput, calls=%fused_computation.20 | convolution fusion | flops 6291456000 | bytes 20971520 | tf_op jit(solution)/shard_map/dot_general | solution.py:22
  36.0 40.1 %collective-permute-done.1.refs_2_.refs_7_ = bf16[1280,256]{1,0:T(8,128)(2,1)} collective-permute-done((bf16[1280,256]{1,0:T(8,128)(2,1)}, bf16[1280,256]{1,0:T(8,128)(2,1)}, u32[]{:S(2)}, u32[]{:S(2)}) %collective-permute-start.1) | collective-permute-done | bytes 655392 | tf_op jit(solution)/shard_map/ppermute | solution.py:294
  76.2 5.0 %shard_map.76 = (f32[640,256]{1,0:T(8,128)}, f32[640,256]{1,0:T(8,128)}) custom-call(s32[4]{0:T(128)} %pad_add_fusion.ids, f32[1280,256]{1,0:T(8,128)} %fusion.5.part, bf16[1280,256]{1,0:T(8,128)(2,1)} %bitcast.33, bf16[1280,256]{1,0:T(8,128)(2,1)} %collective-permute-done.refs_1_.refs_6_, bf16[1280,256]{1,0:T(8,128)(2,1)} %collective-permute-done.1.refs_2_.refs_7_, ...), custom_call_target="tpu_custom_call" | custom-call | flops 1342177280 | bytes 8000000 | tf_op jit(solution)/shard_map/pallas_call | solution.py:121
  81.1 2.3 collective-permute-done.7
  84.7 2.5 collective-permute-start.10
  88.2 2.8 collective-permute-done.8
  90.9 4.9 %collective-permute-done.10 = f32[160,256]{1,0:T(8,128)S(1)} collective-permute-done((f32[160,256]{1,0:T(8,128)S(1)}, f32[160,256]{1,0:T(8,128)S(1)}, u32[]{:S(2)}, u32[]{:S(2)}) %collective-permute-start.10) | collective-permute-done | bytes 163872 | tf_op jit(solution)/shard_map/ppermute | solution.py:294
  95.8 6.8 %collective-permute-done.9 = f32[160,256]{1,0:T(8,128)S(1)} collective-permute-done((f32[160,256]{1,0:T(8,128)S(1)}, f32[160,256]{1,0:T(8,128)S(1)}, u32[]{:S(2)}, u32[]{:S(2)}) %collective-permute-start.9) | collective-permute-done | bytes 163872 | tf_op jit(solution)/shard_map/ppermute | solution.py:294
  102.7 2.9 collective-permute-start.13
  107.2 4.5 %collective-permute-done.13.refs_3_ = f32[160,256]{1,0:T(8,128)S(1)} collective-permute-done((f32[160,256]{1,0:T(8,128)S(1)}, f32[160,256]{1,0:T(8,128)S(1)}, u32[]{:S(2)}, u32[]{:S(2)}) %collective-permute-start.13) | collective-permute-done | bytes 163872 | tf_op jit(solution)/shard_map/ppermute | solution.py:294
  111.7 6.4 %collective-permute-done.12.refs_2_ = f32[160,256]{1,0:T(8,128)S(1)} collective-permute-done((f32[160,256]{1,0:T(8,128)S(1)}, f32[160,256]{1,0:T(8,128)S(1)}, u32[]{:S(2)}, u32[]{:S(2)}) %collective-permute-start.12) | collective-permute-done | bytes 163872 | tf_op jit(solution)/shard_map/ppermute | solution.py:294
  121.1 6.0 %shard_map.77 = (f32[1280,256]{1,0:T(8,128)}, f32[256,256]{1,0:T(8,128)}, f32[4,256,256]{2,1,0:T(8,128)}, bf16[256,1280]{1,0:T(8,128)(2,1)}, bf16[256,1280]{1,0:T(8,128)(2,1)}) custom-call(s32[4]{0:T(128)} %pad_add_fusion.ids, f32[160,256]{1,0:T(8,128)} %copy-done.18, f32[160,256]{1,0:T(8,128)} %copy-done.23, f32[160,256]{1,0:T(8,128)} %copy-done.22, ...), custom_call_target="tpu_custom_call" | custom-call | flops 1677721600 | bytes 8000000 | tf_op jit(solution)/shard_map/pallas_call | solution.py:121
  131.9 5.7 %collective-permute-done.17 = f32[256,256]{1,0:T(8,128)S(1)} collective-permute-done((f32[256,256]{1,0:T(8,128)S(1)}, f32[256,256]{1,0:T(8,128)S(1)}, u32[]{:S(2)}, u32[]{:S(2)}) %collective-permute-start.17) | collective-permute-done | bytes 262176 | tf_op jit(solution)/shard_map/ppermute | solution.py:294
  137.6 4.8 %collective-permute-done.19 = f32[256,256]{1,0:T(8,128)S(1)} collective-permute-done((f32[256,256]{1,0:T(8,128)S(1)}, f32[256,256]{1,0:T(8,128)S(1)}, u32[]{:S(2)}, u32[]{:S(2)}) %collective-permute-start.19) | collective-permute-done | bytes 262176 | tf_op jit(solution)/shard_map/ppermute | solution.py:294
  144.9 12.6 %shard_map.78 = (f32[64,3200]{1,0:T(8,128)}, f32[64,3200]{1,0:T(8,128)}, f32[64,3200]{1,0:T(8,128)}, f32[64,3200]{1,0:T(8,128)}) custom-call(bf16[256,1280]{1,0:T(8,128)(2,1)} %get-tuple-element.28.big_t, bf16[256,1280]{1,0:T(8,128)(2,1)} %get-tuple-element.29.low_t, f32[1280,3200]{1,0:T(8,128)} %refs_9_.1), custom_call_target="tpu_custom_call" | custom-call | flops 6291456000 | bytes 20480000 | tf_op jit(solution)/shard_map/pallas_call | solution.py:121
  158.2 7.9 %shard_map.79 = (f32[64,3200]{1,0:T(8,128)}, f32[64,3200]{1,0:T(8,128)}, f32[64,3200]{1,0:T(8,128)}, f32[64,3200]{1,0:T(8,128)}) custom-call(s32[4]{0:T(128)} %pad_add_fusion.ids, f32[256,256]{1,0:T(8,128)} %copy-done.15, f32[256,256]{1,0:T(8,128)} %copy-done.19, ...), custom_call_target="tpu_custom_call", output_to_operand_aliasing={{0}: (4, {}), {1}: (5, {}), {2}: (6, {}), {3}: (7, {})} | custom-call | flops 1677721600 | bytes 8192000 | tf_op jit(solution)/shard_map/pallas_call | solution.py:121
  170.8 16.7 %collective-permute-done.21 = f32[64,3200]{1,0:T(8,128)S(1)} collective-permute-done((f32[64,3200]{1,0:T(8,128)}, f32[64,3200]{1,0:T(8,128)S(1)}, u32[]{:S(2)}, u32[]{:S(2)}) %collective-permute-start.21) | collective-permute-done | bytes 819232 | tf_op jit(solution)/shard_map/ppermute | solution.py:294
  190.4 2.7 collective-permute-done.15
  194.8 3.4 pad_maximum_fusion.refs_0_.refs_1_.refs_2_.own
  198.2 73.7 %collective-permute-done.16 = f32[256,256]{1,0:T(8,128)S(1)} collective-permute-done((f32[256,256]{1,0:T(8,128)S(1)}, f32[256,256]{1,0:T(8,128)S(1)}, u32[]{:S(2)}, u32[]{:S(2)}) %collective-permute-start.16) | collective-permute-done | bytes 262176 | tf_op jit(solution)/shard_map/ppermute | solution.py:294
  274.9 9.9 %collective-permute-done.26 = f32[32,3200]{1,0:T(8,128)S(1)} collective-permute-done((f32[32,3200]{1,0:T(8,128)S(1)}, f32[32,3200]{1,0:T(8,128)S(1)}, u32[]{:S(2)}, u32[]{:S(2)}) %collective-permute-start.26) | collective-permute-done | bytes 409632 | tf_op jit(solution)/shard_map/ppermute | solution.py:294
  286.3 8.9 %collective-permute-done.23.refs_1_ = f32[32,3200]{1,0:T(8,128)S(1)} collective-permute-done((f32[32,3200]{1,0:T(8,128)S(1)}, f32[32,3200]{1,0:T(8,128)S(1)}, u32[]{:S(2)}, u32[]{:S(2)}) %collective-permute-start.23) | collective-permute-done | bytes 409632 | tf_op jit(solution)/shard_map/ppermute | solution.py:294
  297.7 7.2 %collective-permute-done.27.refs_4_ = f32[32,3200]{1,0:T(8,128)S(1)} collective-permute-done((f32[32,3200]{1,0:T(8,128)S(1)}, f32[32,3200]{1,0:T(8,128)S(1)}, u32[]{:S(2)}, u32[]{:S(2)}) %collective-permute-start.27) | collective-permute-done | bytes 409632 | tf_op jit(solution)/shard_map/ppermute | solution.py:294
  311.4 13.7 %inverse_factor.1.inverse = f32[256,256]{1,0:T(8,128)} custom-call(f32[256,256]{1,0:T(8,128)} %add.71.gram_ref), custom_call_target="tpu_custom_call" | custom-call | flops 20000000000 | bytes 10000000 | tf_op jit(solution)/shard_map/inverse_factor/pallas_call | solution.py:95
  332.0 8.4 %shard_map.80 = (f32[256,3200]{1,0:T(8,128)}, f32[8,256]{1,0:T(8,128)}, f32[1280,256]{1,0:T(8,128)}) custom-call(s32[4]{0:T(128)} %pad_add_fusion.ids, f32[256,256]{1,0:T(8,128)} %inverse_factor.1.inverse, f32[1280,256]{1,0:T(8,128)} %get-tuple-element.26.sketch, f32[32,3200]{1,0:T(8,128)} %copy-done.8, f32[32,3200]{1,0:T(8,128)} %copy-done.12, ...), custom_call_target="tpu_custom_call" | custom-call | flops 1258291200 | bytes 9830400 | tf_op jit(solution)/shard_map/pallas_call | solution.py:121
  340.5 3.5 pad_maximum_fusion.1.refs_3_.refs_4_.refs_5_.other
  344.1 23.7 %gradient.1.base = f32[1280,3200]{1,0:T(8,128)} custom-call(s32[4]{0:T(128)} %pad_add_fusion.ids, bf16[4,1280,256]{2,1,0:T(8,128)(2,1)} %pad_maximum_fusion.refs_0_.refs_1_.refs_2_.own, bf16[4,1280,256]{2,1,0:T(8,128)(2,1)} %pad_maximum_fusion.refs_0_.refs_1_.refs_2_.own, bf16[4,1280,256]{2,1,0:T(8,128)(2,1)} %pad_maximum_fusion.refs_0_.refs_1_.refs_2_.own, ...), custom_call_target="tpu_custom_call" | custom-call | flops 12582912000 | bytes 32768000 | tf_op jit(solution)/shard_map/gradient/pallas_call | solution.py:389
  370.7 20.3 %momentum.3 = f32[1280,3200]{1,0:T(8,128)} custom-call(s32[4]{0:T(128)} %pad_add_fusion.ids, bf16[4,1280,256]{2,1,0:T(8,128)(2,1)} %pad_maximum_fusion.refs_0_.refs_1_.refs_2_.own, bf16[4,1280,256]{2,1,0:T(8,128)(2,1)} %pad_maximum_fusion.1.refs_3_.refs_4_.refs_5_.other, bf16[256,3200]{1,0:T(8,128)(2,1)} %copy-done.14, ...), custom_call_target="tpu_custom_call", output_to_operand_aliasing={{}: (7, {})} | custom-call | flops 6291456000 | bytes 32768000 | tf_op jit(solution)/shard_map/momentum/pallas_call | solution.py:413
  391.7 16.4 %shard_map.81 = (f32[1280,3200]{1,0:T(8,128)}, f32[3200,256]{1,0:T(8,128)}) custom-call(f32[8,256]{1,0:T(8,128)} %add.81.squares, f32[1280,256]{1,0:T(8,128)} %get-tuple-element.39.basis, f32[256,3200]{1,0:T(8,128)} %get-tuple-element.40.right, bf16[1280,3200]{1,0:T(8,128)(2,1)} %weights.1), custom_call_target="tpu_custom_call" | custom-call | flops 6291456000 | bytes 24576000 | tf_op jit(solution)/shard_map/pallas_call | solution.py:121
  (138 shorter events, 60.8 us)
Async XLA Ops:
  10.2 10.9 %collective-permute-start.6 = (f32[256,256]{1,0:T(8,128)S(1)}, f32[256,256]{1,0:T(8,128)}, u32[]{:S(2)}, u32[]{:S(2)}) collective-permute-start(f32[256,256]{1,0:T(8,128)S(1)} %dynamic-slice_add_fusion.refs_4_), channel_id=1, source_target_pairs={{0,24},{8,16},{16,8},{24,0},{1,25},{9,17},{17,9},{25,1},{2,26},{10... | collective-permute-start | bytes 786440 | tf_op jit(solution)/shard_map/ppermute | solution.py:294
  16.2 19.8 %collective-permute-start.2 = (bf16[1280,256]{1,0:T(8,128)(2,1)}, bf16[1280,256]{1,0:T(8,128)(2,1)}, u32[]{:S(2)}, u32[]{:S(2)}) collective-permute-start(bf16[1280,256]{1,0:T(8,128)(2,1)} %bitcast.30), channel_id=1, source_target_pairs={{0,6},{1,7},{2,4},{3,5},{4,2},{5,3},{6,0},{7,1},{8,14},{9,15},{10,... | collective-permute-start | bytes 1966088 | tf_op jit(solution)/shard_map/ppermute | solution.py:294
  19.8 56.4 %collective-permute-start.1 = (bf16[1280,256]{1,0:T(8,128)(2,1)}, bf16[1280,256]{1,0:T(8,128)(2,1)}, u32[]{:S(2)}, u32[]{:S(2)}) collective-permute-start(bf16[1280,256]{1,0:T(8,128)(2,1)} %bitcast.31), channel_id=1, source_target_pairs={{0,4},{1,5},{2,6},{3,7},{4,0},{5,1},{6,2},{7,3},{8,12},{9,13},{10,... | collective-permute-start | bytes 1966088 | tf_op jit(solution)/shard_map/ppermute | solution.py:294
  19.8 56.4 %collective-permute-start = (bf16[1280,256]{1,0:T(8,128)(2,1)}, bf16[1280,256]{1,0:T(8,128)(2,1)}, u32[]{:S(2)}, u32[]{:S(2)}) collective-permute-start(bf16[1280,256]{1,0:T(8,128)(2,1)} %bitcast.32), channel_id=1, source_target_pairs={{0,2},{1,3},{2,0},{3,1},{4,6},{5,7},{6,4},{7,5},{8,10},{9,11},{10,... | collective-permute-start | bytes 1966088 | tf_op jit(solution)/shard_map/ppermute | solution.py:294
  20.6 13.6 %collective-permute-start.5 = (f32[256,256]{1,0:T(8,128)S(1)}, f32[256,256]{1,0:T(8,128)}, u32[]{:S(2)}, u32[]{:S(2)}) collective-permute-start(f32[256,256]{1,0:T(8,128)S(1)} %dynamic-slice_add_fusion.refs_4_), channel_id=1, source_target_pairs={{0,16},{8,24},{16,0},{24,8},{1,17},{9,25},{17,1},{25,9},{2,18},{10... | collective-permute-start | bytes 786440 | tf_op jit(solution)/shard_map/ppermute | solution.py:294
  21.1 13.1 %collective-permute-start.4 = (f32[256,256]{1,0:T(8,128)S(1)}, f32[256,256]{1,0:T(8,128)}, u32[]{:S(2)}, u32[]{:S(2)}) collective-permute-start(f32[256,256]{1,0:T(8,128)S(1)} %dynamic-slice_add_fusion.refs_4_), channel_id=1, source_target_pairs={{0,8},{8,0},{16,24},{24,16},{1,9},{9,1},{17,25},{25,17},{2,10},{10... | collective-permute-start | bytes 786440 | tf_op jit(solution)/shard_map/ppermute | solution.py:294
  84.7 11.1 %collective-permute-start.10 = (f32[160,256]{1,0:T(8,128)S(1)}, f32[160,256]{1,0:T(8,128)S(1)}, u32[]{:S(2)}, u32[]{:S(2)}) collective-permute-start(f32[160,256]{1,0:T(8,128)S(1)} %get-tuple-element.47), channel_id=1, source_target_pairs={{0,6},{1,7},{2,4},{3,5},{4,2},{5,3},{6,0},{7,1},{8,14},{9,15},{10,... | collective-permute-start | bytes 491528 | tf_op jit(solution)/shard_map/ppermute | solution.py:294
  87.3 15.4 %collective-permute-start.9 = (f32[160,256]{1,0:T(8,128)S(1)}, f32[160,256]{1,0:T(8,128)S(1)}, u32[]{:S(2)}, u32[]{:S(2)}) collective-permute-start(f32[160,256]{1,0:T(8,128)S(1)} %get-tuple-element.48), channel_id=1, source_target_pairs={{0,4},{1,5},{2,6},{3,7},{4,0},{5,1},{6,2},{7,3},{8,12},{9,13},{10,... | collective-permute-start | bytes 491528 | tf_op jit(solution)/shard_map/ppermute | solution.py:294
  105.6 12.5 %collective-permute-start.12 = (f32[160,256]{1,0:T(8,128)S(1)}, f32[160,256]{1,0:T(8,128)S(1)}, u32[]{:S(2)}, u32[]{:S(2)}) collective-permute-start(f32[160,256]{1,0:T(8,128)S(1)} %fusion.3.refs_0_), channel_id=1, source_target_pairs={{0,4},{1,5},{2,6},{3,7},{4,0},{5,1},{6,2},{7,3},{8,12},{9,13},{10,... | collective-permute-start | bytes 491528 | tf_op jit(solution)/shard_map/ppermute | solution.py:294
  105.6 12.5 %collective-permute-start.11 = (f32[160,256]{1,0:T(8,128)S(1)}, f32[160,256]{1,0:T(8,128)S(1)}, u32[]{:S(2)}, u32[]{:S(2)}) collective-permute-start(f32[160,256]{1,0:T(8,128)S(1)} %fusion.3.refs_0_), channel_id=1, source_target_pairs={{0,2},{1,3},{2,0},{3,1},{4,6},{5,7},{6,4},{7,5},{8,10},{9,11},{10,... | collective-permute-start | bytes 491528 | tf_op jit(solution)/shard_map/ppermute | solution.py:294
  128.9 13.5 %collective-permute-start.19 = (f32[256,256]{1,0:T(8,128)S(1)}, f32[256,256]{1,0:T(8,128)S(1)}, u32[]{:S(2)}, u32[]{:S(2)}) collective-permute-start(f32[256,256]{1,0:T(8,128)S(1)} %get-tuple-element.44), channel_id=1, source_target_pairs={{0,24},{8,16},{16,8},{24,0},{1,25},{9,17},{17,9},{25,1},{2,26},{10... | collective-permute-start | bytes 786440 | tf_op jit(solution)/shard_map/ppermute | solution.py:294
  130.3 13.4 %collective-permute-start.18 = (f32[256,256]{1,0:T(8,128)S(1)}, f32[256,256]{1,0:T(8,128)S(1)}, u32[]{:S(2)}, u32[]{:S(2)}) collective-permute-start(f32[256,256]{1,0:T(8,128)S(1)} %get-tuple-element.45), channel_id=1, source_target_pairs={{0,16},{8,24},{16,0},{24,8},{1,17},{9,25},{17,1},{25,9},{2,18},{10... | collective-permute-start | bytes 786440 | tf_op jit(solution)/shard_map/ppermute | solution.py:294
  144.8 12.7 %collective-permute-start.20 = (f32[256,256]{1,0:T(8,128)S(1)}, f32[256,256]{1,0:T(8,128)S(1)}, u32[]{:S(2)}, u32[]{:S(2)}) collective-permute-start(f32[256,256]{1,0:T(8,128)S(1)} %fusion.1.own), channel_id=1, source_target_pairs={{0,1},{1,0},{2,3},{3,2},{4,5},{5,4},{6,7},{7,6},{8,9},{9,8},{10,11... | collective-permute-start | bytes 786440 | tf_op jit(solution)/shard_map/ppermute | solution.py:294
  166.1 21.4 %collective-permute-start.21 = (f32[64,3200]{1,0:T(8,128)}, f32[64,3200]{1,0:T(8,128)S(1)}, u32[]{:S(2)}, u32[]{:S(2)}) collective-permute-start(f32[64,3200]{1,0:T(8,128)} %get-tuple-element.35), channel_id=1, source_target_pairs={{0,8},{8,0},{16,24},{24,16},{1,9},{9,1},{17,25},{25,17},{2,10},{10... | collective-permute-start | bytes 2457608 | tf_op jit(solution)/shard_map/ppermute | solution.py:294
  166.7 105.9 %collective-permute-start.25 = (f32[64,3200]{1,0:T(8,128)}, f32[64,3200]{1,0:T(8,128)S(1)}, u32[]{:S(2)}, u32[]{:S(2)}) collective-permute-start(f32[64,3200]{1,0:T(8,128)} %get-tuple-element.37), channel_id=1, source_target_pairs={{0,16},{8,24},{16,0},{24,8},{1,17},{9,25},{17,1},{25,9},{2,18},{10... | collective-permute-start | bytes 2457608 | tf_op jit(solution)/shard_map/ppermute | solution.py:294
  168.2 24.9 %collective-permute-start.15 = (f32[256,256]{1,0:T(8,128)S(1)}, f32[256,256]{1,0:T(8,128)S(1)}, u32[]{:S(2)}, u32[]{:S(2)}) collective-permute-start(f32[256,256]{1,0:T(8,128)S(1)} %copy-done.20), channel_id=1, source_target_pairs={{0,8},{8,0},{16,24},{24,16},{1,9},{9,1},{17,25},{25,17},{2,10},{10... | collective-permute-start | bytes 786440 | tf_op jit(solution)/shard_map/ppermute | solution.py:294
  169.7 136.7 %collective-permute-start.36 = (bf16[512,3200]{1,0:T(8,128)(2,1)S(1)}, bf16[512,3200]{1,0:T(8,128)(2,1)S(1)}, u32[]{:S(2)}, u32[]{:S(2)}) collective-permute-start(bf16[512,3200]{1,0:T(8,128)(2,1)S(1)} %copy-done.2), channel_id=1, source_target_pairs={{0,8},{8,0},{16,24},{24,16},{1,9},{9,1},{17,25},{25,17},{2,10},{10... | collective-permute-start | bytes 9830408 | tf_op jit(solution)/shard_map/ppermute | solution.py:294
  170.3 137.6 %collective-permute-start.38 = (bf16[512,3200]{1,0:T(8,128)(2,1)S(1)}, bf16[512,3200]{1,0:T(8,128)(2,1)S(1)}, u32[]{:S(2)}, u32[]{:S(2)}) collective-permute-start(bf16[512,3200]{1,0:T(8,128)(2,1)S(1)} %copy-done.2), channel_id=1, source_target_pairs={{0,16},{8,24},{16,0},{24,8},{1,17},{9,25},{17,1},{25,9},{2,18},{10... | collective-permute-start | bytes 9830408 | tf_op jit(solution)/shard_map/ppermute | solution.py:294
  188.8 84.5 %collective-permute-start.22 = (f32[32,3200]{1,0:T(8,128)S(1)}, f32[32,3200]{1,0:T(8,128)S(1)}, u32[]{:S(2)}, u32[]{:S(2)}) collective-permute-start(f32[32,3200]{1,0:T(8,128)S(1)} %slice.61), channel_id=1, source_target_pairs={{0,16},{8,24},{16,0},{24,8},{1,17},{9,25},{17,1},{25,9},{2,18},{10... | collective-permute-start | bytes 1228808 | tf_op jit(solution)/shard_map/ppermute | solution.py:294
  193.2 78.8 %collective-permute-start.16 = (f32[256,256]{1,0:T(8,128)S(1)}, f32[256,256]{1,0:T(8,128)S(1)}, u32[]{:S(2)}, u32[]{:S(2)}) collective-permute-start(f32[256,256]{1,0:T(8,128)S(1)} %add.70), channel_id=1, source_target_pairs={{0,16},{8,24},{16,0},{24,8},{1,17},{9,25},{17,1},{25,9},{2,18},{10... | collective-permute-start | bytes 786440 | tf_op jit(solution)/shard_map/ppermute | solution.py:294
  271.9 34.1 %collective-permute-start.32 = (bf16[1280,256]{1,0:T(8,128)(2,1)S(1)}, bf16[1280,256]{1,0:T(8,128)(2,1)S(1)}, u32[]{:S(2)}, u32[]{:S(2)}) collective-permute-start(bf16[1280,256]{1,0:T(8,128)(2,1)S(1)} %bitcast.36), channel_id=1, source_target_pairs={{0,1},{1,0},{2,3},{3,2},{4,5},{5,4},{6,7},{7,6},{8,9},{9,8},{10,11... | collective-permute-start | bytes 1966088 | tf_op jit(solution)/shard_map/ppermute | solution.py:294
  272.7 67.7 %collective-permute-start.35 = (bf16[1280,256]{1,0:T(8,128)(2,1)}, bf16[1280,256]{1,0:T(8,128)(2,1)}, u32[]{:S(2)}, u32[]{:S(2)}) collective-permute-start(bf16[1280,256]{1,0:T(8,128)(2,1)} %collective-permute-done.2.refs_3_.refs_8_), channel_id=1, source_target_pairs={{0,1},{1,0},{2,3},{3,2},{4,5},{5,4},{6,7},{7,6},{8,9},{9,8},{10,11... | collective-permute-start | bytes 1966088 | tf_op jit(solution)/shard_map/ppermute | solution.py:294
  273.3 11.4 %collective-permute-start.26 = (f32[32,3200]{1,0:T(8,128)S(1)}, f32[32,3200]{1,0:T(8,128)S(1)}, u32[]{:S(2)}, u32[]{:S(2)}) collective-permute-start(f32[32,3200]{1,0:T(8,128)S(1)} %slice.63), channel_id=1, source_target_pairs={{0,8},{8,0},{16,24},{24,16},{1,9},{9,1},{17,25},{25,17},{2,10},{10... | collective-permute-start | bytes 1228808 | tf_op jit(solution)/shard_map/ppermute | solution.py:294
  284.8 10.5 %collective-permute-start.23 = (f32[32,3200]{1,0:T(8,128)S(1)}, f32[32,3200]{1,0:T(8,128)S(1)}, u32[]{:S(2)}, u32[]{:S(2)}) collective-permute-start(f32[32,3200]{1,0:T(8,128)S(1)} %slice_add_fusion.1.refs_0_), channel_id=1, source_target_pairs={{0,16},{8,24},{16,0},{24,8},{1,17},{9,25},{17,1},{25,9},{2,18},{10... | collective-permute-start | bytes 1228808 | tf_op jit(solution)/shard_map/ppermute | solution.py:294
  305.0 35.5 %collective-permute-start.34 = (bf16[1280,256]{1,0:T(8,128)(2,1)}, bf16[1280,256]{1,0:T(8,128)(2,1)}, u32[]{:S(2)}, u32[]{:S(2)}) collective-permute-start(bf16[1280,256]{1,0:T(8,128)(2,1)} %collective-permute-done.1.refs_2_.refs_7_), channel_id=1, source_target_pairs={{0,1},{1,0},{2,3},{3,2},{4,5},{5,4},{6,7},{7,6},{8,9},{9,8},{10,11... | collective-permute-start | bytes 1966088 | tf_op jit(solution)/shard_map/ppermute | solution.py:294
  306.0 34.5 %collective-permute-start.33 = (bf16[1280,256]{1,0:T(8,128)(2,1)}, bf16[1280,256]{1,0:T(8,128)(2,1)}, u32[]{:S(2)}, u32[]{:S(2)}) collective-permute-start(bf16[1280,256]{1,0:T(8,128)(2,1)} %collective-permute-done.refs_1_.refs_6_), channel_id=1, source_target_pairs={{0,1},{1,0},{2,3},{3,2},{4,5},{5,4},{6,7},{7,6},{8,9},{9,8},{10,11... | collective-permute-start | bytes 1966088 | tf_op jit(solution)/shard_map/ppermute | solution.py:294
  306.4 21.3 %collective-permute-start.24 = (f32[64,3200]{1,0:T(8,128)}, f32[64,3200]{1,0:T(8,128)}, u32[]{:S(2)}, u32[]{:S(2)}) collective-permute-start(f32[64,3200]{1,0:T(8,128)} %pad_maximum_fusion.2), channel_id=1, source_target_pairs={{0,8},{8,0},{16,24},{24,16},{1,9},{9,1},{17,25},{25,17},{2,10},{10... | collective-permute-start | bytes 2457608 | tf_op jit(solution)/shard_map/ppermute | solution.py:294
  309.8 20.7 %collective-permute-start.28 = (f32[64,3200]{1,0:T(8,128)}, f32[64,3200]{1,0:T(8,128)}, u32[]{:S(2)}, u32[]{:S(2)}) collective-permute-start(f32[64,3200]{1,0:T(8,128)} %pad_maximum_fusion.3), channel_id=1, source_target_pairs={{0,16},{8,24},{16,0},{24,8},{1,17},{9,25},{17,1},{25,9},{2,18},{10... | collective-permute-start | bytes 2457608 | tf_op jit(solution)/shard_map/ppermute | solution.py:294
  327.7 41.8 %collective-permute-start.37 = (bf16[256,3200]{1,0:T(8,128)(2,1)}, bf16[256,3200]{1,0:T(8,128)(2,1)S(1)}, u32[]{:S(2)}, u32[]{:S(2)}) collective-permute-start(bf16[256,3200]{1,0:T(8,128)(2,1)} %slice.64), channel_id=1, source_target_pairs={{0,16},{8,24},{16,0},{24,8},{1,17},{9,25},{17,1},{25,9},{2,18},{10... | collective-permute-start | bytes 4915208 | tf_op jit(solution)/shard_map/ppermute | solution.py:294
  330.5 39.0 %collective-permute-start.39 = (bf16[256,3200]{1,0:T(8,128)(2,1)S(1)}, bf16[256,3200]{1,0:T(8,128)(2,1)}, u32[]{:S(2)}, u32[]{:S(2)}) collective-permute-start(bf16[256,3200]{1,0:T(8,128)(2,1)S(1)} %slice.65), channel_id=1, source_target_pairs={{0,8},{8,0},{16,24},{24,16},{1,9},{9,1},{17,25},{25,17},{2,10},{10... | collective-permute-start | bytes 4915208 | tf_op jit(solution)/shard_map/ppermute | solution.py:294
  344.0 23.8 %collective-permute-start.30 = (f32[8,256]{1,0:T(8,128)S(1)}, f32[8,256]{1,0:T(8,128)S(1)}, u32[]{:S(2)}, u32[]{:S(2)}) collective-permute-start(f32[8,256]{1,0:T(8,128)S(1)} %add.79), channel_id=1, source_target_pairs={{0,2},{1,3},{2,0},{3,1},{4,6},{5,7},{6,4},{7,5},{8,10},{9,11},{10,... | collective-permute-start | bytes 24584 | tf_op jit(solution)/shard_map/ppermute | solution.py:294
  367.8 23.3 %collective-permute-start.31 = (f32[8,256]{1,0:T(8,128)S(1)}, f32[8,256]{1,0:T(8,128)S(1)}, u32[]{:S(2)}, u32[]{:S(2)}) collective-permute-start(f32[8,256]{1,0:T(8,128)S(1)} %add.80), channel_id=1, source_target_pairs={{0,4},{1,5},{2,6},{3,7},{4,0},{5,1},{6,2},{7,3},{8,12},{9,13},{10,... | collective-permute-start | bytes 24584 | tf_op jit(solution)/shard_map/ppermute | solution.py:294
  (34 other events, 356.6 us)

commit v2 on v1

--- a/solution.py
+++ b/solution.py
@@ -98,7 +98,6 @@
         in_specs=[pl.BlockSpec(memory_space=pltpu.VMEM)],
         out_specs=pl.BlockSpec(memory_space=pltpu.VMEM),
         scratch_shapes=[pltpu.VMEM(gram.shape, f32)],
-        name="inverse_factor",
         cost_estimate=pl.CostEstimate(flops=20_000_000_000, bytes_accessed=10_000_000, transcendentals=0),
     )(gram)
 
@@ -114,19 +113,17 @@
 
 
 def tile_of(n):
-    return 640 if n % 640 == 0 else n
-
-
-def call(kernel, outs, ins, specs, out_specs, grid=(), scratch=(), flops=0, moved=0, aliases={}):
+    return min(n, 512)
+
+
+def call(kernel, outs, ins, specs, out_specs, grid=(), scratch=(), flops=0, moved=0, aliases={}, prefetch=0):
     return pl.pallas_call(
         kernel,
         out_shape=outs,
-        grid=grid,
-        in_specs=specs,
-        out_specs=out_specs,
-        scratch_shapes=list(scratch),
+        grid_spec=pltpu.PrefetchScalarGridSpec(
+            num_scalar_prefetch=prefetch, grid=grid, in_specs=specs, out_specs=out_specs, scratch_shapes=list(scratch)
+        ),
         input_output_aliases=aliases,
-        compiler_params=pltpu.CompilerParams(dimension_semantics=("arbitrary",) * len(grid)),
         cost_estimate=pl.CostEstimate(flops=flops, bytes_accessed=moved, transcendentals=0),
     )(*ins)
 
@@ -195,7 +192,7 @@
 
 
 def token_kernel(ids, own, other, inputs, *refs):
-    before, after_refs, flip, tok = refs[:4], refs[4:8], refs[8], refs[9]
+    before, after_refs, flip, tok = refs[:4], refs[4:10], refs[10], refs[11]
     row, core = ids[0], ids[2]
     half = own.shape[0]
     size = flip.shape[0] // 8
@@ -215,25 +212,41 @@
         x = inputs[h * half : (h + 1) * half, :]
         total += mm(tok[h, 0], x, ((1,), (0,)))
         total += mm(tok[h, 1], x, ((1,), (0,)))
-    n = after_refs[0].shape[0]
-    for i in range(4):
-        after_refs[i][...] = before[i][...] + total[i * n : (i + 1) * n, :]
-
-
-def gradient_kernel(count, ids, *refs):
-    own, other, blocks, base, out = refs[:count], refs[count : 2 * count], refs[2 * count : 3 * count], refs[3 * count], refs[3 * count + 1]
+    for p in range(2):
+        keep, send = before[2 * p], before[2 * p + 1]
+        first, second, out = after_refs[3 * p : 3 * p + 3]
+        at = 4 * p * size
+        first[...] = keep[:size, :] + total[at : at + size, :]
+        second[...] = keep[size:, :] + total[at + size : at + 2 * size, :]
+        out[...] = send[...] + total[at + 2 * size : at + 4 * size, :]
+
+
+def gradient_kernel(count, crossing, ids, *refs):
+    own, other = refs[:count], refs[count : 2 * count]
+    blocks, base, out = refs[2 * count : -2], refs[-2], refs[-1]
     core = ids[2]
-    half = blocks[0].shape[0] // 2
     total = base[...]
-    for mine, its, x in zip(own, other, blocks):
+    for at_block in range(count - crossing):
+        x = blocks[at_block]
+        half = x.shape[0] // 2
         at = pl.multiple_of(core * half, half)
-        total += mm(mine[0], x[pl.ds(at, half), :], ((1,), (0,)))
+        total += mm(own[at_block][0], x[pl.ds(at, half), :], ((1,), (0,)))
         at = pl.multiple_of((1 - core) * half, half)
-        total += mm(its[0], x[pl.ds(at, half), :], ((1,), (0,)))
+        total += mm(other[at_block][0], x[pl.ds(at, half), :], ((1,), (0,)))
+    if crossing:
+        total += crossed(core, own[-1], other[-1], blocks[-2], blocks[-1], 0)
     out[...] = total
 
 
-def right_kernel(ids, inverse, sketch, *refs):
+def crossed(core, own, other, first, second, part):
+    size = first.shape[0]
+    cut = slice(part * size, (part + 1) * size)
+    mine = jnp.where(core == 0, first[...], second[...])
+    its = jnp.where(core == 0, second[...], first[...])
+    return mm(own[0][:, cut], mine, ((1,), (0,))) + mm(other[0][:, cut], its, ((1,), (0,)))
+
+
+def right_kernel(n, ids, inverse, sketch, *refs):
     pieces, right, squares, basis, work = refs[:6], refs[6], refs[7], refs[8], refs[9]
     row = ids[0]
     size = work.shape[0] // 8
@@ -255,7 +268,8 @@
     tb, tl = split(work[...])
     total = mm(ib, tb, ((1,), (0,))) + mm(ib, tl, ((1,), (0,))) + mm(il, tb, ((1,), (0,)))
     right[...] = total
-    sb, sl = split(total * total)
+    at = pl.program_id(0) * total.shape[1] + lax.broadcasted_iota(jnp.int32, total.shape, 1)
+    sb, sl = split(jnp.where(at < n, total * total, 0.0))
     ones = jnp.ones((8, total.shape[1]), bf16)
     squares[...] += mm(ones, sb, ((1,), (1,))) + mm(ones, sl, ((1,), (1,)))
 
@@ -273,20 +287,13 @@
     factor_out[...] = right[...].T * scale
 
 
-def momentum_kernel(ids, own, other, first, second, basis, right, base, out, table, small):
-    core = ids[2]
-
+def momentum_kernel(ids, own, other, first, second, basis, right, base, out, small):
     @pl.when(pl.program_id(0) == 0)
     def _():
-        table[core] = own[0]
-        table[1 - core] = other[0]
         small[...] = (basis[...] * -(1.0 - mix_rate)).astype(bf16)
 
-    total = base[...]
-    total += mm(table[0], first[...], ((1,), (0,)))
-    total += mm(table[1], second[...], ((1,), (0,)))
-    total += mm(small[...], right[...].astype(bf16), ((1,), (0,)))
-    out[...] = total
+    total = base[...] + crossed(ids[2], own, other, first, second, 1)
+    out[...] = total + mm(small[...], right[...].astype(bf16), ((1,), (0,)))
 
 
 def swap(x, axis, bit):
@@ -296,6 +303,10 @@
 
 def plane(n_total, m_total, inputs, out_grads, weights, momentum, right_factor):
     return plane_body(n_total, m_total, inputs, out_grads, weights, momentum, right_factor)
+
+
+def swaps(x, axis, unit):
+    return [swap(x, axis, unit * k) for k in (1, 2, 3)]
 
 
 def plane_body(n_total, m_total, inputs, out_grads, weights, momentum, right_factor):
@@ -308,24 +319,30 @@
     m = momentum.shape[0]
     block = out_grads.shape[0]
     tn = tile_of(n)
-    quarter = [1, 2, 3]
-    tiles = (n // tn,)
+    tiles = (pl.cdiv(n, tn),)
 
     def columns(rows):
-        return pl.BlockSpec((rows, tn), lambda i: (0, i))
+        return pl.BlockSpec((rows, tn), lambda i, *_: (0, i))
+
+    def fixed(*shape):
+        return pl.BlockSpec(shape, lambda i, *_: (0,) * len(shape))
+
+    def pick(j):
+        return pl.BlockSpec((1, m, block), lambda i, ids: (ids[3] ^ j, 0, 0))
 
     grads = out_grads.T
-    own = [grads] + [swap(grads, "col", 2 * k) for k in quarter]
+    own = [grads] + swaps(grads, "col", 2)
 
     in_right = mm(inputs.astype(f32), right_factor, ((1,), (0,)), high)
-    flipped = jnp.where(core == 0, 0, 1)
-    keep = lax.dynamic_slice_in_dim(in_right, flipped * block, block, 0)
-    send = lax.dynamic_slice_in_dim(in_right, (1 - flipped) * block, block, 0)
+    keep = lax.dynamic_slice_in_dim(in_right, core * block, block, 0)
+    send = lax.dynamic_slice_in_dim(in_right, (1 - core) * block, block, 0)
     in_right = keep + swap(send, "col", 1)
-    rights = [in_right] + [swap(in_right, "row", k) for k in quarter]
+    rights = [in_right] + swaps(in_right, "row", 1)
     x_all = swap(inputs, "row", 1)
     y_all = swap(inputs, "row", 2)
     other = [swap(g, "col", 1) for g in own]
+    own_all = jnp.stack(own)
+    other_all = jnp.stack(other)
 
     part = mm(momentum, right_factor, ((1,), (0,)), high)
     keep, send = call(
@@ -335,10 +352,16 @@
     mine = keep + swap(send, "col", 1)
     size = m // 8
     total = mine[:size]
-    for k in quarter:
+    for k in (1, 2, 3):
         total = total + swap(mine[k * size : (k + 1) * size], "col", 2 * k)
-    parts = [total] + [swap(total, "col", 2 * k) for k in quarter]
+    parts = [total] + swaps(total, "col", 2)
     rest = swap(jnp.concatenate(parts, axis=0), "col", 1)
+
+    quarter = tokens // 4
+    x_first, x_second = x_all[:quarter], x_all[quarter : 2 * quarter]
+    y_first, y_second = y_all[2 * quarter : 3 * quarter], y_all[3 * quarter :]
+    first_by_y, first_by_x = swap(x_first, "row", 2), swap(y_first, "row", 1)
+    second_by_y, second_by_x = swap(x_second, "row", 2), swap(y_second, "row", 1)
 
     sketch, gram, toks, big_t, low_t = call(
         gram_kernel,
@@ -346,80 +369,65 @@
         (ids, *parts, rest, *own), [whole_smem] + [whole_vmem] * 9, (whole_vmem,) * 5,
         scratch=[pltpu.VMEM((rank, m), f32)], flops=20 * m * rank * rank, moved=8_000_000)
     token = toks[0]
-    for k in quarter:
+    for k in (1, 2, 3):
         token = token + swap(toks[k], "row", k)
     token_other = swap(token, "col", 1)
     gram = gram + swap(gram, "row", 1)
     gram = gram + swap(gram, "row", 2)
 
+    n8 = rank // 8
     sides = call(
         side_kernel, (shaped((rank // 4, n)),) * 4, (big_t, low_t, momentum),
         [whole_vmem] * 2 + [columns(m)], (columns(rank // 4),) * 4, tiles,
         flops=6 * m * n * rank, moved=5 * m * n)
-    top, top_send, low, low_send = call(
-        token_kernel, (shaped((rank // 4, n)),) * 4,
+    top0, top1, top_send, low0, low1, low_send = call(
+        token_kernel, (shaped((n8, n)), shaped((n8, n)), shaped((2 * n8, n))) * 2,
         (ids, token, token_other, inputs, *sides),
-        [whole_smem] + [whole_vmem] * 2 + [columns(tokens)] + [columns(rank // 4)] * 4, (columns(rank // 4),) * 4, tiles,
+        [whole_smem] + [whole_vmem] * 2 + [columns(tokens)] + [columns(2 * n8)] * 4,
+        (columns(n8), columns(n8), columns(2 * n8)) * 2, tiles,
         scratch=[pltpu.VMEM((rank, block), f32), pltpu.VMEM((2, 2, rank, block), bf16)],
-        flops=4 * tokens * n * rank, moved=10 * rank * n, aliases={4: 0, 5: 1, 6: 2, 7: 3})
-    n8 = rank // 8
-    top = top + swap(top_send, "row", 1)
-    low = low + swap(low_send, "row", 2)
-    top0 = top[:n8] + swap(top[n8:], "row", 2)
-    low0 = low[:n8] + swap(low[n8:], "row", 1)
-    top1 = swap(top0, "row", 2)
-    low1 = swap(low0, "row", 1)
+        flops=4 * tokens * n * rank, moved=10 * rank * n)
+    top_in, low_in = swap(top_send, "row", 1), swap(low_send, "row", 2)
+    top1, low1 = top1 + top_in[n8:], low1 + low_in[n8:]
+    top0 = top0 + top_in[:n8] + swap(top1, "row", 2)
+    low0 = low0 + low_in[:n8] + swap(low1, "row", 1)
+    top1, low1 = swap(top0, "row", 2), swap(low0, "row", 1)
     top2 = swap(jnp.concatenate([top0, top1], axis=0), "row", 1)
     low2 = swap(jnp.concatenate([low0, low1], axis=0), "row", 2)
 
     inverse = inverse_factor(gram)
-    half = tokens // 2
-    d_first = swap(x_all[:half], "row", 2)
-    d_second = swap(y_all[half:], "row", 1)
-
-    own_all = jnp.stack(own)
-    other_all = jnp.stack(other)
-
-    def pick(j):
-        return pl.BlockSpec((1, m, block), lambda i, ids: (ids[3] ^ j, 0, 0))
-
-    def cols(rows):
-        return pl.BlockSpec((rows, tn), lambda i, ids: (0, i))
-
-    moment = pl.pallas_call(
-        functools.partial(gradient_kernel, 3),
-        grid_spec=pltpu.PrefetchScalarGridSpec(
-            num_scalar_prefetch=1, grid=tiles,
-            in_specs=[pick(0), pick(1), pick(2)] * 2 + [cols(tokens)] * 3 + [cols(m)],
-            out_specs=cols(m)),
-        out_shape=shaped((m, n)), name="gradient",
-        cost_estimate=pl.CostEstimate(flops=6 * m * n * tokens, bytes_accessed=8 * m * n, transcendentals=0),
-    )(ids, *([own_all] * 3), *([other_all] * 3), inputs, x_all, y_all, momentum)
+
+    def gradient(picks, crossing, blocks, base):
+        count = len(picks)
+        return call(
+            functools.partial(gradient_kernel, count, crossing), shaped((m, n)),
+            (ids, *([own_all] * count), *([other_all] * count), *blocks, base),
+            [pick(j) for j in picks] * 2 + [columns(x.shape[0]) for x in blocks] + [columns(m)], columns(m), tiles,
+            flops=2 * m * n * sum(x.shape[0] for x in blocks), moved=8 * m * n, prefetch=1)
+
+    moment = gradient((0, 1), 0, (inputs, x_all), momentum)
+    moment = gradient((2, 3), 1, (y_all, first_by_y, first_by_x), moment)
 
     right, squares, basis = call(
-        right_kernel, (shaped((rank, n)), shaped((8, rank)), shaped((m, rank))),
+        functools.partial(right_kernel, n), (shaped((rank, n)), shaped((8, rank)), shaped((m, rank))),
         (ids, inverse, sketch, top0, top1, top2, low0, low1, low2),
         [whole_smem] + [whole_vmem] * 2 + [columns(n8), columns(n8), columns(2 * n8)] * 2,
-        (columns(rank), pl.BlockSpec((8, rank), lambda i: (0, 0)), pl.BlockSpec((m, rank), lambda i: (0, 0))), tiles,
+        (columns(rank), fixed(8, rank), fixed(m, rank)), tiles,
         scratch=[pltpu.VMEM((rank, tn), f32)], flops=6 * n * rank * rank, moved=12 * n * rank)
-    for bit in (1, 2, 4):
-        squares = squares + swap(squares, "col", bit)
+    squares = squares + swap(squares, "col", 1)
+    w1, w2, w3 = swaps(squares, "col", 2)
+    squares = (squares + w1) + (w2 + w3)
     weights_new, factor_new = call(
         functools.partial(weights_kernel, n_total, step_rate * math.sqrt(m_total / rank)),
         (shaped((m, n)), shaped((n, rank))), (squares, basis, right, weights),
         [whole_vmem] * 2 + [columns(rank), columns(m)],
-        (columns(m), pl.BlockSpec((tn, rank), lambda i: (i, 0))), tiles,
+        (columns(m), pl.BlockSpec((tn, rank), lambda i, *_: (i, 0))), tiles,
         scratch=[pltpu.VMEM((m, rank), bf16)] * 2, flops=6 * m * n * rank, moved=6 * m * n)
-    momentum_new = pl.pallas_call(
-        momentum_kernel,
-        grid_spec=pltpu.PrefetchScalarGridSpec(
-            num_scalar_prefetch=1, grid=tiles,
-            in_specs=[pick(3), pick(3), cols(half), cols(half), pl.BlockSpec((m, rank), lambda i, ids: (0, 0)), cols(rank), cols(m)],
-            out_specs=cols(m),
-            scratch_shapes=[pltpu.VMEM((2, m, block), bf16), pltpu.VMEM((m, rank), bf16)]),
-        out_shape=shaped((m, n)), name="momentum", input_output_aliases={7: 0},
-        cost_estimate=pl.CostEstimate(flops=2 * m * n * (tokens + rank), bytes_accessed=8 * m * n, transcendentals=0),
-    )(ids, own_all, other_all, d_first, d_second, basis, right, moment)
+    momentum_new = call(
+        momentum_kernel, shaped((m, n)), (ids, own_all, other_all, second_by_y, second_by_x, basis, right, moment),
+        [pick(3), pick(3), columns(quarter), columns(quarter), fixed(m, rank), columns(rank), columns(m)],
+        columns(m), tiles, scratch=[pltpu.VMEM((m, rank), bf16)],
+        flops=2 * m * n * (tokens // 2 + rank), moved=8 * m * n, prefetch=1, aliases={7: 0})
     return (weights_new, momentum_new, factor_new)
 
 

time: 409 us -> 454 us (1.11)
  Pallas kernels: 114 us -> 131 us
  waiting for transfers between devices: 206 us -> 218 us
  starting transfers between devices: 42.8 us -> 54.6 us
    pallas_call x8 -> x9, Pallas kernels: 100 us -> 117 us  [call(): pl.pallas_call(kernel, out_shape=outs, grid_spec=pltpu.PrefetchScalarGrid...]
    ppermute x40 -> x43, waiting for transfers between devices: 206 us -> 218 us  [swap(): return lax.ppermute(x, axis, [(i, i ^ bit) for i in range(size)])]
    ppermute x40 -> x43, starting transfers between devices: 42.8 us -> 54.6 us  [swap(): return lax.ppermute(x, axis, [(i, i ^ bit) for i in range(size)])]
    unnamed x53 -> x47, local copies, waits for them, and re-layouts: 10.8 us -> 7.67 us
  transfers between devices with their start and end apart: 40 -> 43, of which waited for: 20 -> 16; matrix products, arithmetic and copies ran while one was open for 6% -> 8% of each run, Pallas kernels for 19% -> 24%
where the time goes in v2:
time: 454 us; the launch traced here: 452 us
  waiting for transfers between devices  218 us (48%)
  Pallas kernels  131 us (29%)
  starting transfers between devices  54.6 us (12%)
  other arithmetic  19.4 us (4%)
  matrix products  15 us (3%)
  local copies, waits for them, and re-layouts  13.2 us (3%)
    ppermute x43, waiting for transfers between devices, swap(): return lax.ppermute(x, axis, [(i, i ^ bit) for i in range(size)])  218 us
    pallas_call x9, Pallas kernels, call(): pl.pallas_call(kernel, out_shape=outs, grid_spec=pltpu.PrefetchScalarGrid...  117 us
    ppermute x43, starting transfers between devices, swap(): return lax.ppermute(x, axis, [(i, i ^ bit) for i in range(size)])  54.6 us
    dot_general x2, matrix products, mm(): lax.dot_general(a, b, (dims, ((), ())), precision=precision, preferred_el...  15 us
    pallas_call x1, Pallas kernels, inverse_factor(): pl.pallas_call(inverse_kernel, out_shape=jax.ShapeDtypeStruct(gram.shape,...  13.6 us
  transfers between devices with their start and end apart: 43, of which 16 were waited for; matrix products, arithmetic and copies ran while one was open for 8% of the time, Pallas kernels for 24%

profile of v2, /device:TPU:0, one launch (start us, length us, event | category | flops | bytes accessed | tf_op | source)
XLA Modules:
  0.0 452.2 jit_solution(8894127030723251868)
XLA Ops:
  2.6 3.9 fusion.10
  10.2 2.9 collective-permute-start.4
  22.5 11.2 %fusion.9.part = f32[1280,256]{1,0:T(8,128)} fusion(f32[1280,3200]{1,0:T(8,128)} %refs_6_.1, f32[3200,256]{1,0:T(8,128)S(1)} %copy-done), kind=kOutput, calls=%fused_computation.27 | convolution fusion | flops 6291456000 | bytes 20971520 | tf_op jit(solution)/shard_map/dot_general | solution.py:22
  34.2 11.2 %collective-permute-done.refs_1_.refs_6_ = bf16[1280,256]{1,0:T(8,128)(2,1)} collective-permute-done((bf16[1280,256]{1,0:T(8,128)(2,1)}, bf16[1280,256]{1,0:T(8,128)(2,1)}, u32[]{:S(2)}, u32[]{:S(2)}) %collective-permute-start) | collective-permute-done | bytes 655392 | tf_op jit(solution)/shard_map/ppermute | solution.py:301
  45.4 18.4 %collective-permute-done.1.refs_2_.refs_7_ = bf16[1280,256]{1,0:T(8,128)(2,1)} collective-permute-done((bf16[1280,256]{1,0:T(8,128)(2,1)}, bf16[1280,256]{1,0:T(8,128)(2,1)}, u32[]{:S(2)}, u32[]{:S(2)}) %collective-permute-start.1) | collective-permute-done | bytes 655392 | tf_op jit(solution)/shard_map/ppermute | solution.py:301
  63.7 4.9 %shard_map.76 = (f32[640,256]{1,0:T(8,128)}, f32[640,256]{1,0:T(8,128)}) custom-call(s32[4]{0:T(128)} %pad_add_fusion.ids, f32[1280,256]{1,0:T(8,128)} %fusion.9.part, bf16[1280,256]{1,0:T(8,128)(2,1)} %bitcast.4.refs_0_.refs_5_, bf16[1280,256]{1,0:T(8,128)(2,1)} %collective-permute-done.refs_1_.refs_6_, ...), custom_call_target="tpu_custom_call" | custom-call | flops 1342177280 | bytes 8000000 | tf_op jit(solution)/shard_map/pallas_call | solution.py:120
  74.7 12.4 %collective-permute-start.8 = (f32[160,256]{1,0:T(8,128)S(1)}, f32[160,256]{1,0:T(8,128)S(1)}, u32[]{:S(2)}, u32[]{:S(2)}) collective-permute-start(f32[160,256]{1,0:T(8,128)S(1)} %get-tuple-element.54), channel_id=1, source_target_pairs={{0,2},{1,3},{2,0},{3,1},{4,6},{5,7},{6,4},{7,5},{8,10},{9,11},{10,... | collective-permute-start | bytes 491528 | tf_op jit(solution)/shard_map/ppermute | solution.py:301
  87.1 4.8 %collective-permute-done.8 = f32[160,256]{1,0:T(8,128)S(1)} collective-permute-done((f32[160,256]{1,0:T(8,128)S(1)}, f32[160,256]{1,0:T(8,128)S(1)}, u32[]{:S(2)}, u32[]{:S(2)}) %collective-permute-start.8) | collective-permute-done | bytes 163872 | tf_op jit(solution)/shard_map/ppermute | solution.py:301
  91.9 6.3 %collective-permute-done.9 = f32[160,256]{1,0:T(8,128)S(1)} collective-permute-done((f32[160,256]{1,0:T(8,128)S(1)}, f32[160,256]{1,0:T(8,128)S(1)}, u32[]{:S(2)}, u32[]{:S(2)}) %collective-permute-start.9) | collective-permute-done | bytes 163872 | tf_op jit(solution)/shard_map/ppermute | solution.py:301
  98.4 3.0 collective-permute-start.12
  102.8 3.6 collective-permute-done.11.refs_1_
  106.3 7.1 %collective-permute-done.12.refs_2_ = f32[160,256]{1,0:T(8,128)S(1)} collective-permute-done((f32[160,256]{1,0:T(8,128)S(1)}, f32[160,256]{1,0:T(8,128)S(1)}, u32[]{:S(2)}, u32[]{:S(2)}) %collective-permute-start.12) | collective-permute-done | bytes 163872 | tf_op jit(solution)/shard_map/ppermute | solution.py:301
  114.8 3.5 pad_maximum_fusion.refs_0_.refs_1_.own
  119.7 6.0 %shard_map.77 = (f32[1280,256]{1,0:T(8,128)}, f32[256,256]{1,0:T(8,128)}, f32[4,256,256]{2,1,0:T(8,128)}, bf16[256,1280]{1,0:T(8,128)(2,1)}, bf16[256,1280]{1,0:T(8,128)(2,1)}) custom-call(s32[4]{0:T(128)} %pad_add_fusion.ids, f32[160,256]{1,0:T(8,128)} %copy-done.12, f32[160,256]{1,0:T(8,128)} %copy-done.18, f32[160,256]{1,0:T(8,128)} %copy-done.19, ...), custom_call_target="tpu_custom_call" | custom-call | flops 1677721600 | bytes 8000000 | tf_op jit(solution)/shard_map/pallas_call | solution.py:120
  132.0 3.6 pad_maximum_fusion.1.refs_2_.refs_3_.other
  135.6 63.0 %collective-permute-done.17 = f32[256,256]{1,0:T(8,128)S(1)} collective-permute-done((f32[256,256]{1,0:T(8,128)S(1)}, f32[256,256]{1,0:T(8,128)S(1)}, u32[]{:S(2)}, u32[]{:S(2)}) %collective-permute-start.17) | collective-permute-done | bytes 262176 | tf_op jit(solution)/shard_map/ppermute | solution.py:301
  200.1 5.1 %collective-permute-done.19 = f32[256,256]{1,0:T(8,128)S(1)} collective-permute-done((f32[256,256]{1,0:T(8,128)S(1)}, f32[256,256]{1,0:T(8,128)S(1)}, u32[]{:S(2)}, u32[]{:S(2)}) %collective-permute-start.19) | collective-permute-done | bytes 262176 | tf_op jit(solution)/shard_map/ppermute | solution.py:301
  206.3 3.0 collective-permute-done.15
  211.5 13.1 %shard_map.79 = (f32[64,3200]{1,0:T(8,128)}, f32[64,3200]{1,0:T(8,128)}, f32[64,3200]{1,0:T(8,128)}, f32[64,3200]{1,0:T(8,128)}) custom-call(bf16[256,1280]{1,0:T(8,128)(2,1)} %get-tuple-element.30.big_t, bf16[256,1280]{1,0:T(8,128)(2,1)} %get-tuple-element.31.low_t, f32[1280,3200]{1,0:T(8,128)} %refs_6_.1), custom_call_target="tpu_custom_call" | custom-call | flops 6291456000 | bytes 20480000 | tf_op jit(solution)/shard_map/pallas_call | solution.py:120
  224.6 8.1 %shard_map.80 = (f32[32,3200]{1,0:T(8,128)}, f32[32,3200]{1,0:T(8,128)}, f32[64,3200]{1,0:T(8,128)}, f32[32,3200]{1,0:T(8,128)}, f32[32,3200]{1,0:T(8,128)}, /*index=5*/f32[64,3200]{1,0:T(8,128)}) custom-call(s32[4]{0:T(128)} %pad_add_fusion.ids, f32[256,256]{1,0:T(8,128)} %copy-done.8, f32[256,256]{1,0:T(8,128)} %collective-permute-done.20.other, ...), custom_call_target="tpu_custom_call" | custom-call | flops 1677721600 | bytes 8192000 | tf_op jit(solution)/shard_map/pallas_call | solution.py:120
  233.8 46.8 %collective-permute-done.16 = f32[256,256]{1,0:T(8,128)} collective-permute-done((f32[256,256]{1,0:T(8,128)}, f32[256,256]{1,0:T(8,128)}, u32[]{:S(2)}, u32[]{:S(2)}) %collective-permute-start.16) | collective-permute-done | bytes 262176 | tf_op jit(solution)/shard_map/ppermute | solution.py:301
  282.4 13.6 %shard_map.78.inverse = f32[256,256]{1,0:T(8,128)} custom-call(f32[256,256]{1,0:T(8,128)} %add.80.gram_ref), custom_call_target="tpu_custom_call" | custom-call | flops 20000000000 | bytes 10000000 | tf_op jit(solution)/shard_map/pallas_call | solution.py:95
  296.0 2.8 fusion.7
  303.6 7.8 %collective-permute-done.26 = f32[32,3200]{1,0:T(8,128)S(1)} collective-permute-done((f32[32,3200]{1,0:T(8,128)S(1)}, f32[32,3200]{1,0:T(8,128)S(1)}, u32[]{:S(2)}, u32[]{:S(2)}) %collective-permute-start.26) | collective-permute-done | bytes 409632 | tf_op jit(solution)/shard_map/ppermute | solution.py:301
  313.1 14.7 %collective-permute-done.22 = f32[32,3200]{1,0:T(8,128)S(1)} collective-permute-done((f32[32,3200]{1,0:T(8,128)S(1)}, f32[32,3200]{1,0:T(8,128)S(1)}, u32[]{:S(2)}, u32[]{:S(2)}) %collective-permute-start.22) | collective-permute-done | bytes 409632 | tf_op jit(solution)/shard_map/ppermute | solution.py:301
  331.1 10.2 %collective-permute-done.23.refs_1_ = f32[32,3200]{1,0:T(8,128)S(1)} collective-permute-done((f32[32,3200]{1,0:T(8,128)S(1)}, f32[32,3200]{1,0:T(8,128)S(1)}, u32[]{:S(2)}, u32[]{:S(2)}) %collective-permute-start.23) | collective-permute-done | bytes 409632 | tf_op jit(solution)/shard_map/ppermute | solution.py:301
  346.5 12.5 %collective-permute-done.28.refs_5_ = f32[64,3200]{1,0:T(8,128)} collective-permute-done((f32[64,3200]{1,0:T(8,128)S(1)}, f32[64,3200]{1,0:T(8,128)}, u32[]{:S(2)}, u32[]{:S(2)}) %collective-permute-start.28) | collective-permute-done | bytes 819232 | tf_op jit(solution)/shard_map/ppermute | solution.py:301
  359.5 20.5 %shard_map.83.refs_7_ = f32[1280,3200]{1,0:T(8,128)} custom-call(s32[4]{0:T(128)} %pad_add_fusion.ids, bf16[4,1280,256]{2,1,0:T(8,128)(2,1)} %pad_maximum_fusion.refs_0_.refs_1_.own, bf16[4,1280,256]{2,1,0:T(8,128)(2,1)} %pad_maximum_fusion.refs_0_.refs_1_.own, bf16[4,1280,256]{2,1,0:T(8,128)(2,1)} %pad_maximum_fusion.1.refs_2_.refs_3_.other, ...), custom_call_target="tpu_custom_call" | custom-call | flops 8388608000 | bytes 32768000 | tf_op jit(solution)/shard_map/pallas_call | solution.py:120
  380.0 9.8 %shard_map.81 = (f32[256,3200]{1,0:T(8,128)}, f32[8,256]{1,0:T(8,128)}, f32[1280,256]{1,0:T(8,128)}) custom-call(s32[4]{0:T(128)} %pad_add_fusion.ids, f32[256,256]{1,0:T(8,128)} %shard_map.78.inverse, f32[1280,256]{1,0:T(8,128)} %get-tuple-element.28.sketch, f32[32,3200]{1,0:T(8,128)} %copy-done.4, f32[32,3200]{1,0:T(8,128)} %copy-done.7, ...), custom_call_target="tpu_custom_call" | custom-call | flops 1258291200 | bytes 9830400 | tf_op jit(solution)/shard_map/pallas_call | solution.py:120
  390.8 20.1 %shard_map.84.base = f32[1280,3200]{1,0:T(8,128)} custom-call(s32[4]{0:T(128)} %pad_add_fusion.ids, bf16[4,1280,256]{2,1,0:T(8,128)(2,1)} %pad_maximum_fusion.refs_0_.refs_1_.own, bf16[4,1280,256]{2,1,0:T(8,128)(2,1)} %pad_maximum_fusion.refs_0_.refs_1_.own, bf16[4,1280,256]{2,1,0:T(8,128)(2,1)} %pad_maximum_fusion.1.refs_2_.refs_3_.other, ...), custom_call_target="tpu_custom_call" | custom-call | flops 6291456000 | bytes 32768000 | tf_op jit(solution)/shard_map/pallas_call | solution.py:120
  416.8 19.0 %shard_map.85 = f32[1280,3200]{1,0:T(8,128)} custom-call(s32[4]{0:T(128)} %pad_add_fusion.ids, bf16[4,1280,256]{2,1,0:T(8,128)(2,1)} %pad_maximum_fusion.refs_0_.refs_1_.own, bf16[4,1280,256]{2,1,0:T(8,128)(2,1)} %pad_maximum_fusion.1.refs_2_.refs_3_.other, bf16[128,3200]{1,0:T(8,128)(2,1)} %copy-done.11, ...), custom_call_target="tpu_custom_call", output_to_operand_aliasing={{}: (7, {})} | custom-call | flops 4194304000 | bytes 32768000 | tf_op jit(solution)/shard_map/pallas_call | solution.py:120
  436.4 15.6 %shard_map.82 = (f32[1280,3200]{1,0:T(8,128)}, f32[3200,256]{1,0:T(8,128)}) custom-call(f32[8,256]{1,0:T(8,128)} %add_add_fusion.squares, f32[1280,256]{1,0:T(8,128)} %get-tuple-element.43.basis, f32[256,3200]{1,0:T(8,128)} %get-tuple-element.44.right, bf16[1280,3200]{1,0:T(8,128)(2,1)} %weights.1), custom_call_target="tpu_custom_call" | custom-call | flops 6291456000 | bytes 24576000 | tf_op jit(solution)/shard_map/pallas_call | solution.py:120
  (136 shorter events, 62.7 us)
Async XLA Ops:
  15.2 30.1 %collective-permute-start = (bf16[1280,256]{1,0:T(8,128)(2,1)}, bf16[1280,256]{1,0:T(8,128)(2,1)}, u32[]{:S(2)}, u32[]{:S(2)}) collective-permute-start(bf16[1280,256]{1,0:T(8,128)(2,1)} %bitcast.4.refs_0_.refs_5_), channel_id=1, source_target_pairs={{0,2},{1,3},{2,0},{3,1},{4,6},{5,7},{6,4},{7,5},{8,10},{9,11},{10,... | collective-permute-start | bytes 1966088 | tf_op jit(solution)/shard_map/ppermute | solution.py:301
  16.8 46.9 %collective-permute-start.1 = (bf16[1280,256]{1,0:T(8,128)(2,1)}, bf16[1280,256]{1,0:T(8,128)(2,1)}, u32[]{:S(2)}, u32[]{:S(2)}) collective-permute-start(bf16[1280,256]{1,0:T(8,128)(2,1)} %bitcast.4.refs_0_.refs_5_), channel_id=1, source_target_pairs={{0,4},{1,5},{2,6},{3,7},{4,0},{5,1},{6,2},{7,3},{8,12},{9,13},{10,... | collective-permute-start | bytes 1966088 | tf_op jit(solution)/shard_map/ppermute | solution.py:301
  19.4 44.3 %collective-permute-start.2 = (bf16[1280,256]{1,0:T(8,128)(2,1)}, bf16[1280,256]{1,0:T(8,128)(2,1)}, u32[]{:S(2)}, u32[]{:S(2)}) collective-permute-start(bf16[1280,256]{1,0:T(8,128)(2,1)} %bitcast.4.refs_0_.refs_5_), channel_id=1, source_target_pairs={{0,6},{1,7},{2,4},{3,5},{4,2},{5,3},{6,0},{7,1},{8,14},{9,15},{10,... | collective-permute-start | bytes 1966088 | tf_op jit(solution)/shard_map/ppermute | solution.py:301
  19.6 14.6 %collective-permute-start.5 = (f32[256,256]{1,0:T(8,128)S(1)}, f32[256,256]{1,0:T(8,128)}, u32[]{:S(2)}, u32[]{:S(2)}) collective-permute-start(f32[256,256]{1,0:T(8,128)S(1)} %dynamic-slice_add_fusion.refs_4_), channel_id=1, source_target_pairs={{0,16},{8,24},{16,0},{24,8},{1,17},{9,25},{17,1},{25,9},{2,18},{10... | collective-permute-start | bytes 786440 | tf_op jit(solution)/shard_map/ppermute | solution.py:301
  72.2 14.9 %collective-permute-start.10 = (f32[160,256]{1,0:T(8,128)S(1)}, f32[160,256]{1,0:T(8,128)S(1)}, u32[]{:S(2)}, u32[]{:S(2)}) collective-permute-start(f32[160,256]{1,0:T(8,128)S(1)} %get-tuple-element.55), channel_id=1, source_target_pairs={{0,6},{1,7},{2,4},{3,5},{4,2},{5,3},{6,0},{7,1},{8,14},{9,15},{10,... | collective-permute-start | bytes 491528 | tf_op jit(solution)/shard_map/ppermute | solution.py:301
  74.7 17.2 %collective-permute-start.8 = (f32[160,256]{1,0:T(8,128)S(1)}, f32[160,256]{1,0:T(8,128)S(1)}, u32[]{:S(2)}, u32[]{:S(2)}) collective-permute-start(f32[160,256]{1,0:T(8,128)S(1)} %get-tuple-element.54), channel_id=1, source_target_pairs={{0,2},{1,3},{2,0},{3,1},{4,6},{5,7},{6,4},{7,5},{8,10},{9,11},{10,... | collective-permute-start | bytes 491528 | tf_op jit(solution)/shard_map/ppermute | solution.py:301
  98.4 15.1 %collective-permute-start.12 = (f32[160,256]{1,0:T(8,128)S(1)}, f32[160,256]{1,0:T(8,128)S(1)}, u32[]{:S(2)}, u32[]{:S(2)}) collective-permute-start(f32[160,256]{1,0:T(8,128)S(1)} %fusion.5.refs_0_), channel_id=1, source_target_pairs={{0,4},{1,5},{2,6},{3,7},{4,0},{5,1},{6,2},{7,3},{8,12},{9,13},{10,... | collective-permute-start | bytes 491528 | tf_op jit(solution)/shard_map/ppermute | solution.py:301
  114.1 14.3 %collective-permute-start.34 = (bf16[1280,256]{1,0:T(8,128)(2,1)}, bf16[1280,256]{1,0:T(8,128)(2,1)}, u32[]{:S(2)}, u32[]{:S(2)}) collective-permute-start(bf16[1280,256]{1,0:T(8,128)(2,1)} %collective-permute-done.refs_1_.refs_6_), channel_id=1, source_target_pairs={{0,1},{1,0},{2,3},{3,2},{4,5},{5,4},{6,7},{7,6},{8,9},{9,8},{10,11... | collective-permute-start | bytes 1966088 | tf_op jit(solution)/shard_map/ppermute | solution.py:301
  114.2 15.7 %collective-permute-start.35 = (bf16[1280,256]{1,0:T(8,128)(2,1)}, bf16[1280,256]{1,0:T(8,128)(2,1)}, u32[]{:S(2)}, u32[]{:S(2)}) collective-permute-start(bf16[1280,256]{1,0:T(8,128)(2,1)} %collective-permute-done.1.refs_2_.refs_7_), channel_id=1, source_target_pairs={{0,1},{1,0},{2,3},{3,2},{4,5},{5,4},{6,7},{7,6},{8,9},{9,8},{10,11... | collective-permute-start | bytes 1966088 | tf_op jit(solution)/shard_map/ppermute | solution.py:301
  114.6 15.8 %collective-permute-start.36 = (bf16[1280,256]{1,0:T(8,128)(2,1)}, bf16[1280,256]{1,0:T(8,128)(2,1)}, u32[]{:S(2)}, u32[]{:S(2)}) collective-permute-start(bf16[1280,256]{1,0:T(8,128)(2,1)} %collective-permute-done.2.refs_3_.refs_8_), channel_id=1, source_target_pairs={{0,1},{1,0},{2,3},{3,2},{4,5},{5,4},{6,7},{7,6},{8,9},{9,8},{10,11... | collective-permute-start | bytes 1966088 | tf_op jit(solution)/shard_map/ppermute | solution.py:301
  119.2 176.8 %collective-permute-start.37 = (bf16[512,3200]{1,0:T(8,128)(2,1)S(1)}, bf16[512,3200]{1,0:T(8,128)(2,1)}, u32[]{:S(2)}, u32[]{:S(2)}) collective-permute-start(bf16[512,3200]{1,0:T(8,128)(2,1)S(1)} %copy-done.2), channel_id=1, source_target_pairs={{0,8},{8,0},{16,24},{24,16},{1,9},{9,1},{17,25},{25,17},{2,10},{10... | collective-permute-start | bytes 9830408 | tf_op jit(solution)/shard_map/ppermute | solution.py:301
  126.9 71.7 %collective-permute-start.17 = (f32[256,256]{1,0:T(8,128)S(1)}, f32[256,256]{1,0:T(8,128)S(1)}, u32[]{:S(2)}, u32[]{:S(2)}) collective-permute-start(f32[256,256]{1,0:T(8,128)S(1)} %get-tuple-element.51), channel_id=1, source_target_pairs={{0,8},{8,0},{16,24},{24,16},{1,9},{9,1},{17,25},{25,17},{2,10},{10... | collective-permute-start | bytes 786440 | tf_op jit(solution)/shard_map/ppermute | solution.py:301
  128.5 71.6 %collective-permute-start.18 = (f32[256,256]{1,0:T(8,128)S(1)}, f32[256,256]{1,0:T(8,128)S(1)}, u32[]{:S(2)}, u32[]{:S(2)}) collective-permute-start(f32[256,256]{1,0:T(8,128)S(1)} %get-tuple-element.53), channel_id=1, source_target_pairs={{0,16},{8,24},{16,0},{24,8},{1,17},{9,25},{17,1},{25,9},{2,18},{10... | collective-permute-start | bytes 786440 | tf_op jit(solution)/shard_map/ppermute | solution.py:301
  130.0 75.2 %collective-permute-start.19 = (f32[256,256]{1,0:T(8,128)S(1)}, f32[256,256]{1,0:T(8,128)S(1)}, u32[]{:S(2)}, u32[]{:S(2)}) collective-permute-start(f32[256,256]{1,0:T(8,128)S(1)} %get-tuple-element.52), channel_id=1, source_target_pairs={{0,24},{8,16},{16,8},{24,0},{1,25},{9,17},{17,9},{25,1},{2,26},{10... | collective-permute-start | bytes 786440 | tf_op jit(solution)/shard_map/ppermute | solution.py:301
  130.5 78.8 %collective-permute-start.15 = (f32[256,256]{1,0:T(8,128)}, f32[256,256]{1,0:T(8,128)S(1)}, u32[]{:S(2)}, u32[]{:S(2)}) collective-permute-start(f32[256,256]{1,0:T(8,128)} %get-tuple-element.27), channel_id=1, source_target_pairs={{0,8},{8,0},{16,24},{24,16},{1,9},{9,1},{17,25},{25,17},{2,10},{10... | collective-permute-start | bytes 786440 | tf_op jit(solution)/shard_map/ppermute | solution.py:301
  198.6 144.3 %collective-permute-start.39 = (bf16[512,3200]{1,0:T(8,128)(2,1)S(1)}, bf16[512,3200]{1,0:T(8,128)(2,1)}, u32[]{:S(2)}, u32[]{:S(2)}) collective-permute-start(bf16[512,3200]{1,0:T(8,128)(2,1)S(1)} %copy-done.2), channel_id=1, source_target_pairs={{0,16},{8,24},{16,0},{24,8},{1,17},{9,25},{17,1},{25,9},{2,18},{10... | collective-permute-start | bytes 9830408 | tf_op jit(solution)/shard_map/ppermute | solution.py:301
  206.2 18.4 %collective-permute-start.20 = (f32[256,256]{1,0:T(8,128)S(1)}, f32[256,256]{1,0:T(8,128)}, u32[]{:S(2)}, u32[]{:S(2)}) collective-permute-start(f32[256,256]{1,0:T(8,128)S(1)} %fusion.3.own), channel_id=1, source_target_pairs={{0,1},{1,0},{2,3},{3,2},{4,5},{5,4},{6,7},{7,6},{8,9},{9,8},{10,11... | collective-permute-start | bytes 786440 | tf_op jit(solution)/shard_map/ppermute | solution.py:301
  210.0 70.6 %collective-permute-start.16 = (f32[256,256]{1,0:T(8,128)}, f32[256,256]{1,0:T(8,128)}, u32[]{:S(2)}, u32[]{:S(2)}) collective-permute-start(f32[256,256]{1,0:T(8,128)} %add.79), channel_id=1, source_target_pairs={{0,16},{8,24},{16,0},{24,8},{1,17},{9,25},{17,1},{25,9},{2,18},{10... | collective-permute-start | bytes 786440 | tf_op jit(solution)/shard_map/ppermute | solution.py:301
  232.7 66.6 %collective-permute-start.25 = (f32[64,3200]{1,0:T(8,128)}, f32[64,3200]{1,0:T(8,128)}, u32[]{:S(2)}, u32[]{:S(2)}) collective-permute-start(f32[64,3200]{1,0:T(8,128)} %get-tuple-element.40), channel_id=1, source_target_pairs={{0,16},{8,24},{16,0},{24,8},{1,17},{9,25},{17,1},{25,9},{2,18},{10... | collective-permute-start | bytes 2457608 | tf_op jit(solution)/shard_map/ppermute | solution.py:301
  233.3 67.7 %collective-permute-start.21 = (f32[64,3200]{1,0:T(8,128)}, f32[64,3200]{1,0:T(8,128)}, u32[]{:S(2)}, u32[]{:S(2)}) collective-permute-start(f32[64,3200]{1,0:T(8,128)} %get-tuple-element.37), channel_id=1, source_target_pairs={{0,8},{8,0},{16,24},{24,16},{1,9},{9,1},{17,25},{25,17},{2,10},{10... | collective-permute-start | bytes 2457608 | tf_op jit(solution)/shard_map/ppermute | solution.py:301
  298.8 91.2 %collective-permute-start.41 = (bf16[128,3200]{1,0:T(8,128)(2,1)}, bf16[128,3200]{1,0:T(8,128)(2,1)}, u32[]{:S(2)}, u32[]{:S(2)}) collective-permute-start(bf16[128,3200]{1,0:T(8,128)(2,1)} %get-tuple-element.49), channel_id=1, source_target_pairs={{0,16},{8,24},{16,0},{24,8},{1,17},{9,25},{17,1},{25,9},{2,18},{10... | collective-permute-start | bytes 2457608 | tf_op jit(solution)/shard_map/ppermute | solution.py:301
  302.0 25.8 %collective-permute-start.22 = (f32[32,3200]{1,0:T(8,128)S(1)}, f32[32,3200]{1,0:T(8,128)S(1)}, u32[]{:S(2)}, u32[]{:S(2)}) collective-permute-start(f32[32,3200]{1,0:T(8,128)S(1)} %slice_add_fusion.2), channel_id=1, source_target_pairs={{0,16},{8,24},{16,0},{24,8},{1,17},{9,25},{17,1},{25,9},{2,18},{10... | collective-permute-start | bytes 1228808 | tf_op jit(solution)/shard_map/ppermute | solution.py:301
  312.5 17.0 %collective-permute-start.27 = (f32[32,3200]{1,0:T(8,128)S(1)}, f32[32,3200]{1,0:T(8,128)S(1)}, u32[]{:S(2)}, u32[]{:S(2)}) collective-permute-start(f32[32,3200]{1,0:T(8,128)S(1)} %fusion.refs_3_), channel_id=1, source_target_pairs={{0,8},{8,0},{16,24},{24,16},{1,9},{9,1},{17,25},{25,17},{2,10},{10... | collective-permute-start | bytes 1228808 | tf_op jit(solution)/shard_map/ppermute | solution.py:301
  329.6 29.4 %collective-permute-start.28 = (f32[64,3200]{1,0:T(8,128)S(1)}, f32[64,3200]{1,0:T(8,128)}, u32[]{:S(2)}, u32[]{:S(2)}) collective-permute-start(f32[64,3200]{1,0:T(8,128)S(1)} %pad_maximum_fusion.3), channel_id=1, source_target_pairs={{0,16},{8,24},{16,0},{24,8},{1,17},{9,25},{17,1},{25,9},{2,18},{10... | collective-permute-start | bytes 2457608 | tf_op jit(solution)/shard_map/ppermute | solution.py:301
  342.3 37.7 %collective-permute-start.24 = (f32[64,3200]{1,0:T(8,128)}, f32[64,3200]{1,0:T(8,128)}, u32[]{:S(2)}, u32[]{:S(2)}) collective-permute-start(f32[64,3200]{1,0:T(8,128)} %pad_maximum_fusion.2), channel_id=1, source_target_pairs={{0,8},{8,0},{16,24},{24,16},{1,9},{9,1},{17,25},{25,17},{2,10},{10... | collective-permute-start | bytes 2457608 | tf_op jit(solution)/shard_map/ppermute | solution.py:301
  344.4 45.5 %collective-permute-start.42 = (bf16[128,3200]{1,0:T(8,128)(2,1)S(1)}, bf16[128,3200]{1,0:T(8,128)(2,1)S(1)}, u32[]{:S(2)}, u32[]{:S(2)}) collective-permute-start(bf16[128,3200]{1,0:T(8,128)(2,1)S(1)} %get-tuple-element.47), channel_id=1, source_target_pairs={{0,8},{8,0},{16,24},{24,16},{1,9},{9,1},{17,25},{25,17},{2,10},{10... | collective-permute-start | bytes 2457608 | tf_op jit(solution)/shard_map/ppermute | solution.py:301
  346.0 70.0 %collective-permute-start.38 = (bf16[128,3200]{1,0:T(8,128)(2,1)}, bf16[128,3200]{1,0:T(8,128)(2,1)S(1)}, u32[]{:S(2)}, u32[]{:S(2)}) collective-permute-start(bf16[128,3200]{1,0:T(8,128)(2,1)} %get-tuple-element.50), channel_id=1, source_target_pairs={{0,16},{8,24},{16,0},{24,8},{1,17},{9,25},{17,1},{25,9},{2,18},{10... | collective-permute-start | bytes 2457608 | tf_op jit(solution)/shard_map/ppermute | solution.py:301
  359.0 56.9 %collective-permute-start.40 = (bf16[128,3200]{1,0:T(8,128)(2,1)S(1)}, bf16[128,3200]{1,0:T(8,128)(2,1)}, u32[]{:S(2)}, u32[]{:S(2)}) collective-permute-start(bf16[128,3200]{1,0:T(8,128)(2,1)S(1)} %get-tuple-element.48), channel_id=1, source_target_pairs={{0,8},{8,0},{16,24},{24,16},{1,9},{9,1},{17,25},{25,17},{2,10},{10... | collective-permute-start | bytes 2457608 | tf_op jit(solution)/shard_map/ppermute | solution.py:301
  389.8 21.1 %collective-permute-start.29 = (f32[8,256]{1,0:T(8,128)}, f32[8,256]{1,0:T(8,128)S(1)}, u32[]{:S(2)}, u32[]{:S(2)}) collective-permute-start(f32[8,256]{1,0:T(8,128)} %get-tuple-element.42), channel_id=1, source_target_pairs={{0,1},{1,0},{2,3},{3,2},{4,5},{5,4},{6,7},{7,6},{8,9},{9,8},{10,11... | collective-permute-start | bytes 24584 | tf_op jit(solution)/shard_map/ppermute | solution.py:301
  411.0 24.8 %collective-permute-start.30 = (f32[8,256]{1,0:T(8,128)S(1)}, f32[8,256]{1,0:T(8,128)S(1)}, u32[]{:S(2)}, u32[]{:S(2)}) collective-permute-start(f32[8,256]{1,0:T(8,128)S(1)} %add.90), channel_id=1, source_target_pairs={{0,2},{1,3},{2,0},{3,1},{4,6},{5,7},{6,4},{7,5},{8,10},{9,11},{10,... | collective-permute-start | bytes 24584 | tf_op jit(solution)/shard_map/ppermute | solution.py:301
  413.5 22.4 %collective-permute-start.31 = (f32[8,256]{1,0:T(8,128)S(1)}, f32[8,256]{1,0:T(8,128)S(1)}, u32[]{:S(2)}, u32[]{:S(2)}) collective-permute-start(f32[8,256]{1,0:T(8,128)S(1)} %add.90), channel_id=1, source_target_pairs={{0,4},{1,5},{2,6},{3,7},{4,0},{5,1},{6,2},{7,3},{8,12},{9,13},{10,... | collective-permute-start | bytes 24584 | tf_op jit(solution)/shard_map/ppermute | solution.py:301
  414.5 21.3 %collective-permute-start.32 = (f32[8,256]{1,0:T(8,128)S(1)}, f32[8,256]{1,0:T(8,128)S(1)}, u32[]{:S(2)}, u32[]{:S(2)}) collective-permute-start(f32[8,256]{1,0:T(8,128)S(1)} %add.90), channel_id=1, source_target_pairs={{0,6},{1,7},{2,4},{3,5},{4,2},{5,3},{6,0},{7,1},{8,14},{9,15},{10,... | collective-permute-start | bytes 24584 | tf_op jit(solution)/shard_map/ppermute | solution.py:301
  (34 other events, 411.3 us)

commit v3 on v2

--- a/solution.py
+++ b/solution.py
@@ -103,6 +103,7 @@
 
 
 bf16 = jnp.bfloat16
+VMEM_MIB = 40
 whole_vmem = pl.BlockSpec(memory_space=pltpu.VMEM)
 whole_smem = pl.BlockSpec(memory_space=pltpu.SMEM)
 
@@ -124,6 +125,7 @@
             num_scalar_prefetch=prefetch, grid=grid, in_specs=specs, out_specs=out_specs, scratch_shapes=list(scratch)
         ),
         input_output_aliases=aliases,
+        compiler_params=pltpu.CompilerParams(vmem_limit_bytes=VMEM_MIB * 2**20),
         cost_estimate=pl.CostEstimate(flops=flops, bytes_accessed=moved, transcendentals=0),
     )(*ins)
 
@@ -151,7 +153,7 @@
 
 def gram_kernel(ids, *refs):
     parts, other, grads = refs[:4], refs[4], refs[5:9]
-    sketch, gram, tokens, big_t, low_t, flip = refs[9:]
+    sketch, gram, t0, t1, t2, t3, big_t, low_t, flip, tokens = refs[9:]
     row, z, core, shift = ids[0], ids[1], ids[2], ids[3]
     rows = parts[0].shape[0]
     for k in range(4):
@@ -164,6 +166,8 @@
     for k in range(4):
         g = grads[k][...]
         tokens[k ^ shift] = mm(g, big, ((0,), (0,))) + mm(g, low, ((0,), (0,)))
+    for j, ref in enumerate((t0, t1, t2, t3)):
+        ref[...] = tokens[j]
     flip[...] = s.T
     size = flip.shape[0] // 8
     for i in range(8):
@@ -221,29 +225,16 @@
         out[...] = send[...] + total[at + 2 * size : at + 4 * size, :]
 
 
-def gradient_kernel(count, crossing, ids, *refs):
-    own, other = refs[:count], refs[count : 2 * count]
-    blocks, base, out = refs[2 * count : -2], refs[-2], refs[-1]
-    core = ids[2]
+def gradient_kernel(numbers, ids, *refs):
+    count = len(numbers) // 2
+    own, other, pieces = refs[:count], refs[count : 2 * count], list(refs[2 * count : -2])
+    base, out = refs[-2], refs[-1]
     total = base[...]
-    for at_block in range(count - crossing):
-        x = blocks[at_block]
-        half = x.shape[0] // 2
-        at = pl.multiple_of(core * half, half)
-        total += mm(own[at_block][0], x[pl.ds(at, half), :], ((1,), (0,)))
-        at = pl.multiple_of((1 - core) * half, half)
-        total += mm(other[at_block][0], x[pl.ds(at, half), :], ((1,), (0,)))
-    if crossing:
-        total += crossed(core, own[-1], other[-1], blocks[-2], blocks[-1], 0)
+    for at, number in enumerate(numbers):
+        x = jnp.concatenate([pieces.pop(0)[...] for _ in range(number)], axis=0)
+        grad = jnp.where(ids[2] == at % 2, own[at // 2][0], other[at // 2][0])
+        total += mm(grad, x, ((1,), (0,)))
     out[...] = total
-
-
-def crossed(core, own, other, first, second, part):
-    size = first.shape[0]
-    cut = slice(part * size, (part + 1) * size)
-    mine = jnp.where(core == 0, first[...], second[...])
-    its = jnp.where(core == 0, second[...], first[...])
-    return mm(own[0][:, cut], mine, ((1,), (0,))) + mm(other[0][:, cut], its, ((1,), (0,)))
 
 
 def right_kernel(n, ids, inverse, sketch, *refs):
@@ -287,13 +278,12 @@
     factor_out[...] = right[...].T * scale
 
 
-def momentum_kernel(ids, own, other, first, second, basis, right, base, out, small):
+def momentum_kernel(basis, right, base, out, small):
     @pl.when(pl.program_id(0) == 0)
     def _():
         small[...] = (basis[...] * -(1.0 - mix_rate)).astype(bf16)
 
-    total = base[...] + crossed(ids[2], own, other, first, second, 1)
-    out[...] = total + mm(small[...], right[...].astype(bf16), ((1,), (0,)))
+    out[...] = base[...] + mm(small[...], right[...].astype(bf16), ((1,), (0,)))
 
 
 def swap(x, axis, bit):
@@ -338,8 +328,13 @@
     send = lax.dynamic_slice_in_dim(in_right, (1 - core) * block, block, 0)
     in_right = keep + swap(send, "col", 1)
     rights = [in_right] + swaps(in_right, "row", 1)
-    x_all = swap(inputs, "row", 1)
-    y_all = swap(inputs, "row", 2)
+    quarter = tokens // 4
+    cut0, cut2 = inputs[:quarter], inputs[2 * quarter : 3 * quarter]
+    cut1, cut3 = inputs[quarter : 2 * quarter], inputs[3 * quarter :]
+    half0, half1 = inputs[: 2 * quarter], inputs[2 * quarter :]
+    x0, y2 = swap(cut0, "row", 1), swap(cut2, "row", 2)
+    x1, y3 = swap(cut1, "row", 1), swap(cut3, "row", 2)
+    x23, y01 = swap(half1, "row", 1), swap(half0, "row", 2)
     other = [swap(g, "col", 1) for g in own]
     own_all = jnp.stack(own)
     other_all = jnp.stack(other)
@@ -357,17 +352,14 @@
     parts = [total] + swaps(total, "col", 2)
     rest = swap(jnp.concatenate(parts, axis=0), "col", 1)
 
-    quarter = tokens // 4
-    x_first, x_second = x_all[:quarter], x_all[quarter : 2 * quarter]
-    y_first, y_second = y_all[2 * quarter : 3 * quarter], y_all[3 * quarter :]
-    first_by_y, first_by_x = swap(x_first, "row", 2), swap(y_first, "row", 1)
-    second_by_y, second_by_x = swap(x_second, "row", 2), swap(y_second, "row", 1)
-
-    sketch, gram, toks, big_t, low_t = call(
+    first_by_y, first_by_x = swap(x0, "row", 2), swap(y2, "row", 1)
+    second_by_y, second_by_x = swap(x1, "row", 2), swap(y3, "row", 1)
+
+    sketch, gram, *toks, big_t, low_t = call(
         gram_kernel,
-        (shaped((m, rank)), shaped((rank, rank)), shaped((4, block, rank)), shaped((rank, m), bf16), shaped((rank, m), bf16)),
-        (ids, *parts, rest, *own), [whole_smem] + [whole_vmem] * 9, (whole_vmem,) * 5,
-        scratch=[pltpu.VMEM((rank, m), f32)], flops=20 * m * rank * rank, moved=8_000_000)
+        (shaped((m, rank)), shaped((rank, rank)), *([shaped((block, rank))] * 4), shaped((rank, m), bf16), shaped((rank, m), bf16)),
+        (ids, *parts, rest, *own), [whole_smem] + [whole_vmem] * 9, (whole_vmem,) * 8,
+        scratch=[pltpu.VMEM((rank, m), f32), pltpu.VMEM((4, block, rank), f32)], flops=20 * m * rank * rank, moved=8_000_000)
     token = toks[0]
     for k in (1, 2, 3):
         token = token + swap(toks[k], "row", k)
@@ -397,16 +389,16 @@
 
     inverse = inverse_factor(gram)
 
-    def gradient(picks, crossing, blocks, base):
-        count = len(picks)
+    def gradient(picks, numbers, pieces, base):
         return call(
-            functools.partial(gradient_kernel, count, crossing), shaped((m, n)),
-            (ids, *([own_all] * count), *([other_all] * count), *blocks, base),
-            [pick(j) for j in picks] * 2 + [columns(x.shape[0]) for x in blocks] + [columns(m)], columns(m), tiles,
-            flops=2 * m * n * sum(x.shape[0] for x in blocks), moved=8 * m * n, prefetch=1)
-
-    moment = gradient((0, 1), 0, (inputs, x_all), momentum)
-    moment = gradient((2, 3), 1, (y_all, first_by_y, first_by_x), moment)
+            functools.partial(gradient_kernel, numbers), shaped((m, n)),
+            (ids, *([own_all] * len(picks)), *([other_all] * len(picks)), *pieces, base),
+            [pick(j) for j in picks] * 2 + [columns(x.shape[0]) for x in pieces] + [columns(m)], columns(m), tiles,
+            flops=2 * m * n * sum(x.shape[0] for x in pieces), moved=8 * m * n, prefetch=1)
+
+    moment = gradient((0, 1), (1, 1, 2, 1), (half0, half1, x0, x1, x23), momentum)
+    moment = gradient(
+        (2, 3), (1, 2, 2, 2), (y01, y2, y3, first_by_y, second_by_y, first_by_x, second_by_x), moment)
 
     right, squares, basis = call(
         functools.partial(right_kernel, n), (shaped((rank, n)), shaped((8, rank)), shaped((m, rank))),
@@ -424,10 +416,9 @@
         (columns(m), pl.BlockSpec((tn, rank), lambda i, *_: (i, 0))), tiles,
         scratch=[pltpu.VMEM((m, rank), bf16)] * 2, flops=6 * m * n * rank, moved=6 * m * n)
     momentum_new = call(
-        momentum_kernel, shaped((m, n)), (ids, own_all, other_all, second_by_y, second_by_x, basis, right, moment),
-        [pick(3), pick(3), columns(quarter), columns(quarter), fixed(m, rank), columns(rank), columns(m)],
+        momentum_kernel, shaped((m, n)), (basis, right, moment), [fixed(m, rank), columns(rank), columns(m)],
         columns(m), tiles, scratch=[pltpu.VMEM((m, rank), bf16)],
-        flops=2 * m * n * (tokens // 2 + rank), moved=8 * m * n, prefetch=1, aliases={7: 0})
+        flops=2 * m * n * rank, moved=8 * m * n, aliases={2: 0})
     return (weights_new, momentum_new, factor_new)
 
 

time: 454 us -> 446 us (0.982)
  Pallas kernels: 131 us -> 114 us
  other arithmetic: 19.4 us -> 4.81 us
  waiting for transfers between devices: 218 us -> 227 us
  local copies, waits for them, and re-layouts: 13.2 us -> 20.9 us
  starting transfers between devices: 54.6 us -> 61.6 us
    pallas_call x9, Pallas kernels: 117 us -> 100 us  [call(): pl.pallas_call(kernel, out_shape=outs, grid_spec=pltpu.PrefetchScalarGrid...]
    unnamed x47 -> x45, local copies, waits for them, and re-layouts: 7.67 us -> 18.2 us
    ppermute x43 -> x47, waiting for transfers between devices: 218 us -> 227 us  [swap(): return lax.ppermute(x, axis, [(i, i ^ bit) for i in range(size)])]
    ppermute x43 -> x47, starting transfers between devices: 54.6 us -> 61.6 us  [swap(): return lax.ppermute(x, axis, [(i, i ^ bit) for i in range(size)])]
  transfers between devices with their start and end apart: 43 -> 47, of which waited for: 16 -> 22; matrix products, arithmetic and copies ran while one was open for 8% -> 4% of each run, Pallas kernels for 24% -> 22%
where the time goes in v3:
time: 446 us; the launch traced here: 445 us
  waiting for transfers between devices  227 us (51%)
  Pallas kernels  114 us (26%)
  starting transfers between devices  61.6 us (14%)
  local copies, waits for them, and re-layouts  20.9 us (5%)
  matrix products  15.8 us (4%)
  other arithmetic  4.81 us (1%)
    ppermute x47, waiting for transfers between devices, swap(): return lax.ppermute(x, axis, [(i, i ^ bit) for i in range(size)])  227 us
    pallas_call x9, Pallas kernels, call(): pl.pallas_call(kernel, out_shape=outs, grid_spec=pltpu.PrefetchScalarGrid...  100 us
    ppermute x47, starting transfers between devices, swap(): return lax.ppermute(x, axis, [(i, i ^ bit) for i in range(size)])  61.6 us
    unnamed x45, local copies, waits for them, and re-layouts  18.2 us
    dot_general x2, matrix products, mm(): lax.dot_general(a, b, (dims, ((), ())), precision=precision, preferred_el...  15.8 us
    pallas_call x1, Pallas kernels, inverse_factor(): pl.pallas_call(inverse_kernel, out_shape=jax.ShapeDtypeStruct(gram.shape,...  13.6 us
  transfers between devices with their start and end apart: 47, of which 22 were waited for; matrix products, arithmetic and copies ran while one was open for 4% of the time, Pallas kernels for 22%

profile of v3, /device:TPU:0, one launch (start us, length us, event | category | flops | bytes accessed | tf_op | source)
XLA Modules:
  0.0 445.1 jit_solution(3248211578330888614)
XLA Ops:
  2.6 4.6 %fusion.8 = f32[512,256]{1,0:T(8,128)} fusion(bf16[512,3200]{1,0:T(8,128)(2,1)} %inputs.1, f32[3200,256]{1,0:T(8,128)S(1)} %copy-done), kind=kOutput, calls=%fused_computation.23 | convolution fusion | flops 2516582400 | bytes 7077888 | tf_op jit(solution)/shard_map/dot_general | solution.py:22
  23.4 11.2 %fusion.7.part = f32[1280,256]{1,0:T(8,128)} fusion(f32[1280,3200]{1,0:T(8,128)} %refs_9_.1, f32[3200,256]{1,0:T(8,128)S(1)} %copy-done), kind=kOutput, calls=%fused_computation.22 | convolution fusion | flops 6291456000 | bytes 20971520 | tf_op jit(solution)/shard_map/dot_general | solution.py:22
  34.7 11.6 %collective-permute-done.refs_1_.refs_6_ = bf16[1280,256]{1,0:T(8,128)(2,1)} collective-permute-done((bf16[1280,256]{1,0:T(8,128)(2,1)}, bf16[1280,256]{1,0:T(8,128)(2,1)}, u32[]{:S(2)}, u32[]{:S(2)}) %collective-permute-start) | collective-permute-done | bytes 655392 | tf_op jit(solution)/shard_map/ppermute | solution.py:291
  46.3 18.4 %collective-permute-done.1.refs_2_.refs_7_ = bf16[1280,256]{1,0:T(8,128)(2,1)} collective-permute-done((bf16[1280,256]{1,0:T(8,128)(2,1)}, bf16[1280,256]{1,0:T(8,128)(2,1)}, u32[]{:S(2)}, u32[]{:S(2)}) %collective-permute-start.1) | collective-permute-done | bytes 655392 | tf_op jit(solution)/shard_map/ppermute | solution.py:291
  66.0 3.6 shard_map.76
  74.5 15.9 %collective-permute-start.8 = (f32[160,256]{1,0:T(8,128)S(1)}, f32[160,256]{1,0:T(8,128)S(1)}, u32[]{:S(2)}, u32[]{:S(2)}) collective-permute-start(f32[160,256]{1,0:T(8,128)S(1)} %get-tuple-element.59), channel_id=1, source_target_pairs={{0,2},{1,3},{2,0},{3,1},{4,6},{5,7},{6,4},{7,5},{8,10},{9,11},{10,... | collective-permute-start | bytes 491528 | tf_op jit(solution)/shard_map/ppermute | solution.py:291
  90.3 4.8 %collective-permute-done.8 = f32[160,256]{1,0:T(8,128)S(1)} collective-permute-done((f32[160,256]{1,0:T(8,128)S(1)}, f32[160,256]{1,0:T(8,128)S(1)}, u32[]{:S(2)}, u32[]{:S(2)}) %collective-permute-start.8) | collective-permute-done | bytes 163872 | tf_op jit(solution)/shard_map/ppermute | solution.py:291
  95.1 6.3 %collective-permute-done.9 = f32[160,256]{1,0:T(8,128)S(1)} collective-permute-done((f32[160,256]{1,0:T(8,128)S(1)}, f32[160,256]{1,0:T(8,128)S(1)}, u32[]{:S(2)}, u32[]{:S(2)}) %collective-permute-start.9) | collective-permute-done | bytes 163872 | tf_op jit(solution)/shard_map/ppermute | solution.py:291
  106.0 3.6 collective-permute-done.11.refs_1_
  109.5 7.1 %collective-permute-done.12.refs_2_ = f32[160,256]{1,0:T(8,128)S(1)} collective-permute-done((f32[160,256]{1,0:T(8,128)S(1)}, f32[160,256]{1,0:T(8,128)S(1)}, u32[]{:S(2)}, u32[]{:S(2)}) %collective-permute-start.12) | collective-permute-done | bytes 163872 | tf_op jit(solution)/shard_map/ppermute | solution.py:291
  118.9 4.8 %shard_map.77 = (f32[1280,256]{1,0:T(8,128)S(1)}, f32[256,256]{1,0:T(8,128)S(1)}, f32[256,256]{1,0:T(8,128)S(1)}, f32[256,256]{1,0:T(8,128)S(1)}, f32[256,256]{1...) custom-call(s32[4]{0:T(128)S(1)} %pad_add_fusion.ids, ...), custom_call_target="tpu_custom_call" | custom-call | flops 1677721600 | bytes 8000000 | tf_op jit(solution)/shard_map/pallas_call | solution.py:121
  128.1 4.8 %collective-permute-done.17 = f32[256,256]{1,0:T(8,128)S(1)} collective-permute-done((f32[256,256]{1,0:T(8,128)S(1)}, f32[256,256]{1,0:T(8,128)S(1)}, u32[]{:S(2)}, u32[]{:S(2)}) %collective-permute-start.17) | collective-permute-done | bytes 262176 | tf_op jit(solution)/shard_map/ppermute | solution.py:291
  136.3 3.2 collective-permute-done.19
  139.7 12.4 %shard_map.79 = (f32[64,3200]{1,0:T(8,128)S(1)}, f32[64,3200]{1,0:T(8,128)S(1)}, f32[64,3200]{1,0:T(8,128)S(1)}, f32[64,3200]{1,0:T(8,128)S(1)}) custom-call(bf16[256,1280]{1,0:T(8,128)(2,1)S(1)} %get-tuple-element.36.big_t, bf16[256,1280]{1,0:T(8,128)(2,1)S(1)} %get-tuple-element.37.low_t, f32[1280,3200]{1,0:T(8,128)} %refs_9_.1), custom_call_target="tpu_custom_call" | custom-call | flops 6291456000 | bytes 20480000 | tf_op jit(solution)/shard_map/pallas_call | solution.py:121
  152.1 7.6 %shard_map.80 = (f32[32,3200]{1,0:T(8,128)S(1)}, f32[32,3200]{1,0:T(8,128)S(1)}, f32[64,3200]{1,0:T(8,128)S(1)}, f32[32,3200]{1,0:T(8,128)S(1)}, f32[32,3200]{1,0:T(8,128)S(1)}, /*index=5*/f32[64,3200]{1,0:T(8,128)S(1)}) custom-call(s32[4]{0:T(128)S(1)} %pad_add_fusion.ids, f32[256,256]{1,0:T(8,128)S(1)} %add_add_fusion.own, ...), custom_call_target="tpu_custom_call" | custom-call | flops 1677721600 | bytes 8192000 | tf_op jit(solution)/shard_map/pallas_call | solution.py:121
  164.6 15.7 %collective-permute-done.25 = f32[64,3200]{1,0:T(8,128)S(1)} collective-permute-done((f32[64,3200]{1,0:T(8,128)S(1)}, f32[64,3200]{1,0:T(8,128)S(1)}, u32[]{:S(2)}, u32[]{:S(2)}) %collective-permute-start.25) | collective-permute-done | bytes 819232 | tf_op jit(solution)/shard_map/ppermute | solution.py:291
  181.0 44.6 %collective-permute-done.21 = f32[64,3200]{1,0:T(8,128)S(1)} collective-permute-done((f32[64,3200]{1,0:T(8,128)S(1)}, f32[64,3200]{1,0:T(8,128)S(1)}, u32[]{:S(2)}, u32[]{:S(2)}) %collective-permute-start.21) | collective-permute-done | bytes 819232 | tf_op jit(solution)/shard_map/ppermute | solution.py:291
  226.1 10.1 %collective-permute-done.26 = f32[32,3200]{1,0:T(8,128)S(1)} collective-permute-done((f32[32,3200]{1,0:T(8,128)S(1)}, f32[32,3200]{1,0:T(8,128)S(1)}, u32[]{:S(2)}, u32[]{:S(2)}) %collective-permute-start.26) | collective-permute-done | bytes 409632 | tf_op jit(solution)/shard_map/ppermute | solution.py:291
  237.8 8.2 %collective-permute-done.22 = f32[32,3200]{1,0:T(8,128)S(1)} collective-permute-done((f32[32,3200]{1,0:T(8,128)S(1)}, f32[32,3200]{1,0:T(8,128)S(1)}, u32[]{:S(2)}, u32[]{:S(2)}) %collective-permute-start.22) | collective-permute-done | bytes 409632 | tf_op jit(solution)/shard_map/ppermute | solution.py:291
  247.3 7.6 %collective-permute-done.27.refs_4_ = f32[32,3200]{1,0:T(8,128)S(1)} collective-permute-done((f32[32,3200]{1,0:T(8,128)S(1)}, f32[32,3200]{1,0:T(8,128)S(1)}, u32[]{:S(2)}, u32[]{:S(2)}) %collective-permute-start.27) | collective-permute-done | bytes 409632 | tf_op jit(solution)/shard_map/ppermute | solution.py:291
  256.5 7.7 %collective-permute-done.23.refs_1_ = f32[32,3200]{1,0:T(8,128)S(1)} collective-permute-done((f32[32,3200]{1,0:T(8,128)S(1)}, f32[32,3200]{1,0:T(8,128)S(1)}, u32[]{:S(2)}, u32[]{:S(2)}) %collective-permute-start.23) | collective-permute-done | bytes 409632 | tf_op jit(solution)/shard_map/ppermute | solution.py:291
  267.8 5.5 %collective-permute-done.15 = f32[256,256]{1,0:T(8,128)S(1)} collective-permute-done((f32[256,256]{1,0:T(8,128)S(1)}, f32[256,256]{1,0:T(8,128)S(1)}, u32[]{:S(2)}, u32[]{:S(2)}) %collective-permute-start.15) | collective-permute-done | bytes 262176 | tf_op jit(solution)/shard_map/ppermute | solution.py:291
  275.3 18.6 %shard_map.83.refs_11_ = f32[1280,3200]{1,0:T(8,128)} custom-call(s32[4]{0:T(128)S(1)} %pad_add_fusion.ids, bf16[4,1280,256]{2,1,0:T(8,128)(2,1)S(1)} %pad_maximum_fusion.refs_0_.refs_1_, bf16[4,1280,256]{2,1,0:T(8,128)(2,1)S(1)} %pad_maximum_fusion.refs_0_.refs_1_, bf16[4,1280,256]{2,1,0:T(8,128)(2,1)S(1)} %pad_maximum_fusion.1.refs_2_.refs_3_, ...), custom_call_target="tpu_custom_call" | custom-call | flops 8388608000 | bytes 32768000 | tf_op jit(solution)/shard_map/pallas_call | solution.py:121
  293.9 29.3 %collective-permute-done.16 = f32[256,256]{1,0:T(8,128)S(1)} collective-permute-done((f32[256,256]{1,0:T(8,128)S(1)}, f32[256,256]{1,0:T(8,128)S(1)}, u32[]{:S(2)}, u32[]{:S(2)}) %collective-permute-start.16) | collective-permute-done | bytes 262176 | tf_op jit(solution)/shard_map/ppermute | solution.py:291
  331.3 13.6 %shard_map.78.inverse = f32[256,256]{1,0:T(8,128)} custom-call(f32[256,256]{1,0:T(8,128)} %add.80.gram_ref), custom_call_target="tpu_custom_call" | custom-call | flops 20000000000 | bytes 10000000 | tf_op jit(solution)/shard_map/pallas_call | solution.py:95
  352.6 7.9 %shard_map.81 = (f32[256,3200]{1,0:T(8,128)S(1)}, f32[8,256]{1,0:T(8,128)S(1)}, f32[1280,256]{1,0:T(8,128)S(1)}) custom-call(s32[4]{0:T(128)S(1)} %pad_add_fusion.ids, f32[256,256]{1,0:T(8,128)S(1)} %copy-done.20, f32[1280,256]{1,0:T(8,128)S(1)} %copy-done.15, f32[32,3200]{1,0:T(8,128)S(1)} %copy-done.9, f32[32,3200]{1,0:T(8,128)S(1)} %copy-done.13, ...), custom_call_target="tpu_custom_call" | custom-call | flops 1258291200 | bytes 9830400 | tf_op jit(solution)/shard_map/pallas_call | solution.py:121
  360.5 19.2 %collective-permute-done.41.refs_7_ = bf16[128,3200]{1,0:T(8,128)(2,1)} collective-permute-done((bf16[128,3200]{1,0:T(8,128)(2,1)}, bf16[128,3200]{1,0:T(8,128)(2,1)}, u32[]{:S(2)}, u32[]{:S(2)}) %collective-permute-start.41) | collective-permute-done | bytes 819232 | tf_op jit(solution)/shard_map/ppermute | solution.py:291
  379.7 11.9 %collective-permute-done.43.refs_8_ = bf16[128,3200]{1,0:T(8,128)(2,1)} collective-permute-done((bf16[128,3200]{1,0:T(8,128)(2,1)}, bf16[128,3200]{1,0:T(8,128)(2,1)}, u32[]{:S(2)}, u32[]{:S(2)}) %collective-permute-start.43) | collective-permute-done | bytes 819232 | tf_op jit(solution)/shard_map/ppermute | solution.py:291
  391.6 19.8 %shard_map.84.base = f32[1280,3200]{1,0:T(8,128)} custom-call(s32[4]{0:T(128)S(1)} %pad_add_fusion.ids, bf16[4,1280,256]{2,1,0:T(8,128)(2,1)S(1)} %pad_maximum_fusion.refs_0_.refs_1_, bf16[4,1280,256]{2,1,0:T(8,128)(2,1)S(1)} %pad_maximum_fusion.refs_0_.refs_1_, bf16[4,1280,256]{2,1,0:T(8,128)(2,1)S(1)} %copy-done.3, bf16[4,1280,256]{2,1,0:T(8,128)(2,1)S(1)} %copy-done.3, ...), custom_call_target="tpu_custom_call" | custom-call | flops 8388608000 | bytes 32768000 | tf_op jit(solution)/shard_map/pallas_call | solution.py:121
  416.4 13.8 %shard_map.85 = f32[1280,3200]{1,0:T(8,128)} custom-call(f32[1280,256]{1,0:T(8,128)S(1)} %get-tuple-element.49.basis, f32[256,3200]{1,0:T(8,128)S(1)} %get-tuple-element.50.right, f32[1280,3200]{1,0:T(8,128)} %shard_map.84.base), custom_call_target="tpu_custom_call", output_to_operand_aliasing={{}: (2, {})} | custom-call | flops 2097152000 | bytes 32768000 | tf_op jit(solution)/shard_map/pallas_call | solution.py:121
  430.2 3.3 copy-done.21
  433.6 11.5 %shard_map.82 = (f32[1280,3200]{1,0:T(8,128)}, f32[3200,256]{1,0:T(8,128)}) custom-call(f32[8,256]{1,0:T(8,128)S(1)} %add_add_fusion.1.squares, f32[1280,256]{1,0:T(8,128)S(1)} %get-tuple-element.49.basis, f32[256,3200]{1,0:T(8,128)S(1)} %get-tuple-element.50.right, bf16[1280,3200]{1,0:T(8,128)(2,1)S(1)} %copy-done.21), custom_call_target="tpu_custom_call" | custom-call | flops 6291456000 | bytes 24576000 | tf_op jit(solution)/shard_map/pallas_call | solution.py:121
  (141 shorter events, 75.9 us)
Async XLA Ops:
  16.2 30.1 %collective-permute-start = (bf16[1280,256]{1,0:T(8,128)(2,1)}, bf16[1280,256]{1,0:T(8,128)(2,1)}, u32[]{:S(2)}, u32[]{:S(2)}) collective-permute-start(bf16[1280,256]{1,0:T(8,128)(2,1)} %bitcast.4.refs_0_.refs_5_), channel_id=1, source_target_pairs={{0,2},{1,3},{2,0},{3,1},{4,6},{5,7},{6,4},{7,5},{8,10},{9,11},{10,... | collective-permute-start | bytes 1966088 | tf_op jit(solution)/shard_map/ppermute | solution.py:291
  17.7 46.9 %collective-permute-start.1 = (bf16[1280,256]{1,0:T(8,128)(2,1)}, bf16[1280,256]{1,0:T(8,128)(2,1)}, u32[]{:S(2)}, u32[]{:S(2)}) collective-permute-start(bf16[1280,256]{1,0:T(8,128)(2,1)} %bitcast.4.refs_0_.refs_5_), channel_id=1, source_target_pairs={{0,4},{1,5},{2,6},{3,7},{4,0},{5,1},{6,2},{7,3},{8,12},{9,13},{10,... | collective-permute-start | bytes 1966088 | tf_op jit(solution)/shard_map/ppermute | solution.py:291
  20.3 44.3 %collective-permute-start.2 = (bf16[1280,256]{1,0:T(8,128)(2,1)}, bf16[1280,256]{1,0:T(8,128)(2,1)}, u32[]{:S(2)}, u32[]{:S(2)}) collective-permute-start(bf16[1280,256]{1,0:T(8,128)(2,1)} %bitcast.4.refs_0_.refs_5_), channel_id=1, source_target_pairs={{0,6},{1,7},{2,4},{3,5},{4,2},{5,3},{6,0},{7,1},{8,14},{9,15},{10,... | collective-permute-start | bytes 1966088 | tf_op jit(solution)/shard_map/ppermute | solution.py:291
  20.6 14.1 %collective-permute-start.5 = (f32[256,256]{1,0:T(8,128)S(1)}, f32[256,256]{1,0:T(8,128)}, u32[]{:S(2)}, u32[]{:S(2)}) collective-permute-start(f32[256,256]{1,0:T(8,128)S(1)} %dynamic-slice_add_fusion.refs_4_), channel_id=1, source_target_pairs={{0,16},{8,24},{16,0},{24,8},{1,17},{9,25},{17,1},{25,9},{2,18},{10... | collective-permute-start | bytes 786440 | tf_op jit(solution)/shard_map/ppermute | solution.py:291
  22.1 12.6 %collective-permute-start.6 = (f32[256,256]{1,0:T(8,128)S(1)}, f32[256,256]{1,0:T(8,128)}, u32[]{:S(2)}, u32[]{:S(2)}) collective-permute-start(f32[256,256]{1,0:T(8,128)S(1)} %dynamic-slice_add_fusion.refs_4_), channel_id=1, source_target_pairs={{0,24},{8,16},{16,8},{24,0},{1,25},{9,17},{17,9},{25,1},{2,26},{10... | collective-permute-start | bytes 786440 | tf_op jit(solution)/shard_map/ppermute | solution.py:291
  71.9 18.4 %collective-permute-start.10 = (f32[160,256]{1,0:T(8,128)S(1)}, f32[160,256]{1,0:T(8,128)S(1)}, u32[]{:S(2)}, u32[]{:S(2)}) collective-permute-start(f32[160,256]{1,0:T(8,128)S(1)} %get-tuple-element.60), channel_id=1, source_target_pairs={{0,6},{1,7},{2,4},{3,5},{4,2},{5,3},{6,0},{7,1},{8,14},{9,15},{10,... | collective-permute-start | bytes 491528 | tf_op jit(solution)/shard_map/ppermute | solution.py:291
  74.5 20.7 %collective-permute-start.8 = (f32[160,256]{1,0:T(8,128)S(1)}, f32[160,256]{1,0:T(8,128)S(1)}, u32[]{:S(2)}, u32[]{:S(2)}) collective-permute-start(f32[160,256]{1,0:T(8,128)S(1)} %get-tuple-element.59), channel_id=1, source_target_pairs={{0,2},{1,3},{2,0},{3,1},{4,6},{5,7},{6,4},{7,5},{8,10},{9,11},{10,... | collective-permute-start | bytes 491528 | tf_op jit(solution)/shard_map/ppermute | solution.py:291
  101.6 15.1 %collective-permute-start.12 = (f32[160,256]{1,0:T(8,128)S(1)}, f32[160,256]{1,0:T(8,128)S(1)}, u32[]{:S(2)}, u32[]{:S(2)}) collective-permute-start(f32[160,256]{1,0:T(8,128)S(1)} %fusion.3.refs_0_), channel_id=1, source_target_pairs={{0,4},{1,5},{2,6},{3,7},{4,0},{5,1},{6,2},{7,3},{8,12},{9,13},{10,... | collective-permute-start | bytes 491528 | tf_op jit(solution)/shard_map/ppermute | solution.py:291
  116.8 129.8 %collective-permute-start.33 = (bf16[1280,256]{1,0:T(8,128)(2,1)}, bf16[1280,256]{1,0:T(8,128)(2,1)S(1)}, u32[]{:S(2)}, u32[]{:S(2)}) collective-permute-start(bf16[1280,256]{1,0:T(8,128)(2,1)} %bitcast.4.refs_0_.refs_5_), channel_id=1, source_target_pairs={{0,1},{1,0},{2,3},{3,2},{4,5},{5,4},{6,7},{7,6},{8,9},{9,8},{10,11... | collective-permute-start | bytes 1966088 | tf_op jit(solution)/shard_map/ppermute | solution.py:291
  125.8 13.7 %collective-permute-start.19 = (f32[256,256]{1,0:T(8,128)S(1)}, f32[256,256]{1,0:T(8,128)S(1)}, u32[]{:S(2)}, u32[]{:S(2)}) collective-permute-start(f32[256,256]{1,0:T(8,128)S(1)} %get-tuple-element.35), channel_id=1, source_target_pairs={{0,24},{8,16},{16,8},{24,0},{1,25},{9,17},{17,9},{25,1},{2,26},{10... | collective-permute-start | bytes 786440 | tf_op jit(solution)/shard_map/ppermute | solution.py:291
  127.5 119.2 %collective-permute-start.40 = (bf16[128,3200]{1,0:T(8,128)(2,1)S(1)}, bf16[128,3200]{1,0:T(8,128)(2,1)}, u32[]{:S(2)}, u32[]{:S(2)}) collective-permute-start(bf16[128,3200]{1,0:T(8,128)(2,1)S(1)} %get-tuple-element.56), channel_id=1, source_target_pairs={{0,8},{8,0},{16,24},{24,16},{1,9},{9,1},{17,25},{25,17},{2,10},{10... | collective-permute-start | bytes 2457608 | tf_op jit(solution)/shard_map/ppermute | solution.py:291
  132.9 114.3 %collective-permute-start.42 = (bf16[128,3200]{1,0:T(8,128)(2,1)S(1)}, bf16[128,3200]{1,0:T(8,128)(2,1)}, u32[]{:S(2)}, u32[]{:S(2)}) collective-permute-start(bf16[128,3200]{1,0:T(8,128)(2,1)S(1)} %get-tuple-element.55), channel_id=1, source_target_pairs={{0,8},{8,0},{16,24},{24,16},{1,9},{9,1},{17,25},{25,17},{2,10},{10... | collective-permute-start | bytes 2457608 | tf_op jit(solution)/shard_map/ppermute | solution.py:291
  159.6 20.7 %collective-permute-start.25 = (f32[64,3200]{1,0:T(8,128)S(1)}, f32[64,3200]{1,0:T(8,128)S(1)}, u32[]{:S(2)}, u32[]{:S(2)}) collective-permute-start(f32[64,3200]{1,0:T(8,128)S(1)} %get-tuple-element.46), channel_id=1, source_target_pairs={{0,16},{8,24},{16,0},{24,8},{1,17},{9,25},{17,1},{25,9},{2,18},{10... | collective-permute-start | bytes 2457608 | tf_op jit(solution)/shard_map/ppermute | solution.py:291
  161.6 112.1 %collective-permute-start.46 = (bf16[256,3200]{1,0:T(8,128)(2,1)S(1)}, bf16[256,3200]{1,0:T(8,128)(2,1)S(1)}, u32[]{:S(2)}, u32[]{:S(2)}) collective-permute-start(bf16[256,3200]{1,0:T(8,128)(2,1)S(1)} %get-tuple-element.53.refs_5_), channel_id=1, source_target_pairs={{0,8},{8,0},{16,24},{24,16},{1,9},{9,1},{17,25},{25,17},{2,10},{10... | collective-permute-start | bytes 4915208 | tf_op jit(solution)/shard_map/ppermute | solution.py:291
  180.3 45.2 %collective-permute-start.21 = (f32[64,3200]{1,0:T(8,128)S(1)}, f32[64,3200]{1,0:T(8,128)S(1)}, u32[]{:S(2)}, u32[]{:S(2)}) collective-permute-start(f32[64,3200]{1,0:T(8,128)S(1)} %get-tuple-element.43), channel_id=1, source_target_pairs={{0,8},{8,0},{16,24},{24,16},{1,9},{9,1},{17,25},{25,17},{2,10},{10... | collective-permute-start | bytes 2457608 | tf_op jit(solution)/shard_map/ppermute | solution.py:291
  246.6 17.6 %collective-permute-start.34 = (bf16[1280,256]{1,0:T(8,128)(2,1)}, bf16[1280,256]{1,0:T(8,128)(2,1)S(1)}, u32[]{:S(2)}, u32[]{:S(2)}) collective-permute-start(bf16[1280,256]{1,0:T(8,128)(2,1)} %collective-permute-done.refs_1_.refs_6_), channel_id=1, source_target_pairs={{0,1},{1,0},{2,3},{3,2},{4,5},{5,4},{6,7},{7,6},{8,9},{9,8},{10,11... | collective-permute-start | bytes 1966088 | tf_op jit(solution)/shard_map/ppermute | solution.py:291
  246.7 19.1 %collective-permute-start.35 = (bf16[1280,256]{1,0:T(8,128)(2,1)}, bf16[1280,256]{1,0:T(8,128)(2,1)S(1)}, u32[]{:S(2)}, u32[]{:S(2)}) collective-permute-start(bf16[1280,256]{1,0:T(8,128)(2,1)} %collective-permute-done.1.refs_2_.refs_7_), channel_id=1, source_target_pairs={{0,1},{1,0},{2,3},{3,2},{4,5},{5,4},{6,7},{7,6},{8,9},{9,8},{10,11... | collective-permute-start | bytes 1966088 | tf_op jit(solution)/shard_map/ppermute | solution.py:291
  247.2 19.1 %collective-permute-start.36 = (bf16[1280,256]{1,0:T(8,128)(2,1)}, bf16[1280,256]{1,0:T(8,128)(2,1)S(1)}, u32[]{:S(2)}, u32[]{:S(2)}) collective-permute-start(bf16[1280,256]{1,0:T(8,128)(2,1)} %collective-permute-done.2.refs_3_.refs_8_), channel_id=1, source_target_pairs={{0,1},{1,0},{2,3},{3,2},{4,5},{5,4},{6,7},{7,6},{8,9},{9,8},{10,11... | collective-permute-start | bytes 1966088 | tf_op jit(solution)/shard_map/ppermute | solution.py:291
  264.2 61.2 %collective-permute-start.38 = (bf16[128,3200]{1,0:T(8,128)(2,1)S(1)}, bf16[128,3200]{1,0:T(8,128)(2,1)}, u32[]{:S(2)}, u32[]{:S(2)}) collective-permute-start(bf16[128,3200]{1,0:T(8,128)(2,1)S(1)} %get-tuple-element.58), channel_id=1, source_target_pairs={{0,16},{8,24},{16,0},{24,8},{1,17},{9,25},{17,1},{25,9},{2,18},{10... | collective-permute-start | bytes 2457608 | tf_op jit(solution)/shard_map/ppermute | solution.py:291
  265.8 60.2 %collective-permute-start.39 = (bf16[128,3200]{1,0:T(8,128)(2,1)S(1)}, bf16[128,3200]{1,0:T(8,128)(2,1)}, u32[]{:S(2)}, u32[]{:S(2)}) collective-permute-start(bf16[128,3200]{1,0:T(8,128)(2,1)S(1)} %get-tuple-element.57), channel_id=1, source_target_pairs={{0,16},{8,24},{16,0},{24,8},{1,17},{9,25},{17,1},{25,9},{2,18},{10... | collective-permute-start | bytes 2457608 | tf_op jit(solution)/shard_map/ppermute | solution.py:291
  266.3 61.2 %collective-permute-start.28 = (f32[64,3200]{1,0:T(8,128)S(1)}, f32[64,3200]{1,0:T(8,128)S(1)}, u32[]{:S(2)}, u32[]{:S(2)}) collective-permute-start(f32[64,3200]{1,0:T(8,128)S(1)} %pad_maximum_fusion.3), channel_id=1, source_target_pairs={{0,16},{8,24},{16,0},{24,8},{1,17},{9,25},{17,1},{25,9},{2,18},{10... | collective-permute-start | bytes 2457608 | tf_op jit(solution)/shard_map/ppermute | solution.py:291
  273.3 57.1 %collective-permute-start.24 = (f32[64,3200]{1,0:T(8,128)S(1)}, f32[64,3200]{1,0:T(8,128)S(1)}, u32[]{:S(2)}, u32[]{:S(2)}) collective-permute-start(f32[64,3200]{1,0:T(8,128)S(1)} %pad_maximum_fusion.2), channel_id=1, source_target_pairs={{0,8},{8,0},{16,24},{24,16},{1,9},{9,1},{17,25},{25,17},{2,10},{10... | collective-permute-start | bytes 2457608 | tf_op jit(solution)/shard_map/ppermute | solution.py:291
  273.7 49.4 %collective-permute-start.16 = (f32[256,256]{1,0:T(8,128)S(1)}, f32[256,256]{1,0:T(8,128)S(1)}, u32[]{:S(2)}, u32[]{:S(2)}) collective-permute-start(f32[256,256]{1,0:T(8,128)S(1)} %add.79), channel_id=1, source_target_pairs={{0,16},{8,24},{16,0},{24,8},{1,17},{9,25},{17,1},{25,9},{2,18},{10... | collective-permute-start | bytes 786440 | tf_op jit(solution)/shard_map/ppermute | solution.py:291
  323.2 68.4 %collective-permute-start.37 = (bf16[256,3200]{1,0:T(8,128)(2,1)}, bf16[256,3200]{1,0:T(8,128)(2,1)}, u32[]{:S(2)}, u32[]{:S(2)}) collective-permute-start(bf16[256,3200]{1,0:T(8,128)(2,1)} %get-tuple-element.54.refs_4_), channel_id=1, source_target_pairs={{0,16},{8,24},{16,0},{24,8},{1,17},{9,25},{17,1},{25,9},{2,18},{10... | collective-permute-start | bytes 4915208 | tf_op jit(solution)/shard_map/ppermute | solution.py:291
  325.4 54.3 %collective-permute-start.41 = (bf16[128,3200]{1,0:T(8,128)(2,1)}, bf16[128,3200]{1,0:T(8,128)(2,1)}, u32[]{:S(2)}, u32[]{:S(2)}) collective-permute-start(bf16[128,3200]{1,0:T(8,128)(2,1)} %collective-permute-done.40.refs_6_), channel_id=1, source_target_pairs={{0,16},{8,24},{16,0},{24,8},{1,17},{9,25},{17,1},{25,9},{2,18},{10... | collective-permute-start | bytes 2457608 | tf_op jit(solution)/shard_map/ppermute | solution.py:291
  325.9 65.7 %collective-permute-start.43 = (bf16[128,3200]{1,0:T(8,128)(2,1)}, bf16[128,3200]{1,0:T(8,128)(2,1)}, u32[]{:S(2)}, u32[]{:S(2)}) collective-permute-start(bf16[128,3200]{1,0:T(8,128)(2,1)} %collective-permute-done.42.refs_7_), channel_id=1, source_target_pairs={{0,16},{8,24},{16,0},{24,8},{1,17},{9,25},{17,1},{25,9},{2,18},{10... | collective-permute-start | bytes 2457608 | tf_op jit(solution)/shard_map/ppermute | solution.py:291
  328.4 63.2 %collective-permute-start.44 = (bf16[128,3200]{1,0:T(8,128)(2,1)}, bf16[128,3200]{1,0:T(8,128)(2,1)}, u32[]{:S(2)}, u32[]{:S(2)}) collective-permute-start(bf16[128,3200]{1,0:T(8,128)(2,1)} %collective-permute-done.38.refs_5_), channel_id=1, source_target_pairs={{0,8},{8,0},{16,24},{24,16},{1,9},{9,1},{17,25},{25,17},{2,10},{10... | collective-permute-start | bytes 2457608 | tf_op jit(solution)/shard_map/ppermute | solution.py:291
  331.3 60.3 %collective-permute-start.45 = (bf16[128,3200]{1,0:T(8,128)(2,1)}, bf16[128,3200]{1,0:T(8,128)(2,1)}, u32[]{:S(2)}, u32[]{:S(2)}) collective-permute-start(bf16[128,3200]{1,0:T(8,128)(2,1)} %collective-permute-done.39.refs_6_), channel_id=1, source_target_pairs={{0,8},{8,0},{16,24},{24,16},{1,9},{9,1},{17,25},{25,17},{2,10},{10... | collective-permute-start | bytes 2457608 | tf_op jit(solution)/shard_map/ppermute | solution.py:291
  379.7 31.7 %collective-permute-start.29 = (f32[8,256]{1,0:T(8,128)S(1)}, f32[8,256]{1,0:T(8,128)S(1)}, u32[]{:S(2)}, u32[]{:S(2)}) collective-permute-start(f32[8,256]{1,0:T(8,128)S(1)} %get-tuple-element.48), channel_id=1, source_target_pairs={{0,1},{1,0},{2,3},{3,2},{4,5},{5,4},{6,7},{7,6},{8,9},{9,8},{10,11... | collective-permute-start | bytes 24584 | tf_op jit(solution)/shard_map/ppermute | solution.py:291
  411.4 18.8 %collective-permute-start.30 = (f32[8,256]{1,0:T(8,128)S(1)}, f32[8,256]{1,0:T(8,128)S(1)}, u32[]{:S(2)}, u32[]{:S(2)}) collective-permute-start(f32[8,256]{1,0:T(8,128)S(1)} %add.90), channel_id=1, source_target_pairs={{0,2},{1,3},{2,0},{3,1},{4,6},{5,7},{6,4},{7,5},{8,10},{9,11},{10,... | collective-permute-start | bytes 24584 | tf_op jit(solution)/shard_map/ppermute | solution.py:291
  413.9 16.3 %collective-permute-start.31 = (f32[8,256]{1,0:T(8,128)S(1)}, f32[8,256]{1,0:T(8,128)S(1)}, u32[]{:S(2)}, u32[]{:S(2)}) collective-permute-start(f32[8,256]{1,0:T(8,128)S(1)} %add.90), channel_id=1, source_target_pairs={{0,4},{1,5},{2,6},{3,7},{4,0},{5,1},{6,2},{7,3},{8,12},{9,13},{10,... | collective-permute-start | bytes 24584 | tf_op jit(solution)/shard_map/ppermute | solution.py:291
  415.0 15.2 %collective-permute-start.32 = (f32[8,256]{1,0:T(8,128)S(1)}, f32[8,256]{1,0:T(8,128)S(1)}, u32[]{:S(2)}, u32[]{:S(2)}) collective-permute-start(f32[8,256]{1,0:T(8,128)S(1)} %add.90), channel_id=1, source_target_pairs={{0,6},{1,7},{2,4},{3,5},{4,2},{5,3},{6,0},{7,1},{8,14},{9,15},{10,... | collective-permute-start | bytes 24584 | tf_op jit(solution)/shard_map/ppermute | solution.py:291
  (37 other events, 348.5 us)

commit v4 on v3

--- a/solution.py
+++ b/solution.py
@@ -135,7 +135,7 @@
 
 
 def sketch_kernel(ids, part, *refs):
-    grads, rights, keep, send, big, low = refs[:4], refs[4:8], refs[8], refs[9], refs[10], refs[11]
+    grads, rights, keep, send, big, low = refs[:6], refs[6:10], refs[10], refs[11], refs[12], refs[13]
     z, core, shift = ids[1], ids[2], ids[3]
     for k in range(4):
         big[k], low[k] = split(rights[k][...])
@@ -144,8 +144,8 @@
         for b in range(4):
             at = pl.ds(pl.multiple_of(half * (4 * rows) + (z ^ b) * rows, 32), rows)
             total = part[at, :]
-            for k in range(4):
-                g = grads[k][at, :]
+            for k, grad in zip((0, 1, 3, 2, 2, 3), grads):
+                g = grad[at, :]
                 total += mm(g, big[k ^ shift], ((1,), (0,)))
                 total += mm(g, low[k ^ shift], ((1,), (0,)))
             out[b * rows : (b + 1) * rows, :] = total
@@ -225,14 +225,15 @@
         out[...] = send[...] + total[at + 2 * size : at + 4 * size, :]
 
 
-def gradient_kernel(numbers, ids, *refs):
+def gradient_kernel(numbers, cuts, ids, *refs):
     count = len(numbers) // 2
     own, other, pieces = refs[:count], refs[count : 2 * count], list(refs[2 * count : -2])
     base, out = refs[-2], refs[-1]
     total = base[...]
     for at, number in enumerate(numbers):
         x = jnp.concatenate([pieces.pop(0)[...] for _ in range(number)], axis=0)
-        grad = jnp.where(ids[2] == at % 2, own[at // 2][0], other[at // 2][0])
+        cut = cuts[at // 2]
+        grad = jnp.where(ids[2] == at % 2, own[at // 2][0, :, cut], other[at // 2][0, :, cut])
         total += mm(grad, x, ((1,), (0,)))
     out[...] = total
 
@@ -278,12 +279,15 @@
     factor_out[...] = right[...].T * scale
 
 
-def momentum_kernel(basis, right, base, out, small):
+def momentum_kernel(cut, ids, own, other, first, second, basis, right, base, out, small):
     @pl.when(pl.program_id(0) == 0)
     def _():
         small[...] = (basis[...] * -(1.0 - mix_rate)).astype(bf16)
 
-    out[...] = base[...] + mm(small[...], right[...].astype(bf16), ((1,), (0,)))
+    mine, its = own[0, :, cut], other[0, :, cut]
+    total = base[...] + mm(jnp.where(ids[2] == 0, mine, its), first[...], ((1,), (0,)))
+    total += mm(jnp.where(ids[2] == 0, its, mine), second[...], ((1,), (0,)))
+    out[...] = total + mm(small[...], right[...].astype(bf16), ((1,), (0,)))
 
 
 def swap(x, axis, bit):
@@ -293,6 +297,11 @@
 
 def plane(n_total, m_total, inputs, out_grads, weights, momentum, right_factor):
     return plane_body(n_total, m_total, inputs, out_grads, weights, momentum, right_factor)
+
+
+def line(x, inner):
+    steps = ((1, 2), (2, 1)) if inner else ((1, 0), (2, 3))
+    return lax.ppermute(x, "col", [(2 * a + h, 2 * b + h) for a, b in steps for h in range(2)])
 
 
 def swaps(x, axis, unit):
@@ -321,7 +330,12 @@
         return pl.BlockSpec((1, m, block), lambda i, ids: (ids[3] ^ j, 0, 0))
 
     grads = out_grads.T
-    own = [grads] + swaps(grads, "col", 2)
+    near = swap(grads, "col", 2)
+    inner1 = line(grads, True)
+    inner2 = line(near, True)
+    outer1 = line(inner1, False)
+    outer2 = line(inner2, False)
+    own = [grads, near, inner2 + outer1, inner1 + outer2]
 
     in_right = mm(inputs.astype(f32), right_factor, ((1,), (0,)), high)
     keep = lax.dynamic_slice_in_dim(in_right, core * block, block, 0)
@@ -341,8 +355,8 @@
 
     part = mm(momentum, right_factor, ((1,), (0,)), high)
     keep, send = call(
-        sketch_kernel, (shaped((m // 2, rank)),) * 2, (ids, part, *own, *rights),
-        [whole_smem] + [whole_vmem] * 9, (whole_vmem,) * 2,
+        sketch_kernel, (shaped((m // 2, rank)),) * 2, (ids, part, grads, near, inner1, inner2, outer1, outer2, *rights),
+        [whole_smem] + [whole_vmem] * 11, (whole_vmem,) * 2,
         scratch=[pltpu.VMEM((4, block, rank), bf16)] * 2, flops=4 * m * 4 * block * rank, moved=8_000_000)
     mine = keep + swap(send, "col", 1)
     size = m // 8
@@ -389,16 +403,18 @@
 
     inverse = inverse_factor(gram)
 
-    def gradient(picks, numbers, pieces, base):
+    every, early, late = slice(None), slice(0, quarter), slice(quarter, 2 * quarter)
+
+    def gradient(picks, numbers, cuts, pieces, base):
         return call(
-            functools.partial(gradient_kernel, numbers), shaped((m, n)),
+            functools.partial(gradient_kernel, numbers, cuts), shaped((m, n)),
             (ids, *([own_all] * len(picks)), *([other_all] * len(picks)), *pieces, base),
             [pick(j) for j in picks] * 2 + [columns(x.shape[0]) for x in pieces] + [columns(m)], columns(m), tiles,
             flops=2 * m * n * sum(x.shape[0] for x in pieces), moved=8 * m * n, prefetch=1)
 
-    moment = gradient((0, 1), (1, 1, 2, 1), (half0, half1, x0, x1, x23), momentum)
+    moment = gradient((0, 1), (1, 1, 2, 1), (every, every), (half0, half1, x0, x1, x23), momentum)
     moment = gradient(
-        (2, 3), (1, 2, 2, 2), (y01, y2, y3, first_by_y, second_by_y, first_by_x, second_by_x), moment)
+        (2, 3), (1, 2, 1, 1), (every, early), (y01, y2, y3, first_by_y, first_by_x), moment)
 
     right, squares, basis = call(
         functools.partial(right_kernel, n), (shaped((rank, n)), shaped((8, rank)), shaped((m, rank))),
@@ -416,9 +432,11 @@
         (columns(m), pl.BlockSpec((tn, rank), lambda i, *_: (i, 0))), tiles,
         scratch=[pltpu.VMEM((m, rank), bf16)] * 2, flops=6 * m * n * rank, moved=6 * m * n)
     momentum_new = call(
-        momentum_kernel, shaped((m, n)), (basis, right, moment), [fixed(m, rank), columns(rank), columns(m)],
+        functools.partial(momentum_kernel, late), shaped((m, n)),
+        (ids, own_all, other_all, second_by_y, second_by_x, basis, right, moment),
+        [pick(3), pick(3), columns(quarter), columns(quarter), fixed(m, rank), columns(rank), columns(m)],
         columns(m), tiles, scratch=[pltpu.VMEM((m, rank), bf16)],
-        flops=2 * m * n * rank, moved=8 * m * n, aliases={2: 0})
+        flops=2 * m * n * (tokens // 2 + rank), moved=8 * m * n, prefetch=1, aliases={7: 0})
     return (weights_new, momentum_new, factor_new)
 
 

time: 446 us -> 433 us (0.971)
  waiting for transfers between devices: 227 us -> 211 us
    ppermute x47 -> x45, waiting for transfers between devices: 227 us -> 191 us  [swap(): return lax.ppermute(x, axis, [(i, i ^ bit) for i in range(size)])]
    ppermute x0 -> x4, waiting for transfers between devices: none -> 19.5 us  [line(): lax.ppermute(x, 'col', [(2 * a + h, 2 * b + h) for a, b in steps for h in...]
    ppermute x47 -> x45, starting transfers between devices: 61.6 us -> 54.2 us  [swap(): return lax.ppermute(x, axis, [(i, i ^ bit) for i in range(size)])]
    ppermute x0 -> x4, starting transfers between devices: none -> 5.76 us  [line(): lax.ppermute(x, 'col', [(2 * a + h, 2 * b + h) for a, b in steps for h in...]
  transfers between devices with their start and end apart: 47 -> 49, of which waited for: 22 -> 21; matrix products, arithmetic and copies ran while one was open for 4% -> 6% of each run, Pallas kernels for 22% -> 23%
where the time goes in v4:
time: 433 us; the launch traced here: 432 us
  waiting for transfers between devices  211 us (49%)
  Pallas kernels  118 us (27%)
  starting transfers between devices  60 us (14%)
  local copies, waits for them, and re-layouts  19.1 us (4%)
  matrix products  15.8 us (4%)
  other arithmetic  7.32 us (2%)
    ppermute x45, waiting for transfers between devices, swap(): return lax.ppermute(x, axis, [(i, i ^ bit) for i in range(size)])  191 us
    pallas_call x9, Pallas kernels, call(): pl.pallas_call(kernel, out_shape=outs, grid_spec=pltpu.PrefetchScalarGrid...  104 us
    ppermute x45, starting transfers between devices, swap(): return lax.ppermute(x, axis, [(i, i ^ bit) for i in range(size)])  54.2 us
    ppermute x4, waiting for transfers between devices, line(): lax.ppermute(x, 'col', [(2 * a + h, 2 * b + h) for a, b in steps for h in...  19.5 us
    unnamed x45, local copies, waits for them, and re-layouts  16.5 us
    dot_general x2, matrix products, mm(): lax.dot_general(a, b, (dims, ((), ())), precision=precision, preferred_el...  15.8 us
    pallas_call x1, Pallas kernels, inverse_factor(): pl.pallas_call(inverse_kernel, out_shape=jax.ShapeDtypeStruct(gram.shape,...  13.6 us
  transfers between devices with their start and end apart: 49, of which 21 were waited for; matrix products, arithmetic and copies ran while one was open for 6% of the time, Pallas kernels for 23%

profile of v4, /device:TPU:0, one launch (start us, length us, event | category | flops | bytes accessed | tf_op | source)
XLA Modules:
  0.0 431.9 jit_solution(14955835812802502513)
XLA Ops:
  7.5 13.5 %collective-permute-done.refs_1_.refs_6_ = bf16[1280,256]{1,0:T(8,128)(2,1)} collective-permute-done((bf16[1280,256]{1,0:T(8,128)(2,1)}, bf16[1280,256]{1,0:T(8,128)(2,1)}, u32[]{:S(2)}, u32[]{:S(2)}) %collective-permute-start) | collective-permute-done | bytes 655392 | tf_op jit(solution)/shard_map/ppermute | solution.py:295
  22.6 4.6 %fusion.8 = f32[512,256]{1,0:T(8,128)} fusion(bf16[512,3200]{1,0:T(8,128)(2,1)} %inputs.1, f32[3200,256]{1,0:T(8,128)S(1)} %copy-done), kind=kOutput, calls=%fused_computation.23 | convolution fusion | flops 2516582400 | bytes 7077888 | tf_op jit(solution)/shard_map/dot_general | solution.py:22
  37.3 11.2 %fusion.7.part = f32[1280,256]{1,0:T(8,128)} fusion(f32[1280,3200]{1,0:T(8,128)} %refs_9_.1, f32[3200,256]{1,0:T(8,128)S(1)} %copy-done), kind=kOutput, calls=%fused_computation.22 | convolution fusion | flops 6291456000 | bytes 20971520 | tf_op jit(solution)/shard_map/dot_general | solution.py:22
  48.6 6.9 %collective-permute-done.3.refs_4_ = bf16[1280,256]{1,0:T(8,128)(2,1)} collective-permute-done((bf16[1280,256]{1,0:T(8,128)(2,1)}, bf16[1280,256]{1,0:T(8,128)(2,1)}, u32[]{:S(2)}, u32[]{:S(2)}) %collective-permute-start.3) | collective-permute-done | bytes 655392 | tf_op jit(solution)/shard_map/ppermute | solution.py:304
  55.4 12.7 %collective-permute-done.4.refs_5_ = bf16[1280,256]{1,0:T(8,128)(2,1)} collective-permute-done((bf16[1280,256]{1,0:T(8,128)(2,1)}, bf16[1280,256]{1,0:T(8,128)(2,1)}, u32[]{:S(2)}, u32[]{:S(2)}) %collective-permute-start.4) | collective-permute-done | bytes 655392 | tf_op jit(solution)/shard_map/ppermute | solution.py:304
  69.4 4.7 %shard_map.76 = (f32[640,256]{1,0:T(8,128)S(1)}, f32[640,256]{1,0:T(8,128)S(1)}) custom-call(s32[4]{0:T(128)S(1)} %pad_add_fusion.ids, f32[1280,256]{1,0:T(8,128)S(1)} %copy-done.5, bf16[1280,256]{1,0:T(8,128)(2,1)} %bitcast.4.refs_0_.refs_5_, bf16[1280,256]{1,0:T(8,128)(2,1)} %collective-permute-done.refs_1_.refs_6_, ...), custom_call_target="tpu_custom_call" | custom-call | flops 1342177280 | bytes 8000000 | tf_op jit(solution)/shard_map/pallas_call | solution.py:121
  80.9 4.8 %collective-permute-done.10 = f32[160,256]{1,0:T(8,128)S(1)} collective-permute-done((f32[160,256]{1,0:T(8,128)S(1)}, f32[160,256]{1,0:T(8,128)S(1)}, u32[]{:S(2)}, u32[]{:S(2)}) %collective-permute-start.10) | collective-permute-done | bytes 163872 | tf_op jit(solution)/shard_map/ppermute | solution.py:295
  85.7 5.9 %collective-permute-done.11 = f32[160,256]{1,0:T(8,128)S(1)} collective-permute-done((f32[160,256]{1,0:T(8,128)S(1)}, f32[160,256]{1,0:T(8,128)S(1)}, u32[]{:S(2)}, u32[]{:S(2)}) %collective-permute-start.11) | collective-permute-done | bytes 163872 | tf_op jit(solution)/shard_map/ppermute | solution.py:295
  91.6 3.3 collective-permute-start.13
  97.4 3.3 collective-permute-done.13.refs_1_
  100.7 9.1 %collective-permute-done.14.refs_2_ = f32[160,256]{1,0:T(8,128)S(1)} collective-permute-done((f32[160,256]{1,0:T(8,128)S(1)}, f32[160,256]{1,0:T(8,128)S(1)}, u32[]{:S(2)}, u32[]{:S(2)}) %collective-permute-start.14) | collective-permute-done | bytes 163872 | tf_op jit(solution)/shard_map/ppermute | solution.py:295
  113.3 4.6 %shard_map.77 = (f32[1280,256]{1,0:T(8,128)S(1)}, f32[256,256]{1,0:T(8,128)S(1)}, f32[256,256]{1,0:T(8,128)S(1)}, f32[256,256]{1,0:T(8,128)S(1)}, f32[256,256]{1...) custom-call(s32[4]{0:T(128)S(1)} %pad_add_fusion.ids, ...), custom_call_target="tpu_custom_call" | custom-call | flops 1677721600 | bytes 8000000 | tf_op jit(solution)/shard_map/pallas_call | solution.py:121
  123.3 3.9 collective-permute-done.19
  128.6 3.8 collective-permute-done.20
  133.9 12.4 %shard_map.79 = (f32[64,3200]{1,0:T(8,128)S(1)}, f32[64,3200]{1,0:T(8,128)S(1)}, f32[64,3200]{1,0:T(8,128)S(1)}, f32[64,3200]{1,0:T(8,128)S(1)}) custom-call(bf16[256,1280]{1,0:T(8,128)(2,1)S(1)} %get-tuple-element.36.big_t, bf16[256,1280]{1,0:T(8,128)(2,1)S(1)} %get-tuple-element.37.low_t, f32[1280,3200]{1,0:T(8,128)} %refs_9_.1), custom_call_target="tpu_custom_call" | custom-call | flops 6291456000 | bytes 20480000 | tf_op jit(solution)/shard_map/pallas_call | solution.py:121
  146.3 7.6 %shard_map.80 = (f32[32,3200]{1,0:T(8,128)S(1)}, f32[32,3200]{1,0:T(8,128)S(1)}, f32[64,3200]{1,0:T(8,128)S(1)}, f32[32,3200]{1,0:T(8,128)S(1)}, f32[32,3200]{1,0:T(8,128)S(1)}, /*index=5*/f32[64,3200]{1,0:T(8,128)S(1)}) custom-call(s32[4]{0:T(128)S(1)} %pad_add_fusion.ids, f32[256,256]{1,0:T(8,128)S(1)} %add_add_fusion.own, ...), custom_call_target="tpu_custom_call" | custom-call | flops 1677721600 | bytes 8192000 | tf_op jit(solution)/shard_map/pallas_call | solution.py:121
  158.9 15.6 %collective-permute-done.27 = f32[64,3200]{1,0:T(8,128)S(1)} collective-permute-done((f32[64,3200]{1,0:T(8,128)S(1)}, f32[64,3200]{1,0:T(8,128)S(1)}, u32[]{:S(2)}, u32[]{:S(2)}) %collective-permute-start.27) | collective-permute-done | bytes 819232 | tf_op jit(solution)/shard_map/ppermute | solution.py:295
  176.1 43.6 %collective-permute-done.23 = f32[64,3200]{1,0:T(8,128)S(1)} collective-permute-done((f32[64,3200]{1,0:T(8,128)S(1)}, f32[64,3200]{1,0:T(8,128)S(1)}, u32[]{:S(2)}, u32[]{:S(2)}) %collective-permute-start.23) | collective-permute-done | bytes 819232 | tf_op jit(solution)/shard_map/ppermute | solution.py:295
  221.2 9.1 %collective-permute-done.28 = f32[32,3200]{1,0:T(8,128)S(1)} collective-permute-done((f32[32,3200]{1,0:T(8,128)S(1)}, f32[32,3200]{1,0:T(8,128)S(1)}, u32[]{:S(2)}, u32[]{:S(2)}) %collective-permute-start.28) | collective-permute-done | bytes 409632 | tf_op jit(solution)/shard_map/ppermute | solution.py:295
  231.9 8.1 %collective-permute-done.24 = f32[32,3200]{1,0:T(8,128)S(1)} collective-permute-done((f32[32,3200]{1,0:T(8,128)S(1)}, f32[32,3200]{1,0:T(8,128)S(1)}, u32[]{:S(2)}, u32[]{:S(2)}) %collective-permute-start.24) | collective-permute-done | bytes 409632 | tf_op jit(solution)/shard_map/ppermute | solution.py:295
  242.3 6.6 %collective-permute-done.29.refs_4_ = f32[32,3200]{1,0:T(8,128)S(1)} collective-permute-done((f32[32,3200]{1,0:T(8,128)S(1)}, f32[32,3200]{1,0:T(8,128)S(1)}, u32[]{:S(2)}, u32[]{:S(2)}) %collective-permute-start.29) | collective-permute-done | bytes 409632 | tf_op jit(solution)/shard_map/ppermute | solution.py:295
  250.5 6.7 %collective-permute-done.25.refs_1_ = f32[32,3200]{1,0:T(8,128)S(1)} collective-permute-done((f32[32,3200]{1,0:T(8,128)S(1)}, f32[32,3200]{1,0:T(8,128)S(1)}, u32[]{:S(2)}, u32[]{:S(2)}) %collective-permute-start.25) | collective-permute-done | bytes 409632 | tf_op jit(solution)/shard_map/ppermute | solution.py:295
  263.2 3.6 collective-permute-done.17
  270.7 18.6 %shard_map.83.refs_9_ = f32[1280,3200]{1,0:T(8,128)} custom-call(s32[4]{0:T(128)S(1)} %pad_add_fusion.ids, bf16[4,1280,256]{2,1,0:T(8,128)(2,1)S(1)} %pad_maximum_fusion.refs_0_.refs_1_.own, bf16[4,1280,256]{2,1,0:T(8,128)(2,1)S(1)} %pad_maximum_fusion.refs_0_.refs_1_.own, bf16[4,1280,256]{2,1,0:T(8,128)(2,1)S(1)} %pad_maximum_fusion.1.refs_2_.refs_3_.other, ...), custom_call_target="tpu_custom_call" | custom-call | flops 8388608000 | bytes 32768000 | tf_op jit(solution)/shard_map/pallas_call | solution.py:121
  289.3 29.4 %collective-permute-done.18 = f32[256,256]{1,0:T(8,128)S(1)} collective-permute-done((f32[256,256]{1,0:T(8,128)S(1)}, f32[256,256]{1,0:T(8,128)S(1)}, u32[]{:S(2)}, u32[]{:S(2)}) %collective-permute-start.18) | collective-permute-done | bytes 262176 | tf_op jit(solution)/shard_map/ppermute | solution.py:295
  326.7 13.6 %shard_map.78.inverse = f32[256,256]{1,0:T(8,128)} custom-call(f32[256,256]{1,0:T(8,128)} %add.88.gram_ref), custom_call_target="tpu_custom_call" | custom-call | flops 20000000000 | bytes 10000000 | tf_op jit(solution)/shard_map/pallas_call | solution.py:95
  348.0 7.9 %shard_map.81 = (f32[256,3200]{1,0:T(8,128)S(1)}, f32[8,256]{1,0:T(8,128)S(1)}, f32[1280,256]{1,0:T(8,128)S(1)}) custom-call(s32[4]{0:T(128)S(1)} %pad_add_fusion.ids, f32[256,256]{1,0:T(8,128)S(1)} %copy-done.20, f32[1280,256]{1,0:T(8,128)S(1)} %copy-done.15, f32[32,3200]{1,0:T(8,128)S(1)} %copy-done.9, f32[32,3200]{1,0:T(8,128)S(1)} %copy-done.13, ...), custom_call_target="tpu_custom_call" | custom-call | flops 1258291200 | bytes 9830400 | tf_op jit(solution)/shard_map/pallas_call | solution.py:121
  355.9 19.3 %collective-permute-done.46.refs_7_ = bf16[128,3200]{1,0:T(8,128)(2,1)} collective-permute-done((bf16[128,3200]{1,0:T(8,128)(2,1)}, bf16[128,3200]{1,0:T(8,128)(2,1)}, u32[]{:S(2)}, u32[]{:S(2)}) %collective-permute-start.46) | collective-permute-done | bytes 819232 | tf_op jit(solution)/shard_map/ppermute | solution.py:295
  375.2 19.4 %shard_map.84.base = f32[1280,3200]{1,0:T(8,128)} custom-call(s32[4]{0:T(128)S(1)} %pad_add_fusion.ids, bf16[4,1280,256]{2,1,0:T(8,128)(2,1)S(1)} %pad_maximum_fusion.refs_0_.refs_1_.own, bf16[4,1280,256]{2,1,0:T(8,128)(2,1)S(1)} %pad_maximum_fusion.refs_0_.refs_1_.own, bf16[4,1280,256]{2,1,0:T(8,128)(2,1)S(1)} %copy-done.3, ...), custom_call_target="tpu_custom_call" | custom-call | flops 6291456000 | bytes 32768000 | tf_op jit(solution)/shard_map/pallas_call | solution.py:121
  399.6 17.4 %shard_map.85 = f32[1280,3200]{1,0:T(8,128)} custom-call(s32[4]{0:T(128)S(1)} %pad_add_fusion.ids, bf16[4,1280,256]{2,1,0:T(8,128)(2,1)S(1)} %pad_maximum_fusion.refs_0_.refs_1_.own, bf16[4,1280,256]{2,1,0:T(8,128)(2,1)S(1)} %copy-done.3, bf16[128,3200]{1,0:T(8,128)(2,1)} %collective-permute-done.40.first, ...), custom_call_target="tpu_custom_call", output_to_operand_aliasing={{}: (7, {})} | custom-call | flops 4194304000 | bytes 32768000 | tf_op jit(solution)/shard_map/pallas_call | solution.py:121
  417.0 3.3 copy-done.21
  420.3 11.5 %shard_map.82 = (f32[1280,3200]{1,0:T(8,128)}, f32[3200,256]{1,0:T(8,128)}) custom-call(f32[8,256]{1,0:T(8,128)S(1)} %add_add_fusion.1.squares, f32[1280,256]{1,0:T(8,128)S(1)} %get-tuple-element.49.basis, f32[256,3200]{1,0:T(8,128)S(1)} %get-tuple-element.50.right, bf16[1280,3200]{1,0:T(8,128)(2,1)S(1)} %copy-done.21), custom_call_target="tpu_custom_call" | custom-call | flops 6291456000 | bytes 24576000 | tf_op jit(solution)/shard_map/pallas_call | solution.py:121
  (147 shorter events, 84.9 us)
Async XLA Ops:
  3.0 18.1 %collective-permute-start = (bf16[1280,256]{1,0:T(8,128)(2,1)}, bf16[1280,256]{1,0:T(8,128)(2,1)}, u32[]{:S(2)}, u32[]{:S(2)}) collective-permute-start(bf16[1280,256]{1,0:T(8,128)(2,1)} %bitcast.4.refs_0_.refs_5_), channel_id=1, source_target_pairs={{0,2},{1,3},{2,0},{3,1},{4,6},{5,7},{6,4},{7,5},{8,10},{9,11},{10,... | collective-permute-start | bytes 1966088 | tf_op jit(solution)/shard_map/ppermute | solution.py:295
  6.0 28.5 %collective-permute-start.1 = (bf16[1280,256]{1,0:T(8,128)(2,1)}, bf16[1280,256]{1,0:T(8,128)(2,1)}, u32[]{:S(2)}, u32[]{:S(2)}) collective-permute-start(bf16[1280,256]{1,0:T(8,128)(2,1)} %bitcast.4.refs_0_.refs_5_), channel_id=1, source_target_pairs={{2,4},{3,5},{4,2},{5,3},{10,12},{11,13},{12,10},{13,11},{18,20},{1... | collective-permute-start | bytes 1966088 | tf_op jit(solution)/shard_map/ppermute | solution.py:304
  21.1 14.8 %collective-permute-start.2 = (bf16[1280,256]{1,0:T(8,128)(2,1)}, bf16[1280,256]{1,0:T(8,128)(2,1)}, u32[]{:S(2)}, u32[]{:S(2)}) collective-permute-start(bf16[1280,256]{1,0:T(8,128)(2,1)} %collective-permute-done.refs_1_.refs_6_), channel_id=1, source_target_pairs={{2,4},{3,5},{4,2},{5,3},{10,12},{11,13},{12,10},{13,11},{18,20},{1... | collective-permute-start | bytes 1966088 | tf_op jit(solution)/shard_map/ppermute | solution.py:304
  31.0 17.6 %collective-permute-start.6 = (f32[256,256]{1,0:T(8,128)S(1)}, f32[256,256]{1,0:T(8,128)}, u32[]{:S(2)}, u32[]{:S(2)}) collective-permute-start(f32[256,256]{1,0:T(8,128)S(1)} %dynamic-slice_add_fusion.refs_6_), channel_id=1, source_target_pairs={{0,8},{8,0},{16,24},{24,16},{1,9},{9,1},{17,25},{25,17},{2,10},{10... | collective-permute-start | bytes 786440 | tf_op jit(solution)/shard_map/ppermute | solution.py:295
  32.7 15.9 %collective-permute-start.7 = (f32[256,256]{1,0:T(8,128)S(1)}, f32[256,256]{1,0:T(8,128)}, u32[]{:S(2)}, u32[]{:S(2)}) collective-permute-start(f32[256,256]{1,0:T(8,128)S(1)} %dynamic-slice_add_fusion.refs_6_), channel_id=1, source_target_pairs={{0,16},{8,24},{16,0},{24,8},{1,17},{9,25},{17,1},{25,9},{2,18},{10... | collective-permute-start | bytes 786440 | tf_op jit(solution)/shard_map/ppermute | solution.py:295
  34.5 20.9 %collective-permute-start.3 = (bf16[1280,256]{1,0:T(8,128)(2,1)}, bf16[1280,256]{1,0:T(8,128)(2,1)}, u32[]{:S(2)}, u32[]{:S(2)}) collective-permute-start(bf16[1280,256]{1,0:T(8,128)(2,1)} %collective-permute-done.1.refs_2_), channel_id=1, source_target_pairs={{2,0},{3,1},{4,6},{5,7},{10,8},{11,9},{12,14},{13,15},{18,16},{19,... | collective-permute-start | bytes 1966088 | tf_op jit(solution)/shard_map/ppermute | solution.py:304
  35.8 32.3 %collective-permute-start.4 = (bf16[1280,256]{1,0:T(8,128)(2,1)}, bf16[1280,256]{1,0:T(8,128)(2,1)}, u32[]{:S(2)}, u32[]{:S(2)}) collective-permute-start(bf16[1280,256]{1,0:T(8,128)(2,1)} %collective-permute-done.2.refs_3_), channel_id=1, source_target_pairs={{2,0},{3,1},{4,6},{5,7},{10,8},{11,9},{12,14},{13,15},{18,16},{19,... | collective-permute-start | bytes 1966088 | tf_op jit(solution)/shard_map/ppermute | solution.py:304
  76.5 15.1 %collective-permute-start.11 = (f32[160,256]{1,0:T(8,128)S(1)}, f32[160,256]{1,0:T(8,128)S(1)}, u32[]{:S(2)}, u32[]{:S(2)}) collective-permute-start(f32[160,256]{1,0:T(8,128)S(1)} %get-tuple-element.61), channel_id=1, source_target_pairs={{0,4},{1,5},{2,6},{3,7},{4,0},{5,1},{6,2},{7,3},{8,12},{9,13},{10,... | collective-permute-start | bytes 491528 | tf_op jit(solution)/shard_map/ppermute | solution.py:295
  94.9 14.8 %collective-permute-start.14 = (f32[160,256]{1,0:T(8,128)S(1)}, f32[160,256]{1,0:T(8,128)S(1)}, u32[]{:S(2)}, u32[]{:S(2)}) collective-permute-start(f32[160,256]{1,0:T(8,128)S(1)} %fusion.3.refs_0_), channel_id=1, source_target_pairs={{0,4},{1,5},{2,6},{3,7},{4,0},{5,1},{6,2},{7,3},{8,12},{9,13},{10,... | collective-permute-start | bytes 491528 | tf_op jit(solution)/shard_map/ppermute | solution.py:295
  109.9 131.7 %collective-permute-start.35 = (bf16[1280,256]{1,0:T(8,128)(2,1)}, bf16[1280,256]{1,0:T(8,128)(2,1)S(1)}, u32[]{:S(2)}, u32[]{:S(2)}) collective-permute-start(bf16[1280,256]{1,0:T(8,128)(2,1)} %bitcast.4.refs_0_.refs_5_), channel_id=1, source_target_pairs={{0,1},{1,0},{2,3},{3,2},{4,5},{5,4},{6,7},{7,6},{8,9},{9,8},{10,11... | collective-permute-start | bytes 1966088 | tf_op jit(solution)/shard_map/ppermute | solution.py:295
  121.7 120.0 %collective-permute-start.39 = (bf16[128,3200]{1,0:T(8,128)(2,1)S(1)}, bf16[128,3200]{1,0:T(8,128)(2,1)}, u32[]{:S(2)}, u32[]{:S(2)}) collective-permute-start(bf16[128,3200]{1,0:T(8,128)(2,1)S(1)} %get-tuple-element.58), channel_id=1, source_target_pairs={{0,8},{8,0},{16,24},{24,16},{1,9},{9,1},{17,25},{25,17},{2,10},{10... | collective-permute-start | bytes 2457608 | tf_op jit(solution)/shard_map/ppermute | solution.py:295
  127.1 115.0 %collective-permute-start.45 = (bf16[128,3200]{1,0:T(8,128)(2,1)S(1)}, bf16[128,3200]{1,0:T(8,128)(2,1)}, u32[]{:S(2)}, u32[]{:S(2)}) collective-permute-start(bf16[128,3200]{1,0:T(8,128)(2,1)S(1)} %get-tuple-element.55), channel_id=1, source_target_pairs={{0,8},{8,0},{16,24},{24,16},{1,9},{9,1},{17,25},{25,17},{2,10},{10... | collective-permute-start | bytes 2457608 | tf_op jit(solution)/shard_map/ppermute | solution.py:295
  153.9 20.7 %collective-permute-start.27 = (f32[64,3200]{1,0:T(8,128)S(1)}, f32[64,3200]{1,0:T(8,128)S(1)}, u32[]{:S(2)}, u32[]{:S(2)}) collective-permute-start(f32[64,3200]{1,0:T(8,128)S(1)} %get-tuple-element.46), channel_id=1, source_target_pairs={{0,16},{8,24},{16,0},{24,8},{1,17},{9,25},{17,1},{25,9},{2,18},{10... | collective-permute-start | bytes 2457608 | tf_op jit(solution)/shard_map/ppermute | solution.py:295
  156.2 113.0 %collective-permute-start.48 = (bf16[256,3200]{1,0:T(8,128)(2,1)S(1)}, bf16[256,3200]{1,0:T(8,128)(2,1)S(1)}, u32[]{:S(2)}, u32[]{:S(2)}) collective-permute-start(bf16[256,3200]{1,0:T(8,128)(2,1)S(1)} %get-tuple-element.53.refs_5_), channel_id=1, source_target_pairs={{0,8},{8,0},{16,24},{24,16},{1,9},{9,1},{17,25},{25,17},{2,10},{10... | collective-permute-start | bytes 4915208 | tf_op jit(solution)/shard_map/ppermute | solution.py:295
  174.6 45.1 %collective-permute-start.23 = (f32[64,3200]{1,0:T(8,128)S(1)}, f32[64,3200]{1,0:T(8,128)S(1)}, u32[]{:S(2)}, u32[]{:S(2)}) collective-permute-start(f32[64,3200]{1,0:T(8,128)S(1)} %get-tuple-element.43), channel_id=1, source_target_pairs={{0,8},{8,0},{16,24},{24,16},{1,9},{9,1},{17,25},{25,17},{2,10},{10... | collective-permute-start | bytes 2457608 | tf_op jit(solution)/shard_map/ppermute | solution.py:295
  241.6 18.1 %collective-permute-start.36 = (bf16[1280,256]{1,0:T(8,128)(2,1)}, bf16[1280,256]{1,0:T(8,128)(2,1)S(1)}, u32[]{:S(2)}, u32[]{:S(2)}) collective-permute-start(bf16[1280,256]{1,0:T(8,128)(2,1)} %collective-permute-done.refs_1_.refs_6_), channel_id=1, source_target_pairs={{0,1},{1,0},{2,3},{3,2},{4,5},{5,4},{6,7},{7,6},{8,9},{9,8},{10,11... | collective-permute-start | bytes 1966088 | tf_op jit(solution)/shard_map/ppermute | solution.py:295
  241.7 19.5 %collective-permute-start.37 = (bf16[1280,256]{1,0:T(8,128)(2,1)S(1)}, bf16[1280,256]{1,0:T(8,128)(2,1)S(1)}, u32[]{:S(2)}, u32[]{:S(2)}) collective-permute-start(bf16[1280,256]{1,0:T(8,128)(2,1)S(1)} %add.85.refs_7_), channel_id=1, source_target_pairs={{0,1},{1,0},{2,3},{3,2},{4,5},{5,4},{6,7},{7,6},{8,9},{9,8},{10,11... | collective-permute-start | bytes 1966088 | tf_op jit(solution)/shard_map/ppermute | solution.py:295
  242.2 19.6 %collective-permute-start.38 = (bf16[1280,256]{1,0:T(8,128)(2,1)S(1)}, bf16[1280,256]{1,0:T(8,128)(2,1)S(1)}, u32[]{:S(2)}, u32[]{:S(2)}) collective-permute-start(bf16[1280,256]{1,0:T(8,128)(2,1)S(1)} %add.86.refs_8_), channel_id=1, source_target_pairs={{0,1},{1,0},{2,3},{3,2},{4,5},{5,4},{6,7},{7,6},{8,9},{9,8},{10,11... | collective-permute-start | bytes 1966088 | tf_op jit(solution)/shard_map/ppermute | solution.py:295
  259.7 61.2 %collective-permute-start.44 = (bf16[128,3200]{1,0:T(8,128)(2,1)S(1)}, bf16[128,3200]{1,0:T(8,128)(2,1)}, u32[]{:S(2)}, u32[]{:S(2)}) collective-permute-start(bf16[128,3200]{1,0:T(8,128)(2,1)S(1)} %get-tuple-element.56), channel_id=1, source_target_pairs={{0,16},{8,24},{16,0},{24,8},{1,17},{9,25},{17,1},{25,9},{2,18},{10... | collective-permute-start | bytes 2457608 | tf_op jit(solution)/shard_map/ppermute | solution.py:295
  261.2 60.3 %collective-permute-start.41 = (bf16[128,3200]{1,0:T(8,128)(2,1)S(1)}, bf16[128,3200]{1,0:T(8,128)(2,1)}, u32[]{:S(2)}, u32[]{:S(2)}) collective-permute-start(bf16[128,3200]{1,0:T(8,128)(2,1)S(1)} %get-tuple-element.57), channel_id=1, source_target_pairs={{0,16},{8,24},{16,0},{24,8},{1,17},{9,25},{17,1},{25,9},{2,18},{10... | collective-permute-start | bytes 2457608 | tf_op jit(solution)/shard_map/ppermute | solution.py:295
  261.8 61.1 %collective-permute-start.30 = (f32[64,3200]{1,0:T(8,128)S(1)}, f32[64,3200]{1,0:T(8,128)S(1)}, u32[]{:S(2)}, u32[]{:S(2)}) collective-permute-start(f32[64,3200]{1,0:T(8,128)S(1)} %pad_maximum_fusion.3), channel_id=1, source_target_pairs={{0,16},{8,24},{16,0},{24,8},{1,17},{9,25},{17,1},{25,9},{2,18},{10... | collective-permute-start | bytes 2457608 | tf_op jit(solution)/shard_map/ppermute | solution.py:295
  266.8 57.0 %collective-permute-start.26 = (f32[64,3200]{1,0:T(8,128)S(1)}, f32[64,3200]{1,0:T(8,128)S(1)}, u32[]{:S(2)}, u32[]{:S(2)}) collective-permute-start(f32[64,3200]{1,0:T(8,128)S(1)} %pad_maximum_fusion.2), channel_id=1, source_target_pairs={{0,8},{8,0},{16,24},{24,16},{1,9},{9,1},{17,25},{25,17},{2,10},{10... | collective-permute-start | bytes 2457608 | tf_op jit(solution)/shard_map/ppermute | solution.py:295
  269.2 49.5 %collective-permute-start.18 = (f32[256,256]{1,0:T(8,128)S(1)}, f32[256,256]{1,0:T(8,128)S(1)}, u32[]{:S(2)}, u32[]{:S(2)}) collective-permute-start(f32[256,256]{1,0:T(8,128)S(1)} %add.87), channel_id=1, source_target_pairs={{0,16},{8,24},{16,0},{24,8},{1,17},{9,25},{17,1},{25,9},{2,18},{10... | collective-permute-start | bytes 786440 | tf_op jit(solution)/shard_map/ppermute | solution.py:295
  318.7 56.5 %collective-permute-start.43 = (bf16[256,3200]{1,0:T(8,128)(2,1)}, bf16[256,3200]{1,0:T(8,128)(2,1)}, u32[]{:S(2)}, u32[]{:S(2)}) collective-permute-start(bf16[256,3200]{1,0:T(8,128)(2,1)} %get-tuple-element.54.refs_4_), channel_id=1, source_target_pairs={{0,16},{8,24},{16,0},{24,8},{1,17},{9,25},{17,1},{25,9},{2,18},{10... | collective-permute-start | bytes 4915208 | tf_op jit(solution)/shard_map/ppermute | solution.py:295
  320.9 54.4 %collective-permute-start.46 = (bf16[128,3200]{1,0:T(8,128)(2,1)}, bf16[128,3200]{1,0:T(8,128)(2,1)}, u32[]{:S(2)}, u32[]{:S(2)}) collective-permute-start(bf16[128,3200]{1,0:T(8,128)(2,1)} %collective-permute-done.45.refs_6_), channel_id=1, source_target_pairs={{0,16},{8,24},{16,0},{24,8},{1,17},{9,25},{17,1},{25,9},{2,18},{10... | collective-permute-start | bytes 2457608 | tf_op jit(solution)/shard_map/ppermute | solution.py:295
  321.5 78.1 %collective-permute-start.40 = (bf16[128,3200]{1,0:T(8,128)(2,1)}, bf16[128,3200]{1,0:T(8,128)(2,1)}, u32[]{:S(2)}, u32[]{:S(2)}) collective-permute-start(bf16[128,3200]{1,0:T(8,128)(2,1)} %collective-permute-done.39.refs_7_), channel_id=1, source_target_pairs={{0,16},{8,24},{16,0},{24,8},{1,17},{9,25},{17,1},{25,9},{2,18},{10... | collective-permute-start | bytes 2457608 | tf_op jit(solution)/shard_map/ppermute | solution.py:295
  323.8 51.4 %collective-permute-start.47 = (bf16[128,3200]{1,0:T(8,128)(2,1)}, bf16[128,3200]{1,0:T(8,128)(2,1)}, u32[]{:S(2)}, u32[]{:S(2)}) collective-permute-start(bf16[128,3200]{1,0:T(8,128)(2,1)} %collective-permute-done.44.refs_5_), channel_id=1, source_target_pairs={{0,8},{8,0},{16,24},{24,16},{1,9},{9,1},{17,25},{25,17},{2,10},{10... | collective-permute-start | bytes 2457608 | tf_op jit(solution)/shard_map/ppermute | solution.py:295
  324.7 74.9 %collective-permute-start.42 = (bf16[128,3200]{1,0:T(8,128)(2,1)}, bf16[128,3200]{1,0:T(8,128)(2,1)}, u32[]{:S(2)}, u32[]{:S(2)}) collective-permute-start(bf16[128,3200]{1,0:T(8,128)(2,1)} %collective-permute-done.41.refs_6_), channel_id=1, source_target_pairs={{0,8},{8,0},{16,24},{24,16},{1,9},{9,1},{17,25},{25,17},{2,10},{10... | collective-permute-start | bytes 2457608 | tf_op jit(solution)/shard_map/ppermute | solution.py:295
  375.2 19.4 %collective-permute-start.31 = (f32[8,256]{1,0:T(8,128)S(1)}, f32[8,256]{1,0:T(8,128)S(1)}, u32[]{:S(2)}, u32[]{:S(2)}) collective-permute-start(f32[8,256]{1,0:T(8,128)S(1)} %get-tuple-element.48), channel_id=1, source_target_pairs={{0,1},{1,0},{2,3},{3,2},{4,5},{5,4},{6,7},{7,6},{8,9},{9,8},{10,11... | collective-permute-start | bytes 24584 | tf_op jit(solution)/shard_map/ppermute | solution.py:295
  394.7 22.3 %collective-permute-start.32 = (f32[8,256]{1,0:T(8,128)S(1)}, f32[8,256]{1,0:T(8,128)S(1)}, u32[]{:S(2)}, u32[]{:S(2)}) collective-permute-start(f32[8,256]{1,0:T(8,128)S(1)} %add.98), channel_id=1, source_target_pairs={{0,2},{1,3},{2,0},{3,1},{4,6},{5,7},{6,4},{7,5},{8,10},{9,11},{10,... | collective-permute-start | bytes 24584 | tf_op jit(solution)/shard_map/ppermute | solution.py:295
  397.1 19.9 %collective-permute-start.33 = (f32[8,256]{1,0:T(8,128)S(1)}, f32[8,256]{1,0:T(8,128)S(1)}, u32[]{:S(2)}, u32[]{:S(2)}) collective-permute-start(f32[8,256]{1,0:T(8,128)S(1)} %add.98), channel_id=1, source_target_pairs={{0,4},{1,5},{2,6},{3,7},{4,0},{5,1},{6,2},{7,3},{8,12},{9,13},{10,... | collective-permute-start | bytes 24584 | tf_op jit(solution)/shard_map/ppermute | solution.py:295
  398.1 18.9 %collective-permute-start.34 = (f32[8,256]{1,0:T(8,128)S(1)}, f32[8,256]{1,0:T(8,128)S(1)}, u32[]{:S(2)}, u32[]{:S(2)}) collective-permute-start(f32[8,256]{1,0:T(8,128)S(1)} %add.98), channel_id=1, source_target_pairs={{0,6},{1,7},{2,4},{3,5},{4,2},{5,3},{6,0},{7,1},{8,14},{9,15},{10,... | collective-permute-start | bytes 24584 | tf_op jit(solution)/shard_map/ppermute | solution.py:295
  (39 other events, 390.7 us)

commit v5 on v4

--- a/solution.py
+++ b/solution.py
@@ -103,7 +103,7 @@
 
 
 bf16 = jnp.bfloat16
-VMEM_MIB = 40
+VMEM_MIB = 30
 whole_vmem = pl.BlockSpec(memory_space=pltpu.VMEM)
 whole_smem = pl.BlockSpec(memory_space=pltpu.SMEM)
 
@@ -178,11 +178,10 @@
 
 
 def rank_block(row, i):
-    bit_x, bit_y = row % 2, row // 2
     upper, lower = (i // 2) % 2, i % 2
     if i < 4:
-        return 2 * (upper ^ bit_x) + (lower ^ bit_y)
-    return 4 + 2 * (upper ^ bit_y) + (lower ^ bit_x)
+        return 2 * (upper ^ (row % 2)) + lower
+    return 4 + 2 * (upper ^ (row // 2)) + lower
 
 
 def side_kernel(big_t, low_t, momentum, top_keep, top_send, low_keep, low_send):
@@ -196,7 +195,7 @@
 
 
 def token_kernel(ids, own, other, inputs, *refs):
-    before, after_refs, flip, tok = refs[:4], refs[4:10], refs[10], refs[11]
+    before, after_refs, flip, tok = refs[:4], refs[4:8], refs[8], refs[9]
     row, core = ids[0], ids[2]
     half = own.shape[0]
     size = flip.shape[0] // 8
@@ -216,13 +215,8 @@
         x = inputs[h * half : (h + 1) * half, :]
         total += mm(tok[h, 0], x, ((1,), (0,)))
         total += mm(tok[h, 1], x, ((1,), (0,)))
-    for p in range(2):
-        keep, send = before[2 * p], before[2 * p + 1]
-        first, second, out = after_refs[3 * p : 3 * p + 3]
-        at = 4 * p * size
-        first[...] = keep[:size, :] + total[at : at + size, :]
-        second[...] = keep[size:, :] + total[at + size : at + 2 * size, :]
-        out[...] = send[...] + total[at + 2 * size : at + 4 * size, :]
+    for i, (old, new) in enumerate(zip(before, after_refs)):
+        new[...] = old[...] + total[2 * i * size : 2 * (i + 1) * size, :]
 
 
 def gradient_kernel(numbers, cuts, ids, *refs):
@@ -239,7 +233,7 @@
 
 
 def right_kernel(n, ids, inverse, sketch, *refs):
-    pieces, right, squares, basis, work = refs[:6], refs[6], refs[7], refs[8], refs[9]
+    pieces, right, squares, basis, work = refs[:4], refs[4], refs[5], refs[6], refs[7]
     row = ids[0]
     size = work.shape[0] // 8
 
@@ -386,20 +380,14 @@
         side_kernel, (shaped((rank // 4, n)),) * 4, (big_t, low_t, momentum),
         [whole_vmem] * 2 + [columns(m)], (columns(rank // 4),) * 4, tiles,
         flops=6 * m * n * rank, moved=5 * m * n)
-    top0, top1, top_send, low0, low1, low_send = call(
-        token_kernel, (shaped((n8, n)), shaped((n8, n)), shaped((2 * n8, n))) * 2,
-        (ids, token, token_other, inputs, *sides),
-        [whole_smem] + [whole_vmem] * 2 + [columns(tokens)] + [columns(2 * n8)] * 4,
-        (columns(n8), columns(n8), columns(2 * n8)) * 2, tiles,
+    top, top_send, low, low_send = call(
+        token_kernel, (shaped((2 * n8, n)),) * 4, (ids, token, token_other, inputs, *sides),
+        [whole_smem] + [whole_vmem] * 2 + [columns(tokens)] + [columns(2 * n8)] * 4, (columns(2 * n8),) * 4, tiles,
         scratch=[pltpu.VMEM((rank, block), f32), pltpu.VMEM((2, 2, rank, block), bf16)],
         flops=4 * tokens * n * rank, moved=10 * rank * n)
-    top_in, low_in = swap(top_send, "row", 1), swap(low_send, "row", 2)
-    top1, low1 = top1 + top_in[n8:], low1 + low_in[n8:]
-    top0 = top0 + top_in[:n8] + swap(top1, "row", 2)
-    low0 = low0 + low_in[:n8] + swap(low1, "row", 1)
-    top1, low1 = swap(top0, "row", 2), swap(low0, "row", 1)
-    top2 = swap(jnp.concatenate([top0, top1], axis=0), "row", 1)
-    low2 = swap(jnp.concatenate([low0, low1], axis=0), "row", 2)
+    top, low = top + swap(top_send, "row", 1), low + swap(low_send, "row", 2)
+    top, low = top + swap(top, "row", 2), low + swap(low, "row", 1)
+    top_other, low_other = swap(top, "row", 1), swap(low, "row", 2)
 
     inverse = inverse_factor(gram)
 
@@ -418,8 +406,8 @@
 
     right, squares, basis = call(
         functools.partial(right_kernel, n), (shaped((rank, n)), shaped((8, rank)), shaped((m, rank))),
-        (ids, inverse, sketch, top0, top1, top2, low0, low1, low2),
-        [whole_smem] + [whole_vmem] * 2 + [columns(n8), columns(n8), columns(2 * n8)] * 2,
+        (ids, inverse, sketch, top, top_other, low, low_other),
+        [whole_smem] + [whole_vmem] * 2 + [columns(2 * n8)] * 4,
         (columns(rank), fixed(8, rank), fixed(m, rank)), tiles,
         scratch=[pltpu.VMEM((rank, tn), f32)], flops=6 * n * rank * rank, moved=12 * n * rank)
     squares = squares + swap(squares, "col", 1)

time: 433 us -> 408 us (0.942)
  waiting for transfers between devices: 211 us -> 196 us
  starting transfers between devices: 60 us -> 50.1 us
    ppermute x45 -> x43, waiting for transfers between devices: 191 us -> 176 us  [swap(): return lax.ppermute(x, axis, [(i, i ^ bit) for i in range(size)])]
    ppermute x45 -> x43, starting transfers between devices: 54.2 us -> 44.3 us  [swap(): return lax.ppermute(x, axis, [(i, i ^ bit) for i in range(size)])]
    unnamed x45 -> x41, local copies, waits for them, and re-layouts: 16.5 us -> 18.2 us
  transfers between devices with their start and end apart: 49 -> 47, of which waited for: 21 -> 18; matrix products, arithmetic and copies ran while one was open for 6% -> 6% of each run, Pallas kernels for 23% -> 24%
where the time goes in v5:
time: 408 us; the launch traced here: 407 us
  waiting for transfers between devices  196 us (48%)
  Pallas kernels  116 us (28%)
  starting transfers between devices  50.1 us (12%)
  local copies, waits for them, and re-layouts  20.8 us (5%)
  matrix products  15.8 us (4%)
  other arithmetic  7.35 us (2%)
    ppermute x43, waiting for transfers between devices, swap(): return lax.ppermute(x, axis, [(i, i ^ bit) for i in range(size)])  176 us
    pallas_call x9, Pallas kernels, call(): pl.pallas_call(kernel, out_shape=outs, grid_spec=pltpu.PrefetchScalarGrid...  103 us
    ppermute x43, starting transfers between devices, swap(): return lax.ppermute(x, axis, [(i, i ^ bit) for i in range(size)])  44.3 us
    ppermute x4, waiting for transfers between devices, line(): lax.ppermute(x, 'col', [(2 * a + h, 2 * b + h) for a, b in steps for h in...  19.5 us
    unnamed x41, local copies, waits for them, and re-layouts  18.2 us
    dot_general x2, matrix products, mm(): lax.dot_general(a, b, (dims, ((), ())), precision=precision, preferred_el...  15.8 us
    pallas_call x1, Pallas kernels, inverse_factor(): pl.pallas_call(inverse_kernel, out_shape=jax.ShapeDtypeStruct(gram.shape,...  13.6 us
  transfers between devices with their start and end apart: 47, of which 18 were waited for; matrix products, arithmetic and copies ran while one was open for 6% of the time, Pallas kernels for 24%

profile of v5, /device:TPU:0, one launch (start us, length us, event | category | flops | bytes accessed | tf_op | source)
XLA Modules:
  0.0 407.4 jit_solution(2862821175039046247)
XLA Ops:
  3.0 3.1 collective-permute-start
  7.5 13.5 %collective-permute-done.refs_1_.refs_6_ = bf16[1280,256]{1,0:T(8,128)(2,1)} collective-permute-done((bf16[1280,256]{1,0:T(8,128)(2,1)}, bf16[1280,256]{1,0:T(8,128)(2,1)}, u32[]{:S(2)}, u32[]{:S(2)}) %collective-permute-start) | collective-permute-done | bytes 655392 | tf_op jit(solution)/shard_map/ppermute | solution.py:289
  22.6 4.6 %fusion.6 = f32[512,256]{1,0:T(8,128)} fusion(bf16[512,3200]{1,0:T(8,128)(2,1)} %inputs.1, f32[3200,256]{1,0:T(8,128)S(1)} %copy-done), kind=kOutput, calls=%fused_computation.15 | convolution fusion | flops 2516582400 | bytes 7077888 | tf_op jit(solution)/shard_map/dot_general | solution.py:22
  37.3 11.2 %fusion.5.part = f32[1280,256]{1,0:T(8,128)} fusion(f32[1280,3200]{1,0:T(8,128)} %refs_9_.1, f32[3200,256]{1,0:T(8,128)S(1)} %copy-done), kind=kOutput, calls=%fused_computation.14 | convolution fusion | flops 6291456000 | bytes 20971520 | tf_op jit(solution)/shard_map/dot_general | solution.py:22
  48.6 6.9 %collective-permute-done.3.refs_4_ = bf16[1280,256]{1,0:T(8,128)(2,1)} collective-permute-done((bf16[1280,256]{1,0:T(8,128)(2,1)}, bf16[1280,256]{1,0:T(8,128)(2,1)}, u32[]{:S(2)}, u32[]{:S(2)}) %collective-permute-start.3) | collective-permute-done | bytes 655392 | tf_op jit(solution)/shard_map/ppermute | solution.py:298
  55.4 12.7 %collective-permute-done.4.refs_5_ = bf16[1280,256]{1,0:T(8,128)(2,1)} collective-permute-done((bf16[1280,256]{1,0:T(8,128)(2,1)}, bf16[1280,256]{1,0:T(8,128)(2,1)}, u32[]{:S(2)}, u32[]{:S(2)}) %collective-permute-start.4) | collective-permute-done | bytes 655392 | tf_op jit(solution)/shard_map/ppermute | solution.py:298
  69.4 4.7 %shard_map.76 = (f32[640,256]{1,0:T(8,128)S(1)}, f32[640,256]{1,0:T(8,128)S(1)}) custom-call(s32[4]{0:T(128)S(1)} %pad_add_fusion.ids, f32[1280,256]{1,0:T(8,128)S(1)} %copy-done.6, bf16[1280,256]{1,0:T(8,128)(2,1)} %bitcast.4.refs_0_.refs_5_, bf16[1280,256]{1,0:T(8,128)(2,1)} %collective-permute-done.refs_1_.refs_6_, ...), custom_call_target="tpu_custom_call" | custom-call | flops 1342177280 | bytes 8000000 | tf_op jit(solution)/shard_map/pallas_call | solution.py:121
  76.5 2.9 collective-permute-start.11
  80.9 4.8 %collective-permute-done.10 = f32[160,256]{1,0:T(8,128)S(1)} collective-permute-done((f32[160,256]{1,0:T(8,128)S(1)}, f32[160,256]{1,0:T(8,128)S(1)}, u32[]{:S(2)}, u32[]{:S(2)}) %collective-permute-start.10) | collective-permute-done | bytes 163872 | tf_op jit(solution)/shard_map/ppermute | solution.py:289
  85.7 5.9 %collective-permute-done.11 = f32[160,256]{1,0:T(8,128)S(1)} collective-permute-done((f32[160,256]{1,0:T(8,128)S(1)}, f32[160,256]{1,0:T(8,128)S(1)}, u32[]{:S(2)}, u32[]{:S(2)}) %collective-permute-start.11) | collective-permute-done | bytes 163872 | tf_op jit(solution)/shard_map/ppermute | solution.py:289
  91.6 3.3 collective-permute-start.13
  97.4 3.3 collective-permute-done.13.refs_1_
  100.7 9.1 %collective-permute-done.14.refs_2_ = f32[160,256]{1,0:T(8,128)S(1)} collective-permute-done((f32[160,256]{1,0:T(8,128)S(1)}, f32[160,256]{1,0:T(8,128)S(1)}, u32[]{:S(2)}, u32[]{:S(2)}) %collective-permute-start.14) | collective-permute-done | bytes 163872 | tf_op jit(solution)/shard_map/ppermute | solution.py:289
  112.8 4.4 %shard_map.77 = (f32[1280,256]{1,0:T(8,128)S(1)}, f32[256,256]{1,0:T(8,128)S(1)}, f32[256,256]{1,0:T(8,128)S(1)}, f32[256,256]{1,0:T(8,128)S(1)}, f32[256,256]{1...) custom-call(s32[4]{0:T(128)S(1)} %pad_add_fusion.ids, ...), custom_call_target="tpu_custom_call" | custom-call | flops 1677721600 | bytes 8000000 | tf_op jit(solution)/shard_map/pallas_call | solution.py:121
  120.8 5.7 %collective-permute-done.19 = f32[256,256]{1,0:T(8,128)S(1)} collective-permute-done((f32[256,256]{1,0:T(8,128)S(1)}, f32[256,256]{1,0:T(8,128)S(1)}, u32[]{:S(2)}, u32[]{:S(2)}) %collective-permute-start.19) | collective-permute-done | bytes 262176 | tf_op jit(solution)/shard_map/ppermute | solution.py:289
  126.5 6.4 %collective-permute-done.20 = f32[256,256]{1,0:T(8,128)S(1)} collective-permute-done((f32[256,256]{1,0:T(8,128)S(1)}, f32[256,256]{1,0:T(8,128)S(1)}, u32[]{:S(2)}, u32[]{:S(2)}) %collective-permute-start.20) | collective-permute-done | bytes 262176 | tf_op jit(solution)/shard_map/ppermute | solution.py:289
  133.0 5.6 %copy-done.4 = f32[1280,3200]{1,0:T(8,128)S(1)} copy-done((f32[1280,3200]{1,0:T(8,128)S(1)}, f32[1280,3200]{1,0:T(8,128)}, u32[]{:S(2)}) %copy-start.4) | copy-done | bytes 16384024
  138.6 12.2 %shard_map.79 = (f32[64,3200]{1,0:T(8,128)S(1)}, f32[64,3200]{1,0:T(8,128)S(1)}, f32[64,3200]{1,0:T(8,128)S(1)}, f32[64,3200]{1,0:T(8,128)S(1)}) custom-call(bf16[256,1280]{1,0:T(8,128)(2,1)S(1)} %get-tuple-element.34.big_t, bf16[256,1280]{1,0:T(8,128)(2,1)S(1)} %get-tuple-element.35.low_t, f32[1280,3200]{1,0:T(8,128)S(1)} %copy-done.4), custom_call_target="tpu_custom_call" | custom-call | flops 6291456000 | bytes 20480000 | tf_op jit(solution)/shard_map/pallas_call | solution.py:121
  150.8 7.0 %shard_map.80 = (f32[64,3200]{1,0:T(8,128)S(1)}, f32[64,3200]{1,0:T(8,128)S(1)}, f32[64,3200]{1,0:T(8,128)S(1)}, f32[64,3200]{1,0:T(8,128)S(1)}) custom-call(s32[4]{0:T(128)S(1)} %pad_add_fusion.ids, f32[256,256]{1,0:T(8,128)S(1)} %add_add_fusion.own, f32[256,256]{1,0:T(8,128)S(1)} %collective-permute-done.22.other, bf16[512,3200]{1,0:T(8,128)(2,1)S(1)} %copy-done.5, ...), custom_call_target="tpu_custom_call" | custom-call | flops 1677721600 | bytes 8192000 | tf_op jit(solution)/shard_map/pallas_call | solution.py:121
  162.3 16.2 %collective-permute-done.26 = f32[64,3200]{1,0:T(8,128)S(1)} collective-permute-done((f32[64,3200]{1,0:T(8,128)S(1)}, f32[64,3200]{1,0:T(8,128)S(1)}, u32[]{:S(2)}, u32[]{:S(2)}) %collective-permute-start.26) | collective-permute-done | bytes 819232 | tf_op jit(solution)/shard_map/ppermute | solution.py:289
  181.3 34.6 %collective-permute-done.23 = f32[64,3200]{1,0:T(8,128)S(1)} collective-permute-done((f32[64,3200]{1,0:T(8,128)S(1)}, f32[64,3200]{1,0:T(8,128)S(1)}, u32[]{:S(2)}, u32[]{:S(2)}) %collective-permute-start.23) | collective-permute-done | bytes 819232 | tf_op jit(solution)/shard_map/ppermute | solution.py:289
  218.4 15.1 %collective-permute-done.27 = f32[64,3200]{1,0:T(8,128)S(1)} collective-permute-done((f32[64,3200]{1,0:T(8,128)S(1)}, f32[64,3200]{1,0:T(8,128)S(1)}, u32[]{:S(2)}, u32[]{:S(2)}) %collective-permute-start.27) | collective-permute-done | bytes 819232 | tf_op jit(solution)/shard_map/ppermute | solution.py:289
  241.0 32.4 %collective-permute-done.17 = f32[256,256]{1,0:T(8,128)S(1)} collective-permute-done((f32[256,256]{1,0:T(8,128)S(1)}, f32[256,256]{1,0:T(8,128)S(1)}, u32[]{:S(2)}, u32[]{:S(2)}) %collective-permute-start.17) | collective-permute-done | bytes 262176 | tf_op jit(solution)/shard_map/ppermute | solution.py:289
  275.7 18.6 %shard_map.83.refs_9_ = f32[1280,3200]{1,0:T(8,128)} custom-call(s32[4]{0:T(128)S(1)} %pad_add_fusion.ids, bf16[4,1280,256]{2,1,0:T(8,128)(2,1)S(1)} %pad_maximum_fusion.refs_0_.refs_1_.own, bf16[4,1280,256]{2,1,0:T(8,128)(2,1)S(1)} %pad_maximum_fusion.refs_0_.refs_1_.own, bf16[4,1280,256]{2,1,0:T(8,128)(2,1)S(1)} %pad_maximum_fusion.1.refs_2_.refs_3_.other, ...), custom_call_target="tpu_custom_call" | custom-call | flops 8388608000 | bytes 32768000 | tf_op jit(solution)/shard_map/pallas_call | solution.py:121
  294.3 3.0 collective-permute-done.18
  304.9 13.6 %shard_map.78.inverse = f32[256,256]{1,0:T(8,128)} custom-call(f32[256,256]{1,0:T(8,128)} %add.82.gram_ref), custom_call_target="tpu_custom_call" | custom-call | flops 20000000000 | bytes 10000000 | tf_op jit(solution)/shard_map/pallas_call | solution.py:95
  325.5 7.4 %shard_map.81 = (f32[256,3200]{1,0:T(8,128)S(1)}, f32[8,256]{1,0:T(8,128)S(1)}, f32[1280,256]{1,0:T(8,128)S(1)}) custom-call(s32[4]{0:T(128)S(1)} %pad_add_fusion.ids, f32[256,256]{1,0:T(8,128)S(1)} %copy-done.17, f32[1280,256]{1,0:T(8,128)S(1)} %copy-done.12, f32[64,3200]{1,0:T(8,128)S(1)} %copy-done.10, f32[64,3200]{1,0:T(8,128)S(1)} %copy-done.16, ...), custom_call_target="tpu_custom_call" | custom-call | flops 1258291200 | bytes 9830400 | tf_op jit(solution)/shard_map/pallas_call | solution.py:121
  332.9 20.9 %collective-permute-done.44.refs_7_ = bf16[128,3200]{1,0:T(8,128)(2,1)} collective-permute-done((bf16[128,3200]{1,0:T(8,128)(2,1)}, bf16[128,3200]{1,0:T(8,128)(2,1)}, u32[]{:S(2)}, u32[]{:S(2)}) %collective-permute-start.44) | collective-permute-done | bytes 819232 | tf_op jit(solution)/shard_map/ppermute | solution.py:289
  353.8 19.7 %shard_map.84.base = f32[1280,3200]{1,0:T(8,128)} custom-call(s32[4]{0:T(128)S(1)} %pad_add_fusion.ids, bf16[4,1280,256]{2,1,0:T(8,128)(2,1)S(1)} %pad_maximum_fusion.refs_0_.refs_1_.own, bf16[4,1280,256]{2,1,0:T(8,128)(2,1)S(1)} %pad_maximum_fusion.refs_0_.refs_1_.own, bf16[4,1280,256]{2,1,0:T(8,128)(2,1)S(1)} %copy-done.3, ...), custom_call_target="tpu_custom_call" | custom-call | flops 6291456000 | bytes 32768000 | tf_op jit(solution)/shard_map/pallas_call | solution.py:121
  373.5 2.5 collective-permute-start.30
  378.4 17.4 %shard_map.85 = f32[1280,3200]{1,0:T(8,128)} custom-call(s32[4]{0:T(128)S(1)} %pad_add_fusion.ids, bf16[4,1280,256]{2,1,0:T(8,128)(2,1)S(1)} %pad_maximum_fusion.refs_0_.refs_1_.own, bf16[4,1280,256]{2,1,0:T(8,128)(2,1)S(1)} %copy-done.3, bf16[128,3200]{1,0:T(8,128)(2,1)} %collective-permute-done.38.first, ...), custom_call_target="tpu_custom_call", output_to_operand_aliasing={{}: (7, {})} | custom-call | flops 4194304000 | bytes 32768000 | tf_op jit(solution)/shard_map/pallas_call | solution.py:121
  395.9 11.6 %shard_map.82 = (f32[1280,3200]{1,0:T(8,128)}, f32[3200,256]{1,0:T(8,128)}) custom-call(f32[8,256]{1,0:T(8,128)S(1)} %add_add_fusion.1.squares, f32[1280,256]{1,0:T(8,128)S(1)} %get-tuple-element.45.basis, f32[256,3200]{1,0:T(8,128)S(1)} %get-tuple-element.46.right, bf16[1280,3200]{1,0:T(8,128)(2,1)S(1)} %bitcast.21), custom_call_target="tpu_custom_call" | custom-call | flops 6291456000 | bytes 24576000 | tf_op jit(solution)/shard_map/pallas_call | solution.py:121
  (138 shorter events, 66.3 us)
Async XLA Ops:
  3.0 18.1 %collective-permute-start = (bf16[1280,256]{1,0:T(8,128)(2,1)}, bf16[1280,256]{1,0:T(8,128)(2,1)}, u32[]{:S(2)}, u32[]{:S(2)}) collective-permute-start(bf16[1280,256]{1,0:T(8,128)(2,1)} %bitcast.4.refs_0_.refs_5_), channel_id=1, source_target_pairs={{0,2},{1,3},{2,0},{3,1},{4,6},{5,7},{6,4},{7,5},{8,10},{9,11},{10,... | collective-permute-start | bytes 1966088 | tf_op jit(solution)/shard_map/ppermute | solution.py:289
  6.0 28.5 %collective-permute-start.1 = (bf16[1280,256]{1,0:T(8,128)(2,1)}, bf16[1280,256]{1,0:T(8,128)(2,1)}, u32[]{:S(2)}, u32[]{:S(2)}) collective-permute-start(bf16[1280,256]{1,0:T(8,128)(2,1)} %bitcast.4.refs_0_.refs_5_), channel_id=1, source_target_pairs={{2,4},{3,5},{4,2},{5,3},{10,12},{11,13},{12,10},{13,11},{18,20},{1... | collective-permute-start | bytes 1966088 | tf_op jit(solution)/shard_map/ppermute | solution.py:298
  31.0 17.6 %collective-permute-start.6 = (f32[256,256]{1,0:T(8,128)S(1)}, f32[256,256]{1,0:T(8,128)}, u32[]{:S(2)}, u32[]{:S(2)}) collective-permute-start(f32[256,256]{1,0:T(8,128)S(1)} %dynamic-slice_add_fusion.refs_6_), channel_id=1, source_target_pairs={{0,8},{8,0},{16,24},{24,16},{1,9},{9,1},{17,25},{25,17},{2,10},{10... | collective-permute-start | bytes 786440 | tf_op jit(solution)/shard_map/ppermute | solution.py:289
  32.7 15.9 %collective-permute-start.7 = (f32[256,256]{1,0:T(8,128)S(1)}, f32[256,256]{1,0:T(8,128)}, u32[]{:S(2)}, u32[]{:S(2)}) collective-permute-start(f32[256,256]{1,0:T(8,128)S(1)} %dynamic-slice_add_fusion.refs_6_), channel_id=1, source_target_pairs={{0,16},{8,24},{16,0},{24,8},{1,17},{9,25},{17,1},{25,9},{2,18},{10... | collective-permute-start | bytes 786440 | tf_op jit(solution)/shard_map/ppermute | solution.py:289
  34.5 20.9 %collective-permute-start.3 = (bf16[1280,256]{1,0:T(8,128)(2,1)}, bf16[1280,256]{1,0:T(8,128)(2,1)}, u32[]{:S(2)}, u32[]{:S(2)}) collective-permute-start(bf16[1280,256]{1,0:T(8,128)(2,1)} %collective-permute-done.1.refs_2_), channel_id=1, source_target_pairs={{2,0},{3,1},{4,6},{5,7},{10,8},{11,9},{12,14},{13,15},{18,16},{19,... | collective-permute-start | bytes 1966088 | tf_op jit(solution)/shard_map/ppermute | solution.py:298
  35.8 32.3 %collective-permute-start.4 = (bf16[1280,256]{1,0:T(8,128)(2,1)}, bf16[1280,256]{1,0:T(8,128)(2,1)}, u32[]{:S(2)}, u32[]{:S(2)}) collective-permute-start(bf16[1280,256]{1,0:T(8,128)(2,1)} %collective-permute-done.2.refs_3_), channel_id=1, source_target_pairs={{2,0},{3,1},{4,6},{5,7},{10,8},{11,9},{12,14},{13,15},{18,16},{19,... | collective-permute-start | bytes 1966088 | tf_op jit(solution)/shard_map/ppermute | solution.py:298
  120.8 95.8 %collective-permute-start.33 = (bf16[1280,256]{1,0:T(8,128)(2,1)}, bf16[1280,256]{1,0:T(8,128)(2,1)S(1)}, u32[]{:S(2)}, u32[]{:S(2)}) collective-permute-start(bf16[1280,256]{1,0:T(8,128)(2,1)} %bitcast.4.refs_0_.refs_5_), channel_id=1, source_target_pairs={{0,1},{1,0},{2,3},{3,2},{4,5},{5,4},{6,7},{7,6},{8,9},{9,8},{10,11... | collective-permute-start | bytes 1966088 | tf_op jit(solution)/shard_map/ppermute | solution.py:289
  132.9 17.9 %collective-permute-start.22 = (f32[256,256]{1,0:T(8,128)S(1)}, f32[256,256]{1,0:T(8,128)S(1)}, u32[]{:S(2)}, u32[]{:S(2)}) collective-permute-start(f32[256,256]{1,0:T(8,128)S(1)} %add_add_fusion.own), channel_id=1, source_target_pairs={{0,1},{1,0},{2,3},{3,2},{4,5},{5,4},{6,7},{7,6},{8,9},{9,8},{10,11... | collective-permute-start | bytes 786440 | tf_op jit(solution)/shard_map/ppermute | solution.py:289
  157.8 20.7 %collective-permute-start.26 = (f32[64,3200]{1,0:T(8,128)S(1)}, f32[64,3200]{1,0:T(8,128)S(1)}, u32[]{:S(2)}, u32[]{:S(2)}) collective-permute-start(f32[64,3200]{1,0:T(8,128)S(1)} %get-tuple-element.43), channel_id=1, source_target_pairs={{0,16},{8,24},{16,0},{24,8},{1,17},{9,25},{17,1},{25,9},{2,18},{10... | collective-permute-start | bytes 2457608 | tf_op jit(solution)/shard_map/ppermute | solution.py:289
  159.7 58.2 %collective-permute-start.37 = (bf16[128,3200]{1,0:T(8,128)(2,1)S(1)}, bf16[128,3200]{1,0:T(8,128)(2,1)}, u32[]{:S(2)}, u32[]{:S(2)}) collective-permute-start(bf16[128,3200]{1,0:T(8,128)(2,1)S(1)} %get-tuple-element.54), channel_id=1, source_target_pairs={{0,8},{8,0},{16,24},{24,16},{1,9},{9,1},{17,25},{25,17},{2,10},{10... | collective-permute-start | bytes 2457608 | tf_op jit(solution)/shard_map/ppermute | solution.py:289
  160.3 57.6 %collective-permute-start.43 = (bf16[128,3200]{1,0:T(8,128)(2,1)S(1)}, bf16[128,3200]{1,0:T(8,128)(2,1)}, u32[]{:S(2)}, u32[]{:S(2)}) collective-permute-start(bf16[128,3200]{1,0:T(8,128)(2,1)S(1)} %get-tuple-element.51), channel_id=1, source_target_pairs={{0,8},{8,0},{16,24},{24,16},{1,9},{9,1},{17,25},{25,17},{2,10},{10... | collective-permute-start | bytes 2457608 | tf_op jit(solution)/shard_map/ppermute | solution.py:289
  161.7 54.2 %collective-permute-start.23 = (f32[64,3200]{1,0:T(8,128)S(1)}, f32[64,3200]{1,0:T(8,128)S(1)}, u32[]{:S(2)}, u32[]{:S(2)}) collective-permute-start(f32[64,3200]{1,0:T(8,128)S(1)} %get-tuple-element.41), channel_id=1, source_target_pairs={{0,8},{8,0},{16,24},{24,16},{1,9},{9,1},{17,25},{25,17},{2,10},{10... | collective-permute-start | bytes 2457608 | tf_op jit(solution)/shard_map/ppermute | solution.py:289
  178.6 54.9 %collective-permute-start.27 = (f32[64,3200]{1,0:T(8,128)S(1)}, f32[64,3200]{1,0:T(8,128)S(1)}, u32[]{:S(2)}, u32[]{:S(2)}) collective-permute-start(f32[64,3200]{1,0:T(8,128)S(1)} %add.88), channel_id=1, source_target_pairs={{0,8},{8,0},{16,24},{24,16},{1,9},{9,1},{17,25},{25,17},{2,10},{10... | collective-permute-start | bytes 2457608 | tf_op jit(solution)/shard_map/ppermute | solution.py:289
  215.9 58.5 %collective-permute-start.46 = (bf16[256,3200]{1,0:T(8,128)(2,1)S(1)}, bf16[256,3200]{1,0:T(8,128)(2,1)S(1)}, u32[]{:S(2)}, u32[]{:S(2)}) collective-permute-start(bf16[256,3200]{1,0:T(8,128)(2,1)S(1)} %get-tuple-element.49.refs_5_), channel_id=1, source_target_pairs={{0,8},{8,0},{16,24},{24,16},{1,9},{9,1},{17,25},{25,17},{2,10},{10... | collective-permute-start | bytes 4915208 | tf_op jit(solution)/shard_map/ppermute | solution.py:289
  216.6 18.5 %collective-permute-start.24 = (f32[64,3200]{1,0:T(8,128)S(1)}, f32[64,3200]{1,0:T(8,128)S(1)}, u32[]{:S(2)}, u32[]{:S(2)}) collective-permute-start(f32[64,3200]{1,0:T(8,128)S(1)} %add.86), channel_id=1, source_target_pairs={{0,16},{8,24},{16,0},{24,8},{1,17},{9,25},{17,1},{25,9},{2,18},{10... | collective-permute-start | bytes 2457608 | tf_op jit(solution)/shard_map/ppermute | solution.py:289
  217.9 20.6 %collective-permute-start.34 = (bf16[1280,256]{1,0:T(8,128)(2,1)}, bf16[1280,256]{1,0:T(8,128)(2,1)S(1)}, u32[]{:S(2)}, u32[]{:S(2)}) collective-permute-start(bf16[1280,256]{1,0:T(8,128)(2,1)} %collective-permute-done.refs_1_.refs_6_), channel_id=1, source_target_pairs={{0,1},{1,0},{2,3},{3,2},{4,5},{5,4},{6,7},{7,6},{8,9},{9,8},{10,11... | collective-permute-start | bytes 1966088 | tf_op jit(solution)/shard_map/ppermute | solution.py:289
  217.9 21.1 %collective-permute-start.35 = (bf16[1280,256]{1,0:T(8,128)(2,1)S(1)}, bf16[1280,256]{1,0:T(8,128)(2,1)S(1)}, u32[]{:S(2)}, u32[]{:S(2)}) collective-permute-start(bf16[1280,256]{1,0:T(8,128)(2,1)S(1)} %add.79.refs_7_), channel_id=1, source_target_pairs={{0,1},{1,0},{2,3},{3,2},{4,5},{5,4},{6,7},{7,6},{8,9},{9,8},{10,11... | collective-permute-start | bytes 1966088 | tf_op jit(solution)/shard_map/ppermute | solution.py:289
  235.1 38.4 %collective-permute-start.17 = (f32[256,256]{1,0:T(8,128)S(1)}, f32[256,256]{1,0:T(8,128)S(1)}, u32[]{:S(2)}, u32[]{:S(2)}) collective-permute-start(f32[256,256]{1,0:T(8,128)S(1)} %get-tuple-element.28), channel_id=1, source_target_pairs={{0,8},{8,0},{16,24},{24,16},{1,9},{9,1},{17,25},{25,17},{2,10},{10... | collective-permute-start | bytes 786440 | tf_op jit(solution)/shard_map/ppermute | solution.py:289
  238.4 60.6 %collective-permute-start.42 = (bf16[128,3200]{1,0:T(8,128)(2,1)S(1)}, bf16[128,3200]{1,0:T(8,128)(2,1)}, u32[]{:S(2)}, u32[]{:S(2)}) collective-permute-start(bf16[128,3200]{1,0:T(8,128)(2,1)S(1)} %get-tuple-element.52), channel_id=1, source_target_pairs={{0,16},{8,24},{16,0},{24,8},{1,17},{9,25},{17,1},{25,9},{2,18},{10... | collective-permute-start | bytes 2457608 | tf_op jit(solution)/shard_map/ppermute | solution.py:289
  239.0 61.0 %collective-permute-start.39 = (bf16[128,3200]{1,0:T(8,128)(2,1)S(1)}, bf16[128,3200]{1,0:T(8,128)(2,1)}, u32[]{:S(2)}, u32[]{:S(2)}) collective-permute-start(bf16[128,3200]{1,0:T(8,128)(2,1)S(1)} %get-tuple-element.53), channel_id=1, source_target_pairs={{0,16},{8,24},{16,0},{24,8},{1,17},{9,25},{17,1},{25,9},{2,18},{10... | collective-permute-start | bytes 2457608 | tf_op jit(solution)/shard_map/ppermute | solution.py:289
  240.5 60.5 %collective-permute-start.28 = (f32[64,3200]{1,0:T(8,128)S(1)}, f32[64,3200]{1,0:T(8,128)S(1)}, u32[]{:S(2)}, u32[]{:S(2)}) collective-permute-start(f32[64,3200]{1,0:T(8,128)S(1)} %add.89.refs_2_), channel_id=1, source_target_pairs={{0,16},{8,24},{16,0},{24,8},{1,17},{9,25},{17,1},{25,9},{2,18},{10... | collective-permute-start | bytes 2457608 | tf_op jit(solution)/shard_map/ppermute | solution.py:289
  273.5 29.3 %collective-permute-start.25 = (f32[64,3200]{1,0:T(8,128)S(1)}, f32[64,3200]{1,0:T(8,128)S(1)}, u32[]{:S(2)}, u32[]{:S(2)}) collective-permute-start(f32[64,3200]{1,0:T(8,128)S(1)} %add.87.refs_0_), channel_id=1, source_target_pairs={{0,8},{8,0},{16,24},{24,16},{1,9},{9,1},{17,25},{25,17},{2,10},{10... | collective-permute-start | bytes 2457608 | tf_op jit(solution)/shard_map/ppermute | solution.py:289
  274.4 22.8 %collective-permute-start.18 = (f32[256,256]{1,0:T(8,128)S(1)}, f32[256,256]{1,0:T(8,128)S(1)}, u32[]{:S(2)}, u32[]{:S(2)}) collective-permute-start(f32[256,256]{1,0:T(8,128)S(1)} %add.81), channel_id=1, source_target_pairs={{0,16},{8,24},{16,0},{24,8},{1,17},{9,25},{17,1},{25,9},{2,18},{10... | collective-permute-start | bytes 786440 | tf_op jit(solution)/shard_map/ppermute | solution.py:289
  297.2 56.6 %collective-permute-start.41 = (bf16[256,3200]{1,0:T(8,128)(2,1)}, bf16[256,3200]{1,0:T(8,128)(2,1)}, u32[]{:S(2)}, u32[]{:S(2)}) collective-permute-start(bf16[256,3200]{1,0:T(8,128)(2,1)} %get-tuple-element.50.refs_4_), channel_id=1, source_target_pairs={{0,16},{8,24},{16,0},{24,8},{1,17},{9,25},{17,1},{25,9},{2,18},{10... | collective-permute-start | bytes 4915208 | tf_op jit(solution)/shard_map/ppermute | solution.py:289
  299.0 54.8 %collective-permute-start.44 = (bf16[128,3200]{1,0:T(8,128)(2,1)}, bf16[128,3200]{1,0:T(8,128)(2,1)}, u32[]{:S(2)}, u32[]{:S(2)}) collective-permute-start(bf16[128,3200]{1,0:T(8,128)(2,1)} %collective-permute-done.43.refs_6_), channel_id=1, source_target_pairs={{0,16},{8,24},{16,0},{24,8},{1,17},{9,25},{17,1},{25,9},{2,18},{10... | collective-permute-start | bytes 2457608 | tf_op jit(solution)/shard_map/ppermute | solution.py:289
  300.0 78.4 %collective-permute-start.38 = (bf16[128,3200]{1,0:T(8,128)(2,1)}, bf16[128,3200]{1,0:T(8,128)(2,1)}, u32[]{:S(2)}, u32[]{:S(2)}) collective-permute-start(bf16[128,3200]{1,0:T(8,128)(2,1)} %collective-permute-done.37.refs_7_), channel_id=1, source_target_pairs={{0,16},{8,24},{16,0},{24,8},{1,17},{9,25},{17,1},{25,9},{2,18},{10... | collective-permute-start | bytes 2457608 | tf_op jit(solution)/shard_map/ppermute | solution.py:289
  302.0 51.8 %collective-permute-start.45 = (bf16[128,3200]{1,0:T(8,128)(2,1)}, bf16[128,3200]{1,0:T(8,128)(2,1)}, u32[]{:S(2)}, u32[]{:S(2)}) collective-permute-start(bf16[128,3200]{1,0:T(8,128)(2,1)} %collective-permute-done.42.refs_5_), channel_id=1, source_target_pairs={{0,8},{8,0},{16,24},{24,16},{1,9},{9,1},{17,25},{25,17},{2,10},{10... | collective-permute-start | bytes 2457608 | tf_op jit(solution)/shard_map/ppermute | solution.py:289
  303.7 74.7 %collective-permute-start.40 = (bf16[128,3200]{1,0:T(8,128)(2,1)}, bf16[128,3200]{1,0:T(8,128)(2,1)}, u32[]{:S(2)}, u32[]{:S(2)}) collective-permute-start(bf16[128,3200]{1,0:T(8,128)(2,1)} %collective-permute-done.39.refs_6_), channel_id=1, source_target_pairs={{0,8},{8,0},{16,24},{24,16},{1,9},{9,1},{17,25},{25,17},{2,10},{10... | collective-permute-start | bytes 2457608 | tf_op jit(solution)/shard_map/ppermute | solution.py:289
  353.8 19.7 %collective-permute-start.29 = (f32[8,256]{1,0:T(8,128)S(1)}, f32[8,256]{1,0:T(8,128)S(1)}, u32[]{:S(2)}, u32[]{:S(2)}) collective-permute-start(f32[8,256]{1,0:T(8,128)S(1)} %get-tuple-element.44), channel_id=1, source_target_pairs={{0,1},{1,0},{2,3},{3,2},{4,5},{5,4},{6,7},{7,6},{8,9},{9,8},{10,11... | collective-permute-start | bytes 24584 | tf_op jit(solution)/shard_map/ppermute | solution.py:289
  373.5 22.3 %collective-permute-start.30 = (f32[8,256]{1,0:T(8,128)S(1)}, f32[8,256]{1,0:T(8,128)S(1)}, u32[]{:S(2)}, u32[]{:S(2)}) collective-permute-start(f32[8,256]{1,0:T(8,128)S(1)} %add.90), channel_id=1, source_target_pairs={{0,2},{1,3},{2,0},{3,1},{4,6},{5,7},{6,4},{7,5},{8,10},{9,11},{10,... | collective-permute-start | bytes 24584 | tf_op jit(solution)/shard_map/ppermute | solution.py:289
  376.0 19.9 %collective-permute-start.31 = (f32[8,256]{1,0:T(8,128)S(1)}, f32[8,256]{1,0:T(8,128)S(1)}, u32[]{:S(2)}, u32[]{:S(2)}) collective-permute-start(f32[8,256]{1,0:T(8,128)S(1)} %add.90), channel_id=1, source_target_pairs={{0,4},{1,5},{2,6},{3,7},{4,0},{5,1},{6,2},{7,3},{8,12},{9,13},{10,... | collective-permute-start | bytes 24584 | tf_op jit(solution)/shard_map/ppermute | solution.py:289
  376.9 18.9 %collective-permute-start.32 = (f32[8,256]{1,0:T(8,128)S(1)}, f32[8,256]{1,0:T(8,128)S(1)}, u32[]{:S(2)}, u32[]{:S(2)}) collective-permute-start(f32[8,256]{1,0:T(8,128)S(1)} %add.90), channel_id=1, source_target_pairs={{0,6},{1,7},{2,4},{3,5},{4,2},{5,3},{6,0},{7,1},{8,14},{9,15},{10,... | collective-permute-start | bytes 24584 | tf_op jit(solution)/shard_map/ppermute | solution.py:289
  (35 other events, 469.9 us)

commit v6 on v5

--- a/solution.py
+++ b/solution.py
@@ -117,7 +117,7 @@
     return min(n, 512)
 
 
-def call(kernel, outs, ins, specs, out_specs, grid=(), scratch=(), flops=0, moved=0, aliases={}, prefetch=0):
+def call(kernel, outs, ins, specs, out_specs, grid=(), scratch=(), flops=0, moved=0, aliases={}, prefetch=0, grant=VMEM_MIB):
     return pl.pallas_call(
         kernel,
         out_shape=outs,
@@ -125,7 +125,7 @@
             num_scalar_prefetch=prefetch, grid=grid, in_specs=specs, out_specs=out_specs, scratch_shapes=list(scratch)
         ),
         input_output_aliases=aliases,
-        compiler_params=pltpu.CompilerParams(vmem_limit_bytes=VMEM_MIB * 2**20),
+        compiler_params=pltpu.CompilerParams(vmem_limit_bytes=grant * 2**20),
         cost_estimate=pl.CostEstimate(flops=flops, bytes_accessed=moved, transcendentals=0),
     )(*ins)
 
@@ -379,7 +379,7 @@
     sides = call(
         side_kernel, (shaped((rank // 4, n)),) * 4, (big_t, low_t, momentum),
         [whole_vmem] * 2 + [columns(m)], (columns(rank // 4),) * 4, tiles,
-        flops=6 * m * n * rank, moved=5 * m * n)
+        flops=6 * m * n * rank, moved=5 * m * n, grant=40)
     top, top_send, low, low_send = call(
         token_kernel, (shaped((2 * n8, n)),) * 4, (ids, token, token_other, inputs, *sides),
         [whole_smem] + [whole_vmem] * 2 + [columns(tokens)] + [columns(2 * n8)] * 4, (columns(2 * n8),) * 4, tiles,

time: 408 us -> 403 us (0.988)
  local copies, waits for them, and re-layouts: 20.8 us -> 15.2 us
    unnamed x41 -> x39, local copies, waits for them, and re-layouts: 18.2 us -> 12.5 us
where the time goes in v6:
time: 403 us; the launch traced here: 402 us
  waiting for transfers between devices  196 us (49%)
  Pallas kernels  117 us (29%)
  starting transfers between devices  50.1 us (12%)
  matrix products  15.8 us (4%)
  local copies, waits for them, and re-layouts  15.2 us (4%)
  other arithmetic  7.36 us (2%)
    ppermute x43, waiting for transfers between devices, swap(): return lax.ppermute(x, axis, [(i, i ^ bit) for i in range(size)])  176 us
    pallas_call x9, Pallas kernels, call(): pl.pallas_call(kernel, out_shape=outs, grid_spec=pltpu.PrefetchScalarGrid...  103 us
    ppermute x43, starting transfers between devices, swap(): return lax.ppermute(x, axis, [(i, i ^ bit) for i in range(size)])  44.3 us
    ppermute x4, waiting for transfers between devices, line(): lax.ppermute(x, 'col', [(2 * a + h, 2 * b + h) for a, b in steps for h in...  19.5 us
    dot_general x2, matrix products, mm(): lax.dot_general(a, b, (dims, ((), ())), precision=precision, preferred_el...  15.8 us
    pallas_call x1, Pallas kernels, inverse_factor(): pl.pallas_call(inverse_kernel, out_shape=jax.ShapeDtypeStruct(gram.shape,...  13.6 us
    unnamed x39, local copies, waits for them, and re-layouts  12.5 us
  transfers between devices with their start and end apart: 47, of which 18 were waited for; matrix products, arithmetic and copies ran while one was open for 6% of the time, Pallas kernels for 24%

profile of v6, /device:TPU:0, one launch (start us, length us, event | category | flops | bytes accessed | tf_op | source)
XLA Modules:
  0.0 402.1 jit_solution(12127710208749906114)
XLA Ops:
  0.6 2.3 copy.9
  3.0 3.1 collective-permute-start
  7.5 13.5 %collective-permute-done.refs_1_.refs_6_ = bf16[1280,256]{1,0:T(8,128)(2,1)} collective-permute-done((bf16[1280,256]{1,0:T(8,128)(2,1)}, bf16[1280,256]{1,0:T(8,128)(2,1)}, u32[]{:S(2)}, u32[]{:S(2)}) %collective-permute-start) | collective-permute-done | bytes 655392 | tf_op jit(solution)/shard_map/ppermute | solution.py:289
  22.5 4.6 %fusion.6 = f32[512,256]{1,0:T(8,128)} fusion(bf16[512,3200]{1,0:T(8,128)(2,1)} %inputs.1, f32[3200,256]{1,0:T(8,128)S(1)} %copy-done), kind=kOutput, calls=%fused_computation.15 | convolution fusion | flops 2516582400 | bytes 7077888 | tf_op jit(solution)/shard_map/dot_general | solution.py:22
  37.3 11.2 %fusion.5.part = f32[1280,256]{1,0:T(8,128)} fusion(f32[1280,3200]{1,0:T(8,128)} %refs_9_.1, f32[3200,256]{1,0:T(8,128)S(1)} %copy-done), kind=kOutput, calls=%fused_computation.14 | convolution fusion | flops 6291456000 | bytes 20971520 | tf_op jit(solution)/shard_map/dot_general | solution.py:22
  48.6 6.9 %collective-permute-done.3.refs_4_ = bf16[1280,256]{1,0:T(8,128)(2,1)} collective-permute-done((bf16[1280,256]{1,0:T(8,128)(2,1)}, bf16[1280,256]{1,0:T(8,128)(2,1)}, u32[]{:S(2)}, u32[]{:S(2)}) %collective-permute-start.3) | collective-permute-done | bytes 655392 | tf_op jit(solution)/shard_map/ppermute | solution.py:298
  55.4 12.7 %collective-permute-done.4.refs_5_ = bf16[1280,256]{1,0:T(8,128)(2,1)} collective-permute-done((bf16[1280,256]{1,0:T(8,128)(2,1)}, bf16[1280,256]{1,0:T(8,128)(2,1)}, u32[]{:S(2)}, u32[]{:S(2)}) %collective-permute-start.4) | collective-permute-done | bytes 655392 | tf_op jit(solution)/shard_map/ppermute | solution.py:298
  69.4 4.7 %shard_map.76 = (f32[640,256]{1,0:T(8,128)S(1)}, f32[640,256]{1,0:T(8,128)S(1)}) custom-call(s32[4]{0:T(128)S(1)} %pad_add_fusion.ids, f32[1280,256]{1,0:T(8,128)S(1)} %copy-done.5, bf16[1280,256]{1,0:T(8,128)(2,1)} %bitcast.4.refs_0_.refs_5_, bf16[1280,256]{1,0:T(8,128)(2,1)} %collective-permute-done.refs_1_.refs_6_, ...), custom_call_target="tpu_custom_call" | custom-call | flops 1342177280 | bytes 8000000 | tf_op jit(solution)/shard_map/pallas_call | solution.py:121
  76.5 2.9 collective-permute-start.11
  80.9 4.8 %collective-permute-done.10 = f32[160,256]{1,0:T(8,128)S(1)} collective-permute-done((f32[160,256]{1,0:T(8,128)S(1)}, f32[160,256]{1,0:T(8,128)S(1)}, u32[]{:S(2)}, u32[]{:S(2)}) %collective-permute-start.10) | collective-permute-done | bytes 163872 | tf_op jit(solution)/shard_map/ppermute | solution.py:289
  85.7 5.9 %collective-permute-done.11 = f32[160,256]{1,0:T(8,128)S(1)} collective-permute-done((f32[160,256]{1,0:T(8,128)S(1)}, f32[160,256]{1,0:T(8,128)S(1)}, u32[]{:S(2)}, u32[]{:S(2)}) %collective-permute-start.11) | collective-permute-done | bytes 163872 | tf_op jit(solution)/shard_map/ppermute | solution.py:289
  91.6 3.3 collective-permute-start.13
  97.4 3.3 collective-permute-done.13.refs_1_
  100.7 9.1 %collective-permute-done.14.refs_2_ = f32[160,256]{1,0:T(8,128)S(1)} collective-permute-done((f32[160,256]{1,0:T(8,128)S(1)}, f32[160,256]{1,0:T(8,128)S(1)}, u32[]{:S(2)}, u32[]{:S(2)}) %collective-permute-start.14) | collective-permute-done | bytes 163872 | tf_op jit(solution)/shard_map/ppermute | solution.py:289
  112.8 4.4 %shard_map.77 = (f32[1280,256]{1,0:T(8,128)S(1)}, f32[256,256]{1,0:T(8,128)S(1)}, f32[256,256]{1,0:T(8,128)S(1)}, f32[256,256]{1,0:T(8,128)S(1)}, f32[256,256]{1...) custom-call(s32[4]{0:T(128)S(1)} %pad_add_fusion.ids, ...), custom_call_target="tpu_custom_call" | custom-call | flops 1677721600 | bytes 8000000 | tf_op jit(solution)/shard_map/pallas_call | solution.py:121
  120.8 5.7 %collective-permute-done.19 = f32[256,256]{1,0:T(8,128)S(1)} collective-permute-done((f32[256,256]{1,0:T(8,128)S(1)}, f32[256,256]{1,0:T(8,128)S(1)}, u32[]{:S(2)}, u32[]{:S(2)}) %collective-permute-start.19) | collective-permute-done | bytes 262176 | tf_op jit(solution)/shard_map/ppermute | solution.py:289
  126.5 6.4 %collective-permute-done.20 = f32[256,256]{1,0:T(8,128)S(1)} collective-permute-done((f32[256,256]{1,0:T(8,128)S(1)}, f32[256,256]{1,0:T(8,128)S(1)}, u32[]{:S(2)}, u32[]{:S(2)}) %collective-permute-start.20) | collective-permute-done | bytes 262176 | tf_op jit(solution)/shard_map/ppermute | solution.py:289
  133.0 12.5 %shard_map.79 = (f32[64,3200]{1,0:T(8,128)S(1)}, f32[64,3200]{1,0:T(8,128)S(1)}, f32[64,3200]{1,0:T(8,128)S(1)}, f32[64,3200]{1,0:T(8,128)S(1)}) custom-call(bf16[256,1280]{1,0:T(8,128)(2,1)S(1)} %get-tuple-element.34.big_t, bf16[256,1280]{1,0:T(8,128)(2,1)S(1)} %get-tuple-element.35.low_t, f32[1280,3200]{1,0:T(8,128)} %refs_9_.1), custom_call_target="tpu_custom_call" | custom-call | flops 6291456000 | bytes 20480000 | tf_op jit(solution)/shard_map/pallas_call | solution.py:121
  145.6 7.0 %shard_map.80 = (f32[64,3200]{1,0:T(8,128)S(1)}, f32[64,3200]{1,0:T(8,128)S(1)}, f32[64,3200]{1,0:T(8,128)S(1)}, f32[64,3200]{1,0:T(8,128)S(1)}) custom-call(s32[4]{0:T(128)S(1)} %pad_add_fusion.ids, f32[256,256]{1,0:T(8,128)S(1)} %add_add_fusion.own, f32[256,256]{1,0:T(8,128)S(1)} %collective-permute-done.22.other, bf16[512,3200]{1,0:T(8,128)(2,1)S(1)} %copy-done.4, ...), custom_call_target="tpu_custom_call" | custom-call | flops 1677721600 | bytes 8192000 | tf_op jit(solution)/shard_map/pallas_call | solution.py:121
  157.0 16.2 %collective-permute-done.26 = f32[64,3200]{1,0:T(8,128)S(1)} collective-permute-done((f32[64,3200]{1,0:T(8,128)S(1)}, f32[64,3200]{1,0:T(8,128)S(1)}, u32[]{:S(2)}, u32[]{:S(2)}) %collective-permute-start.26) | collective-permute-done | bytes 819232 | tf_op jit(solution)/shard_map/ppermute | solution.py:289
  176.0 34.7 %collective-permute-done.23 = f32[64,3200]{1,0:T(8,128)S(1)} collective-permute-done((f32[64,3200]{1,0:T(8,128)S(1)}, f32[64,3200]{1,0:T(8,128)S(1)}, u32[]{:S(2)}, u32[]{:S(2)}) %collective-permute-start.23) | collective-permute-done | bytes 819232 | tf_op jit(solution)/shard_map/ppermute | solution.py:289
  213.1 15.1 %collective-permute-done.27 = f32[64,3200]{1,0:T(8,128)S(1)} collective-permute-done((f32[64,3200]{1,0:T(8,128)S(1)}, f32[64,3200]{1,0:T(8,128)S(1)}, u32[]{:S(2)}, u32[]{:S(2)}) %collective-permute-start.27) | collective-permute-done | bytes 819232 | tf_op jit(solution)/shard_map/ppermute | solution.py:289
  235.7 32.5 %collective-permute-done.17 = f32[256,256]{1,0:T(8,128)S(1)} collective-permute-done((f32[256,256]{1,0:T(8,128)S(1)}, f32[256,256]{1,0:T(8,128)S(1)}, u32[]{:S(2)}, u32[]{:S(2)}) %collective-permute-start.17) | collective-permute-done | bytes 262176 | tf_op jit(solution)/shard_map/ppermute | solution.py:289
  270.4 18.6 %shard_map.83.refs_9_ = f32[1280,3200]{1,0:T(8,128)} custom-call(s32[4]{0:T(128)S(1)} %pad_add_fusion.ids, bf16[4,1280,256]{2,1,0:T(8,128)(2,1)S(1)} %pad_maximum_fusion.refs_0_.refs_1_.own, bf16[4,1280,256]{2,1,0:T(8,128)(2,1)S(1)} %pad_maximum_fusion.refs_0_.refs_1_.own, bf16[4,1280,256]{2,1,0:T(8,128)(2,1)S(1)} %pad_maximum_fusion.1.refs_2_.refs_3_.other, ...), custom_call_target="tpu_custom_call" | custom-call | flops 8388608000 | bytes 32768000 | tf_op jit(solution)/shard_map/pallas_call | solution.py:121
  289.0 3.0 collective-permute-done.18
  299.6 13.6 %shard_map.78.inverse = f32[256,256]{1,0:T(8,128)} custom-call(f32[256,256]{1,0:T(8,128)} %add.82.gram_ref), custom_call_target="tpu_custom_call" | custom-call | flops 20000000000 | bytes 10000000 | tf_op jit(solution)/shard_map/pallas_call | solution.py:95
  320.2 7.4 %shard_map.81 = (f32[256,3200]{1,0:T(8,128)S(1)}, f32[8,256]{1,0:T(8,128)S(1)}, f32[1280,256]{1,0:T(8,128)S(1)}) custom-call(s32[4]{0:T(128)S(1)} %pad_add_fusion.ids, f32[256,256]{1,0:T(8,128)S(1)} %copy-done.16, f32[1280,256]{1,0:T(8,128)S(1)} %copy-done.11, f32[64,3200]{1,0:T(8,128)S(1)} %copy-done.9, f32[64,3200]{1,0:T(8,128)S(1)} %copy-done.15, ...), custom_call_target="tpu_custom_call" | custom-call | flops 1258291200 | bytes 9830400 | tf_op jit(solution)/shard_map/pallas_call | solution.py:121
  327.6 20.8 %collective-permute-done.44.refs_7_ = bf16[128,3200]{1,0:T(8,128)(2,1)} collective-permute-done((bf16[128,3200]{1,0:T(8,128)(2,1)}, bf16[128,3200]{1,0:T(8,128)(2,1)}, u32[]{:S(2)}, u32[]{:S(2)}) %collective-permute-start.44) | collective-permute-done | bytes 819232 | tf_op jit(solution)/shard_map/ppermute | solution.py:289
  348.5 19.7 %shard_map.84.base = f32[1280,3200]{1,0:T(8,128)} custom-call(s32[4]{0:T(128)S(1)} %pad_add_fusion.ids, bf16[4,1280,256]{2,1,0:T(8,128)(2,1)S(1)} %pad_maximum_fusion.refs_0_.refs_1_.own, bf16[4,1280,256]{2,1,0:T(8,128)(2,1)S(1)} %pad_maximum_fusion.refs_0_.refs_1_.own, bf16[4,1280,256]{2,1,0:T(8,128)(2,1)S(1)} %copy-done.3, ...), custom_call_target="tpu_custom_call" | custom-call | flops 6291456000 | bytes 32768000 | tf_op jit(solution)/shard_map/pallas_call | solution.py:121
  368.2 2.4 collective-permute-start.30
  373.1 17.4 %shard_map.85 = f32[1280,3200]{1,0:T(8,128)} custom-call(s32[4]{0:T(128)S(1)} %pad_add_fusion.ids, bf16[4,1280,256]{2,1,0:T(8,128)(2,1)S(1)} %pad_maximum_fusion.refs_0_.refs_1_.own, bf16[4,1280,256]{2,1,0:T(8,128)(2,1)S(1)} %copy-done.3, bf16[128,3200]{1,0:T(8,128)(2,1)} %collective-permute-done.38.first, ...), custom_call_target="tpu_custom_call", output_to_operand_aliasing={{}: (7, {})} | custom-call | flops 4194304000 | bytes 32768000 | tf_op jit(solution)/shard_map/pallas_call | solution.py:121
  390.5 11.6 %shard_map.82 = (f32[1280,3200]{1,0:T(8,128)}, f32[3200,256]{1,0:T(8,128)}) custom-call(f32[8,256]{1,0:T(8,128)S(1)} %add_add_fusion.1.squares, f32[1280,256]{1,0:T(8,128)S(1)} %get-tuple-element.45.basis, f32[256,3200]{1,0:T(8,128)S(1)} %get-tuple-element.46.right, bf16[1280,3200]{1,0:T(8,128)(2,1)S(1)} %bitcast.21), custom_call_target="tpu_custom_call" | custom-call | flops 6291456000 | bytes 24576000 | tf_op jit(solution)/shard_map/pallas_call | solution.py:121
  (136 shorter events, 63.9 us)
Async XLA Ops:
  3.0 18.1 %collective-permute-start = (bf16[1280,256]{1,0:T(8,128)(2,1)}, bf16[1280,256]{1,0:T(8,128)(2,1)}, u32[]{:S(2)}, u32[]{:S(2)}) collective-permute-start(bf16[1280,256]{1,0:T(8,128)(2,1)} %bitcast.4.refs_0_.refs_5_), channel_id=1, source_target_pairs={{0,2},{1,3},{2,0},{3,1},{4,6},{5,7},{6,4},{7,5},{8,10},{9,11},{10,... | collective-permute-start | bytes 1966088 | tf_op jit(solution)/shard_map/ppermute | solution.py:289
  6.0 28.5 %collective-permute-start.1 = (bf16[1280,256]{1,0:T(8,128)(2,1)}, bf16[1280,256]{1,0:T(8,128)(2,1)}, u32[]{:S(2)}, u32[]{:S(2)}) collective-permute-start(bf16[1280,256]{1,0:T(8,128)(2,1)} %bitcast.4.refs_0_.refs_5_), channel_id=1, source_target_pairs={{2,4},{3,5},{4,2},{5,3},{10,12},{11,13},{12,10},{13,11},{18,20},{1... | collective-permute-start | bytes 1966088 | tf_op jit(solution)/shard_map/ppermute | solution.py:298
  31.0 17.6 %collective-permute-start.6 = (f32[256,256]{1,0:T(8,128)S(1)}, f32[256,256]{1,0:T(8,128)}, u32[]{:S(2)}, u32[]{:S(2)}) collective-permute-start(f32[256,256]{1,0:T(8,128)S(1)} %dynamic-slice_add_fusion.refs_6_), channel_id=1, source_target_pairs={{0,8},{8,0},{16,24},{24,16},{1,9},{9,1},{17,25},{25,17},{2,10},{10... | collective-permute-start | bytes 786440 | tf_op jit(solution)/shard_map/ppermute | solution.py:289
  32.7 15.9 %collective-permute-start.7 = (f32[256,256]{1,0:T(8,128)S(1)}, f32[256,256]{1,0:T(8,128)}, u32[]{:S(2)}, u32[]{:S(2)}) collective-permute-start(f32[256,256]{1,0:T(8,128)S(1)} %dynamic-slice_add_fusion.refs_6_), channel_id=1, source_target_pairs={{0,16},{8,24},{16,0},{24,8},{1,17},{9,25},{17,1},{25,9},{2,18},{10... | collective-permute-start | bytes 786440 | tf_op jit(solution)/shard_map/ppermute | solution.py:289
  34.5 20.9 %collective-permute-start.3 = (bf16[1280,256]{1,0:T(8,128)(2,1)}, bf16[1280,256]{1,0:T(8,128)(2,1)}, u32[]{:S(2)}, u32[]{:S(2)}) collective-permute-start(bf16[1280,256]{1,0:T(8,128)(2,1)} %collective-permute-done.1.refs_2_), channel_id=1, source_target_pairs={{2,0},{3,1},{4,6},{5,7},{10,8},{11,9},{12,14},{13,15},{18,16},{19,... | collective-permute-start | bytes 1966088 | tf_op jit(solution)/shard_map/ppermute | solution.py:298
  35.8 32.3 %collective-permute-start.4 = (bf16[1280,256]{1,0:T(8,128)(2,1)}, bf16[1280,256]{1,0:T(8,128)(2,1)}, u32[]{:S(2)}, u32[]{:S(2)}) collective-permute-start(bf16[1280,256]{1,0:T(8,128)(2,1)} %collective-permute-done.2.refs_3_), channel_id=1, source_target_pairs={{2,0},{3,1},{4,6},{5,7},{10,8},{11,9},{12,14},{13,15},{18,16},{19,... | collective-permute-start | bytes 1966088 | tf_op jit(solution)/shard_map/ppermute | solution.py:298
  76.5 15.1 %collective-permute-start.11 = (f32[160,256]{1,0:T(8,128)S(1)}, f32[160,256]{1,0:T(8,128)S(1)}, u32[]{:S(2)}, u32[]{:S(2)}) collective-permute-start(f32[160,256]{1,0:T(8,128)S(1)} %get-tuple-element.57), channel_id=1, source_target_pairs={{0,4},{1,5},{2,6},{3,7},{4,0},{5,1},{6,2},{7,3},{8,12},{9,13},{10,... | collective-permute-start | bytes 491528 | tf_op jit(solution)/shard_map/ppermute | solution.py:289
  120.8 90.5 %collective-permute-start.33 = (bf16[1280,256]{1,0:T(8,128)(2,1)}, bf16[1280,256]{1,0:T(8,128)(2,1)S(1)}, u32[]{:S(2)}, u32[]{:S(2)}) collective-permute-start(bf16[1280,256]{1,0:T(8,128)(2,1)} %bitcast.4.refs_0_.refs_5_), channel_id=1, source_target_pairs={{0,1},{1,0},{2,3},{3,2},{4,5},{5,4},{6,7},{7,6},{8,9},{9,8},{10,11... | collective-permute-start | bytes 1966088 | tf_op jit(solution)/shard_map/ppermute | solution.py:289
  152.5 20.7 %collective-permute-start.26 = (f32[64,3200]{1,0:T(8,128)S(1)}, f32[64,3200]{1,0:T(8,128)S(1)}, u32[]{:S(2)}, u32[]{:S(2)}) collective-permute-start(f32[64,3200]{1,0:T(8,128)S(1)} %get-tuple-element.43), channel_id=1, source_target_pairs={{0,16},{8,24},{16,0},{24,8},{1,17},{9,25},{17,1},{25,9},{2,18},{10... | collective-permute-start | bytes 2457608 | tf_op jit(solution)/shard_map/ppermute | solution.py:289
  154.4 58.2 %collective-permute-start.37 = (bf16[128,3200]{1,0:T(8,128)(2,1)S(1)}, bf16[128,3200]{1,0:T(8,128)(2,1)}, u32[]{:S(2)}, u32[]{:S(2)}) collective-permute-start(bf16[128,3200]{1,0:T(8,128)(2,1)S(1)} %get-tuple-element.54), channel_id=1, source_target_pairs={{0,8},{8,0},{16,24},{24,16},{1,9},{9,1},{17,25},{25,17},{2,10},{10... | collective-permute-start | bytes 2457608 | tf_op jit(solution)/shard_map/ppermute | solution.py:289
  155.0 57.6 %collective-permute-start.43 = (bf16[128,3200]{1,0:T(8,128)(2,1)S(1)}, bf16[128,3200]{1,0:T(8,128)(2,1)}, u32[]{:S(2)}, u32[]{:S(2)}) collective-permute-start(bf16[128,3200]{1,0:T(8,128)(2,1)S(1)} %get-tuple-element.51), channel_id=1, source_target_pairs={{0,8},{8,0},{16,24},{24,16},{1,9},{9,1},{17,25},{25,17},{2,10},{10... | collective-permute-start | bytes 2457608 | tf_op jit(solution)/shard_map/ppermute | solution.py:289
  156.5 54.2 %collective-permute-start.23 = (f32[64,3200]{1,0:T(8,128)S(1)}, f32[64,3200]{1,0:T(8,128)S(1)}, u32[]{:S(2)}, u32[]{:S(2)}) collective-permute-start(f32[64,3200]{1,0:T(8,128)S(1)} %get-tuple-element.41), channel_id=1, source_target_pairs={{0,8},{8,0},{16,24},{24,16},{1,9},{9,1},{17,25},{25,17},{2,10},{10... | collective-permute-start | bytes 2457608 | tf_op jit(solution)/shard_map/ppermute | solution.py:289
  173.3 54.9 %collective-permute-start.27 = (f32[64,3200]{1,0:T(8,128)S(1)}, f32[64,3200]{1,0:T(8,128)S(1)}, u32[]{:S(2)}, u32[]{:S(2)}) collective-permute-start(f32[64,3200]{1,0:T(8,128)S(1)} %add.88), channel_id=1, source_target_pairs={{0,8},{8,0},{16,24},{24,16},{1,9},{9,1},{17,25},{25,17},{2,10},{10... | collective-permute-start | bytes 2457608 | tf_op jit(solution)/shard_map/ppermute | solution.py:289
  210.7 58.4 %collective-permute-start.46 = (bf16[256,3200]{1,0:T(8,128)(2,1)S(1)}, bf16[256,3200]{1,0:T(8,128)(2,1)S(1)}, u32[]{:S(2)}, u32[]{:S(2)}) collective-permute-start(bf16[256,3200]{1,0:T(8,128)(2,1)S(1)} %get-tuple-element.49.refs_5_), channel_id=1, source_target_pairs={{0,8},{8,0},{16,24},{24,16},{1,9},{9,1},{17,25},{25,17},{2,10},{10... | collective-permute-start | bytes 4915208 | tf_op jit(solution)/shard_map/ppermute | solution.py:289
  211.3 18.5 %collective-permute-start.24 = (f32[64,3200]{1,0:T(8,128)S(1)}, f32[64,3200]{1,0:T(8,128)S(1)}, u32[]{:S(2)}, u32[]{:S(2)}) collective-permute-start(f32[64,3200]{1,0:T(8,128)S(1)} %add.86), channel_id=1, source_target_pairs={{0,16},{8,24},{16,0},{24,8},{1,17},{9,25},{17,1},{25,9},{2,18},{10... | collective-permute-start | bytes 2457608 | tf_op jit(solution)/shard_map/ppermute | solution.py:289
  212.6 20.5 %collective-permute-start.34 = (bf16[1280,256]{1,0:T(8,128)(2,1)}, bf16[1280,256]{1,0:T(8,128)(2,1)S(1)}, u32[]{:S(2)}, u32[]{:S(2)}) collective-permute-start(bf16[1280,256]{1,0:T(8,128)(2,1)} %collective-permute-done.refs_1_.refs_6_), channel_id=1, source_target_pairs={{0,1},{1,0},{2,3},{3,2},{4,5},{5,4},{6,7},{7,6},{8,9},{9,8},{10,11... | collective-permute-start | bytes 1966088 | tf_op jit(solution)/shard_map/ppermute | solution.py:289
  212.6 21.1 %collective-permute-start.35 = (bf16[1280,256]{1,0:T(8,128)(2,1)S(1)}, bf16[1280,256]{1,0:T(8,128)(2,1)S(1)}, u32[]{:S(2)}, u32[]{:S(2)}) collective-permute-start(bf16[1280,256]{1,0:T(8,128)(2,1)S(1)} %add.79.refs_7_), channel_id=1, source_target_pairs={{0,1},{1,0},{2,3},{3,2},{4,5},{5,4},{6,7},{7,6},{8,9},{9,8},{10,11... | collective-permute-start | bytes 1966088 | tf_op jit(solution)/shard_map/ppermute | solution.py:289
  229.8 38.4 %collective-permute-start.17 = (f32[256,256]{1,0:T(8,128)S(1)}, f32[256,256]{1,0:T(8,128)S(1)}, u32[]{:S(2)}, u32[]{:S(2)}) collective-permute-start(f32[256,256]{1,0:T(8,128)S(1)} %get-tuple-element.28), channel_id=1, source_target_pairs={{0,8},{8,0},{16,24},{24,16},{1,9},{9,1},{17,25},{25,17},{2,10},{10... | collective-permute-start | bytes 786440 | tf_op jit(solution)/shard_map/ppermute | solution.py:289
  233.1 60.6 %collective-permute-start.42 = (bf16[128,3200]{1,0:T(8,128)(2,1)S(1)}, bf16[128,3200]{1,0:T(8,128)(2,1)}, u32[]{:S(2)}, u32[]{:S(2)}) collective-permute-start(bf16[128,3200]{1,0:T(8,128)(2,1)S(1)} %get-tuple-element.52), channel_id=1, source_target_pairs={{0,16},{8,24},{16,0},{24,8},{1,17},{9,25},{17,1},{25,9},{2,18},{10... | collective-permute-start | bytes 2457608 | tf_op jit(solution)/shard_map/ppermute | solution.py:289
  233.7 61.1 %collective-permute-start.39 = (bf16[128,3200]{1,0:T(8,128)(2,1)S(1)}, bf16[128,3200]{1,0:T(8,128)(2,1)}, u32[]{:S(2)}, u32[]{:S(2)}) collective-permute-start(bf16[128,3200]{1,0:T(8,128)(2,1)S(1)} %get-tuple-element.53), channel_id=1, source_target_pairs={{0,16},{8,24},{16,0},{24,8},{1,17},{9,25},{17,1},{25,9},{2,18},{10... | collective-permute-start | bytes 2457608 | tf_op jit(solution)/shard_map/ppermute | solution.py:289
  235.2 60.6 %collective-permute-start.28 = (f32[64,3200]{1,0:T(8,128)S(1)}, f32[64,3200]{1,0:T(8,128)S(1)}, u32[]{:S(2)}, u32[]{:S(2)}) collective-permute-start(f32[64,3200]{1,0:T(8,128)S(1)} %add.89.refs_2_), channel_id=1, source_target_pairs={{0,16},{8,24},{16,0},{24,8},{1,17},{9,25},{17,1},{25,9},{2,18},{10... | collective-permute-start | bytes 2457608 | tf_op jit(solution)/shard_map/ppermute | solution.py:289
  268.2 29.3 %collective-permute-start.25 = (f32[64,3200]{1,0:T(8,128)S(1)}, f32[64,3200]{1,0:T(8,128)S(1)}, u32[]{:S(2)}, u32[]{:S(2)}) collective-permute-start(f32[64,3200]{1,0:T(8,128)S(1)} %add.87.refs_0_), channel_id=1, source_target_pairs={{0,8},{8,0},{16,24},{24,16},{1,9},{9,1},{17,25},{25,17},{2,10},{10... | collective-permute-start | bytes 2457608 | tf_op jit(solution)/shard_map/ppermute | solution.py:289
  269.1 22.8 %collective-permute-start.18 = (f32[256,256]{1,0:T(8,128)S(1)}, f32[256,256]{1,0:T(8,128)S(1)}, u32[]{:S(2)}, u32[]{:S(2)}) collective-permute-start(f32[256,256]{1,0:T(8,128)S(1)} %add.81), channel_id=1, source_target_pairs={{0,16},{8,24},{16,0},{24,8},{1,17},{9,25},{17,1},{25,9},{2,18},{10... | collective-permute-start | bytes 786440 | tf_op jit(solution)/shard_map/ppermute | solution.py:289
  291.9 56.6 %collective-permute-start.41 = (bf16[256,3200]{1,0:T(8,128)(2,1)}, bf16[256,3200]{1,0:T(8,128)(2,1)}, u32[]{:S(2)}, u32[]{:S(2)}) collective-permute-start(bf16[256,3200]{1,0:T(8,128)(2,1)} %get-tuple-element.50.refs_4_), channel_id=1, source_target_pairs={{0,16},{8,24},{16,0},{24,8},{1,17},{9,25},{17,1},{25,9},{2,18},{10... | collective-permute-start | bytes 4915208 | tf_op jit(solution)/shard_map/ppermute | solution.py:289
  293.7 54.8 %collective-permute-start.44 = (bf16[128,3200]{1,0:T(8,128)(2,1)}, bf16[128,3200]{1,0:T(8,128)(2,1)}, u32[]{:S(2)}, u32[]{:S(2)}) collective-permute-start(bf16[128,3200]{1,0:T(8,128)(2,1)} %collective-permute-done.43.refs_6_), channel_id=1, source_target_pairs={{0,16},{8,24},{16,0},{24,8},{1,17},{9,25},{17,1},{25,9},{2,18},{10... | collective-permute-start | bytes 2457608 | tf_op jit(solution)/shard_map/ppermute | solution.py:289
  294.7 78.3 %collective-permute-start.38 = (bf16[128,3200]{1,0:T(8,128)(2,1)}, bf16[128,3200]{1,0:T(8,128)(2,1)}, u32[]{:S(2)}, u32[]{:S(2)}) collective-permute-start(bf16[128,3200]{1,0:T(8,128)(2,1)} %collective-permute-done.37.refs_7_), channel_id=1, source_target_pairs={{0,16},{8,24},{16,0},{24,8},{1,17},{9,25},{17,1},{25,9},{2,18},{10... | collective-permute-start | bytes 2457608 | tf_op jit(solution)/shard_map/ppermute | solution.py:289
  296.7 51.8 %collective-permute-start.45 = (bf16[128,3200]{1,0:T(8,128)(2,1)}, bf16[128,3200]{1,0:T(8,128)(2,1)}, u32[]{:S(2)}, u32[]{:S(2)}) collective-permute-start(bf16[128,3200]{1,0:T(8,128)(2,1)} %collective-permute-done.42.refs_5_), channel_id=1, source_target_pairs={{0,8},{8,0},{16,24},{24,16},{1,9},{9,1},{17,25},{25,17},{2,10},{10... | collective-permute-start | bytes 2457608 | tf_op jit(solution)/shard_map/ppermute | solution.py:289
  298.4 74.7 %collective-permute-start.40 = (bf16[128,3200]{1,0:T(8,128)(2,1)}, bf16[128,3200]{1,0:T(8,128)(2,1)}, u32[]{:S(2)}, u32[]{:S(2)}) collective-permute-start(bf16[128,3200]{1,0:T(8,128)(2,1)} %collective-permute-done.39.refs_6_), channel_id=1, source_target_pairs={{0,8},{8,0},{16,24},{24,16},{1,9},{9,1},{17,25},{25,17},{2,10},{10... | collective-permute-start | bytes 2457608 | tf_op jit(solution)/shard_map/ppermute | solution.py:289
  348.5 19.7 %collective-permute-start.29 = (f32[8,256]{1,0:T(8,128)S(1)}, f32[8,256]{1,0:T(8,128)S(1)}, u32[]{:S(2)}, u32[]{:S(2)}) collective-permute-start(f32[8,256]{1,0:T(8,128)S(1)} %get-tuple-element.44), channel_id=1, source_target_pairs={{0,1},{1,0},{2,3},{3,2},{4,5},{5,4},{6,7},{7,6},{8,9},{9,8},{10,11... | collective-permute-start | bytes 24584 | tf_op jit(solution)/shard_map/ppermute | solution.py:289
  368.2 22.3 %collective-permute-start.30 = (f32[8,256]{1,0:T(8,128)S(1)}, f32[8,256]{1,0:T(8,128)S(1)}, u32[]{:S(2)}, u32[]{:S(2)}) collective-permute-start(f32[8,256]{1,0:T(8,128)S(1)} %add.90), channel_id=1, source_target_pairs={{0,2},{1,3},{2,0},{3,1},{4,6},{5,7},{6,4},{7,5},{8,10},{9,11},{10,... | collective-permute-start | bytes 24584 | tf_op jit(solution)/shard_map/ppermute | solution.py:289
  370.6 19.8 %collective-permute-start.31 = (f32[8,256]{1,0:T(8,128)S(1)}, f32[8,256]{1,0:T(8,128)S(1)}, u32[]{:S(2)}, u32[]{:S(2)}) collective-permute-start(f32[8,256]{1,0:T(8,128)S(1)} %add.90), channel_id=1, source_target_pairs={{0,4},{1,5},{2,6},{3,7},{4,0},{5,1},{6,2},{7,3},{8,12},{9,13},{10,... | collective-permute-start | bytes 24584 | tf_op jit(solution)/shard_map/ppermute | solution.py:289
  371.6 18.9 %collective-permute-start.32 = (f32[8,256]{1,0:T(8,128)S(1)}, f32[8,256]{1,0:T(8,128)S(1)}, u32[]{:S(2)}, u32[]{:S(2)}) collective-permute-start(f32[8,256]{1,0:T(8,128)S(1)} %add.90), channel_id=1, source_target_pairs={{0,6},{1,7},{2,4},{3,5},{4,2},{5,3},{6,0},{7,1},{8,14},{9,15},{10,... | collective-permute-start | bytes 24584 | tf_op jit(solution)/shard_map/ppermute | solution.py:289
  (34 other events, 462.0 us)

commit v7 on v6

--- a/solution.py
+++ b/solution.py
@@ -224,11 +224,15 @@
     own, other, pieces = refs[:count], refs[count : 2 * count], list(refs[2 * count : -2])
     base, out = refs[-2], refs[-1]
     total = base[...]
-    for at, number in enumerate(numbers):
-        x = jnp.concatenate([pieces.pop(0)[...] for _ in range(number)], axis=0)
-        cut = cuts[at // 2]
-        grad = jnp.where(ids[2] == at % 2, own[at // 2][0, :, cut], other[at // 2][0, :, cut])
-        total += mm(grad, x, ((1,), (0,)))
+    for j, cut in enumerate(cuts):
+        x = [jnp.concatenate([pieces.pop(0)[...] for _ in range(numbers[2 * j + h])], axis=0) for h in range(2)]
+        mine, its = own[j][0, :, cut], other[j][0, :, cut]
+        grads = [jnp.where(ids[2] == 0, mine, its), jnp.where(ids[2] == 0, its, mine)]
+        if cut == slice(None):
+            total += mm(grads[0], x[0], ((1,), (0,)))
+            total += mm(grads[1], x[1], ((1,), (0,)))
+        else:
+            total += mm(jnp.concatenate(grads, axis=1), jnp.concatenate(x, axis=0), ((1,), (0,)))
     out[...] = total
 
 
@@ -279,8 +283,8 @@
         small[...] = (basis[...] * -(1.0 - mix_rate)).astype(bf16)
 
     mine, its = own[0, :, cut], other[0, :, cut]
-    total = base[...] + mm(jnp.where(ids[2] == 0, mine, its), first[...], ((1,), (0,)))
-    total += mm(jnp.where(ids[2] == 0, its, mine), second[...], ((1,), (0,)))
+    grads = jnp.concatenate([jnp.where(ids[2] == 0, mine, its), jnp.where(ids[2] == 0, its, mine)], axis=1)
+    total = base[...] + mm(grads, jnp.concatenate([first[...], second[...]], axis=0), ((1,), (0,)))
     out[...] = total + mm(small[...], right[...].astype(bf16), ((1,), (0,)))
 
 

time: 403 us -> 400 us (level)
  transfers between devices with their start and end apart: 47 -> 47, of which waited for: 18 -> 18; matrix products, arithmetic and copies ran while one was open for 6% -> 6% of each run, Pallas kernels for 24% -> 23%
where the time goes in v7:
time: 400 us; the launch traced here: 399 us
  waiting for transfers between devices  196 us (49%)
  Pallas kernels  114 us (28%)
  starting transfers between devices  50.1 us (13%)
  matrix products  15.8 us (4%)
  local copies, waits for them, and re-layouts  15.2 us (4%)
  other arithmetic  7.36 us (2%)
    ppermute x43, waiting for transfers between devices, swap(): return lax.ppermute(x, axis, [(i, i ^ bit) for i in range(size)])  176 us
    pallas_call x9, Pallas kernels, call(): pl.pallas_call(kernel, out_shape=outs, grid_spec=pltpu.PrefetchScalarGrid...  101 us
    ppermute x43, starting transfers between devices, swap(): return lax.ppermute(x, axis, [(i, i ^ bit) for i in range(size)])  44.3 us
    ppermute x4, waiting for transfers between devices, line(): lax.ppermute(x, 'col', [(2 * a + h, 2 * b + h) for a, b in steps for h in...  19.5 us
    dot_general x2, matrix products, mm(): lax.dot_general(a, b, (dims, ((), ())), precision=precision, preferred_el...  15.8 us
    pallas_call x1, Pallas kernels, inverse_factor(): pl.pallas_call(inverse_kernel, out_shape=jax.ShapeDtypeStruct(gram.shape,...  13.6 us
    unnamed x39, local copies, waits for them, and re-layouts  12.5 us
  transfers between devices with their start and end apart: 47, of which 18 were waited for; matrix products, arithmetic and copies ran while one was open for 6% of the time, Pallas kernels for 23%

profile of v7, /device:TPU:0, one launch (start us, length us, event | category | flops | bytes accessed | tf_op | source)
XLA Modules:
  0.0 399.5 jit_solution(6008332797525267925)
XLA Ops:
  0.6 2.3 copy.9
  3.0 3.1 collective-permute-start
  7.5 13.5 %collective-permute-done.refs_1_.refs_6_ = bf16[1280,256]{1,0:T(8,128)(2,1)} collective-permute-done((bf16[1280,256]{1,0:T(8,128)(2,1)}, bf16[1280,256]{1,0:T(8,128)(2,1)}, u32[]{:S(2)}, u32[]{:S(2)}) %collective-permute-start) | collective-permute-done | bytes 655392 | tf_op jit(solution)/shard_map/ppermute | solution.py:293
  22.5 4.6 %fusion.6 = f32[512,256]{1,0:T(8,128)} fusion(bf16[512,3200]{1,0:T(8,128)(2,1)} %inputs.1, f32[3200,256]{1,0:T(8,128)S(1)} %copy-done), kind=kOutput, calls=%fused_computation.15 | convolution fusion | flops 2516582400 | bytes 7077888 | tf_op jit(solution)/shard_map/dot_general | solution.py:22
  37.3 11.2 %fusion.5.part = f32[1280,256]{1,0:T(8,128)} fusion(f32[1280,3200]{1,0:T(8,128)} %refs_9_.1, f32[3200,256]{1,0:T(8,128)S(1)} %copy-done), kind=kOutput, calls=%fused_computation.14 | convolution fusion | flops 6291456000 | bytes 20971520 | tf_op jit(solution)/shard_map/dot_general | solution.py:22
  48.6 6.9 %collective-permute-done.3.refs_4_ = bf16[1280,256]{1,0:T(8,128)(2,1)} collective-permute-done((bf16[1280,256]{1,0:T(8,128)(2,1)}, bf16[1280,256]{1,0:T(8,128)(2,1)}, u32[]{:S(2)}, u32[]{:S(2)}) %collective-permute-start.3) | collective-permute-done | bytes 655392 | tf_op jit(solution)/shard_map/ppermute | solution.py:302
  55.4 12.7 %collective-permute-done.4.refs_5_ = bf16[1280,256]{1,0:T(8,128)(2,1)} collective-permute-done((bf16[1280,256]{1,0:T(8,128)(2,1)}, bf16[1280,256]{1,0:T(8,128)(2,1)}, u32[]{:S(2)}, u32[]{:S(2)}) %collective-permute-start.4) | collective-permute-done | bytes 655392 | tf_op jit(solution)/shard_map/ppermute | solution.py:302
  69.4 4.7 %shard_map.76 = (f32[640,256]{1,0:T(8,128)S(1)}, f32[640,256]{1,0:T(8,128)S(1)}) custom-call(s32[4]{0:T(128)S(1)} %pad_add_fusion.ids, f32[1280,256]{1,0:T(8,128)S(1)} %copy-done.5, bf16[1280,256]{1,0:T(8,128)(2,1)} %bitcast.4.refs_0_.refs_5_, bf16[1280,256]{1,0:T(8,128)(2,1)} %collective-permute-done.refs_1_.refs_6_, ...), custom_call_target="tpu_custom_call" | custom-call | flops 1342177280 | bytes 8000000 | tf_op jit(solution)/shard_map/pallas_call | solution.py:121
  76.5 2.9 collective-permute-start.11
  80.9 4.8 %collective-permute-done.10 = f32[160,256]{1,0:T(8,128)S(1)} collective-permute-done((f32[160,256]{1,0:T(8,128)S(1)}, f32[160,256]{1,0:T(8,128)S(1)}, u32[]{:S(2)}, u32[]{:S(2)}) %collective-permute-start.10) | collective-permute-done | bytes 163872 | tf_op jit(solution)/shard_map/ppermute | solution.py:293
  85.7 5.9 %collective-permute-done.11 = f32[160,256]{1,0:T(8,128)S(1)} collective-permute-done((f32[160,256]{1,0:T(8,128)S(1)}, f32[160,256]{1,0:T(8,128)S(1)}, u32[]{:S(2)}, u32[]{:S(2)}) %collective-permute-start.11) | collective-permute-done | bytes 163872 | tf_op jit(solution)/shard_map/ppermute | solution.py:293
  91.6 3.3 collective-permute-start.13
  97.4 3.3 collective-permute-done.13.refs_1_
  100.7 9.1 %collective-permute-done.14.refs_2_ = f32[160,256]{1,0:T(8,128)S(1)} collective-permute-done((f32[160,256]{1,0:T(8,128)S(1)}, f32[160,256]{1,0:T(8,128)S(1)}, u32[]{:S(2)}, u32[]{:S(2)}) %collective-permute-start.14) | collective-permute-done | bytes 163872 | tf_op jit(solution)/shard_map/ppermute | solution.py:293
  112.8 4.4 %shard_map.77 = (f32[1280,256]{1,0:T(8,128)S(1)}, f32[256,256]{1,0:T(8,128)S(1)}, f32[256,256]{1,0:T(8,128)S(1)}, f32[256,256]{1,0:T(8,128)S(1)}, f32[256,256]{1...) custom-call(s32[4]{0:T(128)S(1)} %pad_add_fusion.ids, ...), custom_call_target="tpu_custom_call" | custom-call | flops 1677721600 | bytes 8000000 | tf_op jit(solution)/shard_map/pallas_call | solution.py:121
  120.8 5.7 %collective-permute-done.19 = f32[256,256]{1,0:T(8,128)S(1)} collective-permute-done((f32[256,256]{1,0:T(8,128)S(1)}, f32[256,256]{1,0:T(8,128)S(1)}, u32[]{:S(2)}, u32[]{:S(2)}) %collective-permute-start.19) | collective-permute-done | bytes 262176 | tf_op jit(solution)/shard_map/ppermute | solution.py:293
  126.5 6.4 %collective-permute-done.20 = f32[256,256]{1,0:T(8,128)S(1)} collective-permute-done((f32[256,256]{1,0:T(8,128)S(1)}, f32[256,256]{1,0:T(8,128)S(1)}, u32[]{:S(2)}, u32[]{:S(2)}) %collective-permute-start.20) | collective-permute-done | bytes 262176 | tf_op jit(solution)/shard_map/ppermute | solution.py:293
  133.0 12.5 %shard_map.79 = (f32[64,3200]{1,0:T(8,128)S(1)}, f32[64,3200]{1,0:T(8,128)S(1)}, f32[64,3200]{1,0:T(8,128)S(1)}, f32[64,3200]{1,0:T(8,128)S(1)}) custom-call(bf16[256,1280]{1,0:T(8,128)(2,1)S(1)} %get-tuple-element.34.big_t, bf16[256,1280]{1,0:T(8,128)(2,1)S(1)} %get-tuple-element.35.low_t, f32[1280,3200]{1,0:T(8,128)} %refs_9_.1), custom_call_target="tpu_custom_call" | custom-call | flops 6291456000 | bytes 20480000 | tf_op jit(solution)/shard_map/pallas_call | solution.py:121
  145.6 7.0 %shard_map.80 = (f32[64,3200]{1,0:T(8,128)S(1)}, f32[64,3200]{1,0:T(8,128)S(1)}, f32[64,3200]{1,0:T(8,128)S(1)}, f32[64,3200]{1,0:T(8,128)S(1)}) custom-call(s32[4]{0:T(128)S(1)} %pad_add_fusion.ids, f32[256,256]{1,0:T(8,128)S(1)} %add_add_fusion.own, f32[256,256]{1,0:T(8,128)S(1)} %collective-permute-done.22.other, bf16[512,3200]{1,0:T(8,128)(2,1)S(1)} %copy-done.4, ...), custom_call_target="tpu_custom_call" | custom-call | flops 1677721600 | bytes 8192000 | tf_op jit(solution)/shard_map/pallas_call | solution.py:121
  157.0 16.2 %collective-permute-done.26 = f32[64,3200]{1,0:T(8,128)S(1)} collective-permute-done((f32[64,3200]{1,0:T(8,128)S(1)}, f32[64,3200]{1,0:T(8,128)S(1)}, u32[]{:S(2)}, u32[]{:S(2)}) %collective-permute-start.26) | collective-permute-done | bytes 819232 | tf_op jit(solution)/shard_map/ppermute | solution.py:293
  176.0 34.7 %collective-permute-done.23 = f32[64,3200]{1,0:T(8,128)S(1)} collective-permute-done((f32[64,3200]{1,0:T(8,128)S(1)}, f32[64,3200]{1,0:T(8,128)S(1)}, u32[]{:S(2)}, u32[]{:S(2)}) %collective-permute-start.23) | collective-permute-done | bytes 819232 | tf_op jit(solution)/shard_map/ppermute | solution.py:293
  213.1 15.1 %collective-permute-done.27 = f32[64,3200]{1,0:T(8,128)S(1)} collective-permute-done((f32[64,3200]{1,0:T(8,128)S(1)}, f32[64,3200]{1,0:T(8,128)S(1)}, u32[]{:S(2)}, u32[]{:S(2)}) %collective-permute-start.27) | collective-permute-done | bytes 819232 | tf_op jit(solution)/shard_map/ppermute | solution.py:293
  235.7 32.5 %collective-permute-done.17 = f32[256,256]{1,0:T(8,128)S(1)} collective-permute-done((f32[256,256]{1,0:T(8,128)S(1)}, f32[256,256]{1,0:T(8,128)S(1)}, u32[]{:S(2)}, u32[]{:S(2)}) %collective-permute-start.17) | collective-permute-done | bytes 262176 | tf_op jit(solution)/shard_map/ppermute | solution.py:293
  270.4 18.6 %shard_map.83.refs_9_ = f32[1280,3200]{1,0:T(8,128)} custom-call(s32[4]{0:T(128)S(1)} %pad_add_fusion.ids, bf16[4,1280,256]{2,1,0:T(8,128)(2,1)S(1)} %pad_maximum_fusion.refs_0_.refs_1_.own, bf16[4,1280,256]{2,1,0:T(8,128)(2,1)S(1)} %pad_maximum_fusion.refs_0_.refs_1_.own, bf16[4,1280,256]{2,1,0:T(8,128)(2,1)S(1)} %pad_maximum_fusion.1.refs_2_.refs_3_.other, ...), custom_call_target="tpu_custom_call" | custom-call | flops 8388608000 | bytes 32768000 | tf_op jit(solution)/shard_map/pallas_call | solution.py:121
  289.0 3.0 collective-permute-done.18
  299.6 13.6 %shard_map.78.inverse = f32[256,256]{1,0:T(8,128)} custom-call(f32[256,256]{1,0:T(8,128)} %add.82.gram_ref), custom_call_target="tpu_custom_call" | custom-call | flops 20000000000 | bytes 10000000 | tf_op jit(solution)/shard_map/pallas_call | solution.py:95
  320.2 7.4 %shard_map.81 = (f32[256,3200]{1,0:T(8,128)S(1)}, f32[8,256]{1,0:T(8,128)S(1)}, f32[1280,256]{1,0:T(8,128)S(1)}) custom-call(s32[4]{0:T(128)S(1)} %pad_add_fusion.ids, f32[256,256]{1,0:T(8,128)S(1)} %copy-done.16, f32[1280,256]{1,0:T(8,128)S(1)} %copy-done.11, f32[64,3200]{1,0:T(8,128)S(1)} %copy-done.9, f32[64,3200]{1,0:T(8,128)S(1)} %copy-done.15, ...), custom_call_target="tpu_custom_call" | custom-call | flops 1258291200 | bytes 9830400 | tf_op jit(solution)/shard_map/pallas_call | solution.py:121
  327.6 20.8 %collective-permute-done.44.refs_7_ = bf16[128,3200]{1,0:T(8,128)(2,1)} collective-permute-done((bf16[128,3200]{1,0:T(8,128)(2,1)}, bf16[128,3200]{1,0:T(8,128)(2,1)}, u32[]{:S(2)}, u32[]{:S(2)}) %collective-permute-start.44) | collective-permute-done | bytes 819232 | tf_op jit(solution)/shard_map/ppermute | solution.py:293
  348.5 18.3 %shard_map.84.base = f32[1280,3200]{1,0:T(8,128)} custom-call(s32[4]{0:T(128)S(1)} %pad_add_fusion.ids, bf16[4,1280,256]{2,1,0:T(8,128)(2,1)S(1)} %pad_maximum_fusion.refs_0_.refs_1_.own, bf16[4,1280,256]{2,1,0:T(8,128)(2,1)S(1)} %pad_maximum_fusion.refs_0_.refs_1_.own, bf16[4,1280,256]{2,1,0:T(8,128)(2,1)S(1)} %copy-done.3, ...), custom_call_target="tpu_custom_call" | custom-call | flops 6291456000 | bytes 32768000 | tf_op jit(solution)/shard_map/pallas_call | solution.py:121
  366.8 2.4 collective-permute-start.30
  371.7 16.1 %shard_map.85 = f32[1280,3200]{1,0:T(8,128)} custom-call(s32[4]{0:T(128)S(1)} %pad_add_fusion.ids, bf16[4,1280,256]{2,1,0:T(8,128)(2,1)S(1)} %pad_maximum_fusion.refs_0_.refs_1_.own, bf16[4,1280,256]{2,1,0:T(8,128)(2,1)S(1)} %copy-done.3, bf16[128,3200]{1,0:T(8,128)(2,1)} %collective-permute-done.38.first, ...), custom_call_target="tpu_custom_call", output_to_operand_aliasing={{}: (7, {})} | custom-call | flops 4194304000 | bytes 32768000 | tf_op jit(solution)/shard_map/pallas_call | solution.py:121
  387.9 11.6 %shard_map.82 = (f32[1280,3200]{1,0:T(8,128)}, f32[3200,256]{1,0:T(8,128)}) custom-call(f32[8,256]{1,0:T(8,128)S(1)} %add_add_fusion.1.squares, f32[1280,256]{1,0:T(8,128)S(1)} %get-tuple-element.45.basis, f32[256,3200]{1,0:T(8,128)S(1)} %get-tuple-element.46.right, bf16[1280,3200]{1,0:T(8,128)(2,1)S(1)} %bitcast.21), custom_call_target="tpu_custom_call" | custom-call | flops 6291456000 | bytes 24576000 | tf_op jit(solution)/shard_map/pallas_call | solution.py:121
  (136 shorter events, 63.9 us)
Async XLA Ops:
  3.0 18.1 %collective-permute-start = (bf16[1280,256]{1,0:T(8,128)(2,1)}, bf16[1280,256]{1,0:T(8,128)(2,1)}, u32[]{:S(2)}, u32[]{:S(2)}) collective-permute-start(bf16[1280,256]{1,0:T(8,128)(2,1)} %bitcast.4.refs_0_.refs_5_), channel_id=1, source_target_pairs={{0,2},{1,3},{2,0},{3,1},{4,6},{5,7},{6,4},{7,5},{8,10},{9,11},{10,... | collective-permute-start | bytes 1966088 | tf_op jit(solution)/shard_map/ppermute | solution.py:293
  6.0 28.5 %collective-permute-start.1 = (bf16[1280,256]{1,0:T(8,128)(2,1)}, bf16[1280,256]{1,0:T(8,128)(2,1)}, u32[]{:S(2)}, u32[]{:S(2)}) collective-permute-start(bf16[1280,256]{1,0:T(8,128)(2,1)} %bitcast.4.refs_0_.refs_5_), channel_id=1, source_target_pairs={{2,4},{3,5},{4,2},{5,3},{10,12},{11,13},{12,10},{13,11},{18,20},{1... | collective-permute-start | bytes 1966088 | tf_op jit(solution)/shard_map/ppermute | solution.py:302
  31.0 17.6 %collective-permute-start.6 = (f32[256,256]{1,0:T(8,128)S(1)}, f32[256,256]{1,0:T(8,128)}, u32[]{:S(2)}, u32[]{:S(2)}) collective-permute-start(f32[256,256]{1,0:T(8,128)S(1)} %dynamic-slice_add_fusion.refs_6_), channel_id=1, source_target_pairs={{0,8},{8,0},{16,24},{24,16},{1,9},{9,1},{17,25},{25,17},{2,10},{10... | collective-permute-start | bytes 786440 | tf_op jit(solution)/shard_map/ppermute | solution.py:293
  32.7 15.9 %collective-permute-start.7 = (f32[256,256]{1,0:T(8,128)S(1)}, f32[256,256]{1,0:T(8,128)}, u32[]{:S(2)}, u32[]{:S(2)}) collective-permute-start(f32[256,256]{1,0:T(8,128)S(1)} %dynamic-slice_add_fusion.refs_6_), channel_id=1, source_target_pairs={{0,16},{8,24},{16,0},{24,8},{1,17},{9,25},{17,1},{25,9},{2,18},{10... | collective-permute-start | bytes 786440 | tf_op jit(solution)/shard_map/ppermute | solution.py:293
  34.5 20.9 %collective-permute-start.3 = (bf16[1280,256]{1,0:T(8,128)(2,1)}, bf16[1280,256]{1,0:T(8,128)(2,1)}, u32[]{:S(2)}, u32[]{:S(2)}) collective-permute-start(bf16[1280,256]{1,0:T(8,128)(2,1)} %collective-permute-done.1.refs_2_), channel_id=1, source_target_pairs={{2,0},{3,1},{4,6},{5,7},{10,8},{11,9},{12,14},{13,15},{18,16},{19,... | collective-permute-start | bytes 1966088 | tf_op jit(solution)/shard_map/ppermute | solution.py:302
  35.8 32.3 %collective-permute-start.4 = (bf16[1280,256]{1,0:T(8,128)(2,1)}, bf16[1280,256]{1,0:T(8,128)(2,1)}, u32[]{:S(2)}, u32[]{:S(2)}) collective-permute-start(bf16[1280,256]{1,0:T(8,128)(2,1)} %collective-permute-done.2.refs_3_), channel_id=1, source_target_pairs={{2,0},{3,1},{4,6},{5,7},{10,8},{11,9},{12,14},{13,15},{18,16},{19,... | collective-permute-start | bytes 1966088 | tf_op jit(solution)/shard_map/ppermute | solution.py:302
  76.5 15.1 %collective-permute-start.11 = (f32[160,256]{1,0:T(8,128)S(1)}, f32[160,256]{1,0:T(8,128)S(1)}, u32[]{:S(2)}, u32[]{:S(2)}) collective-permute-start(f32[160,256]{1,0:T(8,128)S(1)} %get-tuple-element.57), channel_id=1, source_target_pairs={{0,4},{1,5},{2,6},{3,7},{4,0},{5,1},{6,2},{7,3},{8,12},{9,13},{10,... | collective-permute-start | bytes 491528 | tf_op jit(solution)/shard_map/ppermute | solution.py:293
  120.8 90.5 %collective-permute-start.33 = (bf16[1280,256]{1,0:T(8,128)(2,1)}, bf16[1280,256]{1,0:T(8,128)(2,1)S(1)}, u32[]{:S(2)}, u32[]{:S(2)}) collective-permute-start(bf16[1280,256]{1,0:T(8,128)(2,1)} %bitcast.4.refs_0_.refs_5_), channel_id=1, source_target_pairs={{0,1},{1,0},{2,3},{3,2},{4,5},{5,4},{6,7},{7,6},{8,9},{9,8},{10,11... | collective-permute-start | bytes 1966088 | tf_op jit(solution)/shard_map/ppermute | solution.py:293
  152.5 20.7 %collective-permute-start.26 = (f32[64,3200]{1,0:T(8,128)S(1)}, f32[64,3200]{1,0:T(8,128)S(1)}, u32[]{:S(2)}, u32[]{:S(2)}) collective-permute-start(f32[64,3200]{1,0:T(8,128)S(1)} %get-tuple-element.43), channel_id=1, source_target_pairs={{0,16},{8,24},{16,0},{24,8},{1,17},{9,25},{17,1},{25,9},{2,18},{10... | collective-permute-start | bytes 2457608 | tf_op jit(solution)/shard_map/ppermute | solution.py:293
  154.4 58.2 %collective-permute-start.37 = (bf16[128,3200]{1,0:T(8,128)(2,1)S(1)}, bf16[128,3200]{1,0:T(8,128)(2,1)}, u32[]{:S(2)}, u32[]{:S(2)}) collective-permute-start(bf16[128,3200]{1,0:T(8,128)(2,1)S(1)} %get-tuple-element.54), channel_id=1, source_target_pairs={{0,8},{8,0},{16,24},{24,16},{1,9},{9,1},{17,25},{25,17},{2,10},{10... | collective-permute-start | bytes 2457608 | tf_op jit(solution)/shard_map/ppermute | solution.py:293
  155.0 57.6 %collective-permute-start.43 = (bf16[128,3200]{1,0:T(8,128)(2,1)S(1)}, bf16[128,3200]{1,0:T(8,128)(2,1)}, u32[]{:S(2)}, u32[]{:S(2)}) collective-permute-start(bf16[128,3200]{1,0:T(8,128)(2,1)S(1)} %get-tuple-element.51), channel_id=1, source_target_pairs={{0,8},{8,0},{16,24},{24,16},{1,9},{9,1},{17,25},{25,17},{2,10},{10... | collective-permute-start | bytes 2457608 | tf_op jit(solution)/shard_map/ppermute | solution.py:293
  156.5 54.2 %collective-permute-start.23 = (f32[64,3200]{1,0:T(8,128)S(1)}, f32[64,3200]{1,0:T(8,128)S(1)}, u32[]{:S(2)}, u32[]{:S(2)}) collective-permute-start(f32[64,3200]{1,0:T(8,128)S(1)} %get-tuple-element.41), channel_id=1, source_target_pairs={{0,8},{8,0},{16,24},{24,16},{1,9},{9,1},{17,25},{25,17},{2,10},{10... | collective-permute-start | bytes 2457608 | tf_op jit(solution)/shard_map/ppermute | solution.py:293
  173.3 54.9 %collective-permute-start.27 = (f32[64,3200]{1,0:T(8,128)S(1)}, f32[64,3200]{1,0:T(8,128)S(1)}, u32[]{:S(2)}, u32[]{:S(2)}) collective-permute-start(f32[64,3200]{1,0:T(8,128)S(1)} %add.88), channel_id=1, source_target_pairs={{0,8},{8,0},{16,24},{24,16},{1,9},{9,1},{17,25},{25,17},{2,10},{10... | collective-permute-start | bytes 2457608 | tf_op jit(solution)/shard_map/ppermute | solution.py:293
  210.7 58.4 %collective-permute-start.46 = (bf16[256,3200]{1,0:T(8,128)(2,1)S(1)}, bf16[256,3200]{1,0:T(8,128)(2,1)S(1)}, u32[]{:S(2)}, u32[]{:S(2)}) collective-permute-start(bf16[256,3200]{1,0:T(8,128)(2,1)S(1)} %get-tuple-element.49.refs_5_), channel_id=1, source_target_pairs={{0,8},{8,0},{16,24},{24,16},{1,9},{9,1},{17,25},{25,17},{2,10},{10... | collective-permute-start | bytes 4915208 | tf_op jit(solution)/shard_map/ppermute | solution.py:293
  211.3 18.5 %collective-permute-start.24 = (f32[64,3200]{1,0:T(8,128)S(1)}, f32[64,3200]{1,0:T(8,128)S(1)}, u32[]{:S(2)}, u32[]{:S(2)}) collective-permute-start(f32[64,3200]{1,0:T(8,128)S(1)} %add.86), channel_id=1, source_target_pairs={{0,16},{8,24},{16,0},{24,8},{1,17},{9,25},{17,1},{25,9},{2,18},{10... | collective-permute-start | bytes 2457608 | tf_op jit(solution)/shard_map/ppermute | solution.py:293
  212.6 20.5 %collective-permute-start.34 = (bf16[1280,256]{1,0:T(8,128)(2,1)}, bf16[1280,256]{1,0:T(8,128)(2,1)S(1)}, u32[]{:S(2)}, u32[]{:S(2)}) collective-permute-start(bf16[1280,256]{1,0:T(8,128)(2,1)} %collective-permute-done.refs_1_.refs_6_), channel_id=1, source_target_pairs={{0,1},{1,0},{2,3},{3,2},{4,5},{5,4},{6,7},{7,6},{8,9},{9,8},{10,11... | collective-permute-start | bytes 1966088 | tf_op jit(solution)/shard_map/ppermute | solution.py:293
  212.6 21.1 %collective-permute-start.35 = (bf16[1280,256]{1,0:T(8,128)(2,1)S(1)}, bf16[1280,256]{1,0:T(8,128)(2,1)S(1)}, u32[]{:S(2)}, u32[]{:S(2)}) collective-permute-start(bf16[1280,256]{1,0:T(8,128)(2,1)S(1)} %add.79.refs_7_), channel_id=1, source_target_pairs={{0,1},{1,0},{2,3},{3,2},{4,5},{5,4},{6,7},{7,6},{8,9},{9,8},{10,11... | collective-permute-start | bytes 1966088 | tf_op jit(solution)/shard_map/ppermute | solution.py:293
  229.8 38.4 %collective-permute-start.17 = (f32[256,256]{1,0:T(8,128)S(1)}, f32[256,256]{1,0:T(8,128)S(1)}, u32[]{:S(2)}, u32[]{:S(2)}) collective-permute-start(f32[256,256]{1,0:T(8,128)S(1)} %get-tuple-element.28), channel_id=1, source_target_pairs={{0,8},{8,0},{16,24},{24,16},{1,9},{9,1},{17,25},{25,17},{2,10},{10... | collective-permute-start | bytes 786440 | tf_op jit(solution)/shard_map/ppermute | solution.py:293
  233.1 60.6 %collective-permute-start.42 = (bf16[128,3200]{1,0:T(8,128)(2,1)S(1)}, bf16[128,3200]{1,0:T(8,128)(2,1)}, u32[]{:S(2)}, u32[]{:S(2)}) collective-permute-start(bf16[128,3200]{1,0:T(8,128)(2,1)S(1)} %get-tuple-element.52), channel_id=1, source_target_pairs={{0,16},{8,24},{16,0},{24,8},{1,17},{9,25},{17,1},{25,9},{2,18},{10... | collective-permute-start | bytes 2457608 | tf_op jit(solution)/shard_map/ppermute | solution.py:293
  233.7 61.1 %collective-permute-start.39 = (bf16[128,3200]{1,0:T(8,128)(2,1)S(1)}, bf16[128,3200]{1,0:T(8,128)(2,1)}, u32[]{:S(2)}, u32[]{:S(2)}) collective-permute-start(bf16[128,3200]{1,0:T(8,128)(2,1)S(1)} %get-tuple-element.53), channel_id=1, source_target_pairs={{0,16},{8,24},{16,0},{24,8},{1,17},{9,25},{17,1},{25,9},{2,18},{10... | collective-permute-start | bytes 2457608 | tf_op jit(solution)/shard_map/ppermute | solution.py:293
  235.2 60.6 %collective-permute-start.28 = (f32[64,3200]{1,0:T(8,128)S(1)}, f32[64,3200]{1,0:T(8,128)S(1)}, u32[]{:S(2)}, u32[]{:S(2)}) collective-permute-start(f32[64,3200]{1,0:T(8,128)S(1)} %add.89.refs_2_), channel_id=1, source_target_pairs={{0,16},{8,24},{16,0},{24,8},{1,17},{9,25},{17,1},{25,9},{2,18},{10... | collective-permute-start | bytes 2457608 | tf_op jit(solution)/shard_map/ppermute | solution.py:293
  268.2 29.3 %collective-permute-start.25 = (f32[64,3200]{1,0:T(8,128)S(1)}, f32[64,3200]{1,0:T(8,128)S(1)}, u32[]{:S(2)}, u32[]{:S(2)}) collective-permute-start(f32[64,3200]{1,0:T(8,128)S(1)} %add.87.refs_0_), channel_id=1, source_target_pairs={{0,8},{8,0},{16,24},{24,16},{1,9},{9,1},{17,25},{25,17},{2,10},{10... | collective-permute-start | bytes 2457608 | tf_op jit(solution)/shard_map/ppermute | solution.py:293
  269.1 22.8 %collective-permute-start.18 = (f32[256,256]{1,0:T(8,128)S(1)}, f32[256,256]{1,0:T(8,128)S(1)}, u32[]{:S(2)}, u32[]{:S(2)}) collective-permute-start(f32[256,256]{1,0:T(8,128)S(1)} %add.81), channel_id=1, source_target_pairs={{0,16},{8,24},{16,0},{24,8},{1,17},{9,25},{17,1},{25,9},{2,18},{10... | collective-permute-start | bytes 786440 | tf_op jit(solution)/shard_map/ppermute | solution.py:293
  291.9 56.6 %collective-permute-start.41 = (bf16[256,3200]{1,0:T(8,128)(2,1)}, bf16[256,3200]{1,0:T(8,128)(2,1)}, u32[]{:S(2)}, u32[]{:S(2)}) collective-permute-start(bf16[256,3200]{1,0:T(8,128)(2,1)} %get-tuple-element.50.refs_4_), channel_id=1, source_target_pairs={{0,16},{8,24},{16,0},{24,8},{1,17},{9,25},{17,1},{25,9},{2,18},{10... | collective-permute-start | bytes 4915208 | tf_op jit(solution)/shard_map/ppermute | solution.py:293
  293.7 54.8 %collective-permute-start.44 = (bf16[128,3200]{1,0:T(8,128)(2,1)}, bf16[128,3200]{1,0:T(8,128)(2,1)}, u32[]{:S(2)}, u32[]{:S(2)}) collective-permute-start(bf16[128,3200]{1,0:T(8,128)(2,1)} %collective-permute-done.43.refs_6_), channel_id=1, source_target_pairs={{0,16},{8,24},{16,0},{24,8},{1,17},{9,25},{17,1},{25,9},{2,18},{10... | collective-permute-start | bytes 2457608 | tf_op jit(solution)/shard_map/ppermute | solution.py:293
  294.7 77.0 %collective-permute-start.38 = (bf16[128,3200]{1,0:T(8,128)(2,1)}, bf16[128,3200]{1,0:T(8,128)(2,1)}, u32[]{:S(2)}, u32[]{:S(2)}) collective-permute-start(bf16[128,3200]{1,0:T(8,128)(2,1)} %collective-permute-done.37.refs_7_), channel_id=1, source_target_pairs={{0,16},{8,24},{16,0},{24,8},{1,17},{9,25},{17,1},{25,9},{2,18},{10... | collective-permute-start | bytes 2457608 | tf_op jit(solution)/shard_map/ppermute | solution.py:293
  296.7 51.8 %collective-permute-start.45 = (bf16[128,3200]{1,0:T(8,128)(2,1)}, bf16[128,3200]{1,0:T(8,128)(2,1)}, u32[]{:S(2)}, u32[]{:S(2)}) collective-permute-start(bf16[128,3200]{1,0:T(8,128)(2,1)} %collective-permute-done.42.refs_5_), channel_id=1, source_target_pairs={{0,8},{8,0},{16,24},{24,16},{1,9},{9,1},{17,25},{25,17},{2,10},{10... | collective-permute-start | bytes 2457608 | tf_op jit(solution)/shard_map/ppermute | solution.py:293
  298.4 73.3 %collective-permute-start.40 = (bf16[128,3200]{1,0:T(8,128)(2,1)}, bf16[128,3200]{1,0:T(8,128)(2,1)}, u32[]{:S(2)}, u32[]{:S(2)}) collective-permute-start(bf16[128,3200]{1,0:T(8,128)(2,1)} %collective-permute-done.39.refs_6_), channel_id=1, source_target_pairs={{0,8},{8,0},{16,24},{24,16},{1,9},{9,1},{17,25},{25,17},{2,10},{10... | collective-permute-start | bytes 2457608 | tf_op jit(solution)/shard_map/ppermute | solution.py:293
  348.5 18.4 %collective-permute-start.29 = (f32[8,256]{1,0:T(8,128)S(1)}, f32[8,256]{1,0:T(8,128)S(1)}, u32[]{:S(2)}, u32[]{:S(2)}) collective-permute-start(f32[8,256]{1,0:T(8,128)S(1)} %get-tuple-element.44), channel_id=1, source_target_pairs={{0,1},{1,0},{2,3},{3,2},{4,5},{5,4},{6,7},{7,6},{8,9},{9,8},{10,11... | collective-permute-start | bytes 24584 | tf_op jit(solution)/shard_map/ppermute | solution.py:293
  366.8 21.0 %collective-permute-start.30 = (f32[8,256]{1,0:T(8,128)S(1)}, f32[8,256]{1,0:T(8,128)S(1)}, u32[]{:S(2)}, u32[]{:S(2)}) collective-permute-start(f32[8,256]{1,0:T(8,128)S(1)} %add.90), channel_id=1, source_target_pairs={{0,2},{1,3},{2,0},{3,1},{4,6},{5,7},{6,4},{7,5},{8,10},{9,11},{10,... | collective-permute-start | bytes 24584 | tf_op jit(solution)/shard_map/ppermute | solution.py:293
  369.3 18.6 %collective-permute-start.31 = (f32[8,256]{1,0:T(8,128)S(1)}, f32[8,256]{1,0:T(8,128)S(1)}, u32[]{:S(2)}, u32[]{:S(2)}) collective-permute-start(f32[8,256]{1,0:T(8,128)S(1)} %add.90), channel_id=1, source_target_pairs={{0,4},{1,5},{2,6},{3,7},{4,0},{5,1},{6,2},{7,3},{8,12},{9,13},{10,... | collective-permute-start | bytes 24584 | tf_op jit(solution)/shard_map/ppermute | solution.py:293
  370.2 17.6 %collective-permute-start.32 = (f32[8,256]{1,0:T(8,128)S(1)}, f32[8,256]{1,0:T(8,128)S(1)}, u32[]{:S(2)}, u32[]{:S(2)}) collective-permute-start(f32[8,256]{1,0:T(8,128)S(1)} %add.90), channel_id=1, source_target_pairs={{0,6},{1,7},{2,4},{3,5},{4,2},{5,3},{6,0},{7,1},{8,14},{9,15},{10,... | collective-permute-start | bytes 24584 | tf_op jit(solution)/shard_map/ppermute | solution.py:293
  (34 other events, 456.8 us)
